TPU v7x, 32 devices: a whole 2x2x4 slice. The times are simulated.
32 devices in a mesh: dp: 2 (over core), space: 16 (over z, y, x).
Axes of the slice: x: 2, y: 2, z: 4, core: 2. Of those that a mesh axis runs over, the one named last changes fastest.
Arguments:
- features: bfloat16 [32, 2304, 2048], P('dp', 'space'), parts along dimension 0, may hold values from 0 to 18
- depth_weights: bfloat16 [3, 9, 2048], replicated, may hold values from -2 to 2
- point_weights: bfloat16 [3, 2048, 256], replicated, may hold values from -0.125 to 0.125
- branch_weight: bfloat16 [2048, 256], replicated, may hold values from -0.125 to 0.125
- pooling_weight: bfloat16 [2048, 256], replicated, may hold values from -0.125 to 0.125
- project_weight: bfloat16 [1280, 256], replicated, may hold values from -0.15625 to 0.15625
- refine_depth: bfloat16 [9, 256], replicated, may hold values from -2 to 2
- refine_point: bfloat16 [256, 256], replicated, may hold values from -0.375 to 0.375
Outputs:
- refined: bfloat16 [32, 2304, 256], P('dp', 'space'), parts along dimension 0
There are 2 independent parts, one for each index of `dp`. A program takes and returns all parts, laid end to end along the dimension named above; an argument that names none is the same for every part. Nothing has to cross between parts.
All inputs are finite; a program needn't handle non-finite values.
Results may differ from a plain program's by a relative error of at most 0.0066.
Values may be sent and summed in bfloat16 or wider, within the bound.
No kernel may reach another device: no remote copies, remote signals or barrier semaphores. Data moves between devices by JAX's collectives and lax.ppermute only.
A program may use at most 128 MiB of HBM per device.

v0:
```python
import jax
import jax.numpy as jnp
from jax import lax
from jax.sharding import PartitionSpec as P

RATE_LOW = 12
RATE_MID = 24
RATE_HIGH = 36
ROWS = 48
COLS = 48


def depthwise(image, taps, rate):
    padded = jnp.pad(image, ((0, 0), (rate, rate), (rate, rate), (0, 0)))
    height = image.shape[1]
    width = image.shape[2]
    total = jnp.zeros(image.shape, jnp.float32)
    for row in range(3):
        for col in range(3):
            window = padded[:, row * rate : row * rate + height, col * rate : col * rate + width, :]
            total = total + window.astype(jnp.float32) * taps[3 * row + col].astype(jnp.float32)
    return jax.nn.relu(total).astype(jnp.bfloat16)


def pointwise(image, weight):
    flat = image.reshape(-1, image.shape[-1])
    product = jnp.dot(flat, weight, preferred_element_type=jnp.float32)
    return jax.nn.relu(product).reshape(image.shape[:-1] + (weight.shape[1],)).astype(jnp.bfloat16)


def pool_branch(pooled, pooling_weight):
    return jax.nn.relu(
        jnp.dot(pooled.astype(jnp.bfloat16), pooling_weight, preferred_element_type=jnp.float32)
    ).astype(jnp.bfloat16)


def body(
    features,
    depth_weights,
    point_weights,
    branch_weight,
    pooling_weight,
    project_weight,
    refine_depth,
    refine_point,
):
    parts = lax.axis_size("space")
    mine = features.shape[0] // parts
    block = features.shape[1]
    cells = block * parts
    flat_whole = lax.all_to_all(features, "space", split_axis=0, concat_axis=1, tiled=True)
    whole = flat_whole.reshape(mine, ROWS, COLS, features.shape[2])
    pooled = jnp.mean(flat_whole.astype(jnp.float32), axis=1)
    pool_vector = pool_branch(pooled, pooling_weight)
    rates = (RATE_LOW, RATE_MID, RATE_HIGH)
    branches = [pointwise(whole, branch_weight)]
    for index in range(3):
        spread = depthwise(whole, depth_weights[index], rates[index])
        branches.append(pointwise(spread, point_weights[index]))
    branches.append(
        jnp.broadcast_to(pool_vector[:, None, None, :], whole.shape[:3] + (pool_vector.shape[1],))
    )
    context = pointwise(jnp.concatenate(branches, axis=-1), project_weight)
    width = context.shape[-1]
    margin = COLS + 1
    extent = block + 2 * margin
    flat_context = jnp.pad(context.reshape(mine, cells, width), ((0, 0), (margin, margin), (0, 0)))
    window_index = (jnp.arange(parts, dtype=jnp.int32) * block)[:, None] + jnp.arange(
        extent, dtype=jnp.int32
    )[None, :]
    windows = flat_context[:, window_index]
    received = lax.all_to_all(windows, "space", split_axis=1, concat_axis=0, tiled=True)
    bordered = received.reshape(mine * parts, extent, width)
    start = lax.axis_index("space") * block
    column = (start + jnp.arange(block, dtype=jnp.int32)) % COLS
    left_ok = (column > 0).astype(jnp.float32)[None, :, None]
    right_ok = (column < COLS - 1).astype(jnp.float32)[None, :, None]
    total = jnp.zeros((bordered.shape[0], block, width), jnp.float32)
    for row in range(3):
        for col in range(3):
            offset = margin + (row - 1) * COLS + (col - 1)
            window = bordered[:, offset : offset + block, :].astype(jnp.float32)
            if col == 0:
                window = window * left_ok
            if col == 2:
                window = window * right_ok
            total = total + window * refine_depth[3 * row + col].astype(jnp.float32)
    spread_rows = jax.nn.relu(total).astype(jnp.bfloat16)
    return pointwise(spread_rows, refine_point)


def solution(mesh):
    return jax.shard_map(
        body,
        mesh=mesh,
        in_specs=(P("dp", "space", None), P(), P(), P(), P(), P(), P(), P()),
        out_specs=P("dp", "space", None),
        check_vma=False,
    )
```

profile of v0, /device:TPU:0, one launch (start us, length us, event | category | flops | bytes accessed | tf_op | source)
XLA Modules:
  0.0 392.3 jit_solution(16624007131997138501)
XLA Ops:
  0.0 8.5 %all-to-all-start = ((bf16[16,144,2048]{2,1,0:T(8,128)(2,1)}), bf16[16,144,2048]{2,1,0:T(8,128)(2,1)}, u32[]{:S(2)}, u32[]{:S(2)}) async-start(bf16[16,144,2048]{2,1,0:T(8,128)(2,1)} %param.8), calls=%async_computation | async-start | bytes 18874368 | tf_op jit(solution)/shard_map/all_to_all | solution.py:51
  8.6 0.1 reshape.577
  8.8 0.1 slice_convert_fusion.8
  8.9 177.6 %all-to-all-done = bf16[16,144,2048]{2,1,0:T(8,128)(2,1)} async-done(((bf16[16,144,2048]{2,1,0:T(8,128)(2,1)}), bf16[16,144,2048]{2,1,0:T(8,128)(2,1)}, u32[]{:S(2)}, u32[]{:S(2)}) %all-to-all-start) | async-done | bytes 9437216 | tf_op jit(solution)/shard_map/all_to_all | solution.py:51
  186.5 5.2 %convert_reduce_fusion = f32[2048]{0:T(1024)S(1)} fusion(bf16[16,144,2048]{2,1,0:T(8,128)(2,1)} %all-to-all-done), kind=kLoop, calls=%fused_computation.49 | loop fusion | flops 9435136 | bytes 9445376 | tf_op jit(solution)/shard_map/reduce_sum | solution.py:53
  191.7 0.2 fusion.38
  191.9 7.4 %fusion.22 = bf16[2304,1280]{0,1:T(8,128)(2,1)} fusion(bf16[2304,2048]{1,0:T(8,128)(2,1)} %bitcast, bf16[2048,256]{1,0:T(8,128)(2,1)S(1)} %copy-done), kind=kOutput, calls=%fused_computation.57 | convolution fusion | flops 2417098752 | bytes 11665408 | tf_op jit(solution)/shard_map/dot_general | solution.py:27
  199.3 35.9 %fusion.6 = bf16[1,48,48,2048]{3,2,1,0:T(8,128)(2,1)} fusion(bf16[1,48,48,2048]{3,2,1,0:T(8,128)(2,1)} %bitcast.1, f32[2048]{0:T(1024)S(1)} %bitcast.102, f32[2048]{0:T(1024)S(1)} %bitcast.103, f32[2048]{0:T(1024)S(1)} %bitcast.104, f32[2048]{0:T(1024)S(1)} %bitcast.96, f32[2048]{0:T(1024)S(1)} %bitcast.97, f32[2048]{0:T(1024)S(1)} %bitcast.98, ...), kind=kLoop, calls=%fused_computation.34 | loop fusion | flops 132120576 | bytes 18948096 | tf_op jit(solution)/shard_map/convert_element_type | solution.py:22
  235.2 7.6 %fusion.24 = bf16[2304,1280]{0,1:T(8,128)(2,1)} fusion(bf16[2304,1280]{0,1:T(8,128)(2,1)} %fusion.22, bf16[2304,2048]{1,0:T(8,128)(2,1)} %bitcast.74, bf16[3,2048,256]{2,1,0:T(8,128)(2,1)} %param.10), kind=kOutput, calls=%fused_computation.59 | convolution fusion | flops 2417098752 | bytes 11665408 | tf_op jit(solution)/shard_map/dot_general | solution.py:27
  242.9 20.3 %fusion.13 = bf16[1,48,48,2048]{3,2,1,0:T(8,128)(2,1)S(1)} fusion(bf16[1,48,48,2048]{3,2,1,0:T(8,128)(2,1)} %bitcast.1, f32[2048]{0:T(1024)S(1)} %bitcast.87, f32[2048]{0:T(1024)S(1)} %bitcast.88, f32[2048]{0:T(1024)S(1)} %bitcast.89, f32[2048]{0:T(1024)S(1)} %bitcast.90, f32[2048]{0:T(1024)S(1)} %bitcast.91, f32[2048]{0:T(1024)S(1)} %bitcast.92, ...), kind=kLoop, calls=%fused_computation.41 | loop fusion | flops 132120576 | bytes 18948096 | tf_op jit(solution)/shard_map/convert_element_type | solution.py:22
  263.2 3.0 fusion.26
  266.1 16.3 %fusion.20 = bf16[1,48,48,2048]{3,2,1,0:T(8,128)(2,1)S(1)} fusion(bf16[1,48,48,2048]{3,2,1,0:T(8,128)(2,1)} %bitcast.1, f32[2048]{0:T(1024)S(1)} %bitcast.79, f32[2048]{0:T(1024)S(1)} %bitcast.78, f32[2048]{0:T(1024)S(1)} %bitcast.81, f32[2048]{0:T(1024)S(1)} %bitcast.82, f32[2048]{0:T(1024)S(1)} %bitcast.83, f32[2048]{0:T(1024)S(1)} %bitcast.84, ...), kind=kLoop, calls=%fused_computation.48 | loop fusion | flops 132120576 | bytes 18948096 | tf_op jit(solution)/shard_map/convert_element_type | solution.py:22
  282.5 3.0 fusion.28
  285.4 0.1 broadcast_dynamic-update-slice_fusion
  285.6 1.8 fusion.31
  287.5 0.5 pad_bitcast_fusion
  287.9 0.8 copy.15
  288.7 12.3 %gather_fusion = bf16[3872,256]{1,0:T(8,128)(2,1)} fusion(bf16[2402,256]{1,0:T(8,128)(2,1)S(1)} %copy.15, s32[4096]{0:T(1024)S(1)} %pad_clamp_fusion), kind=kCustom, calls=%fused_computation | custom fusion | bytes 3980416 | tf_op jit(solution)/shard_map/gather | solution.py:71
  301.0 2.8 reshape.574
  303.8 42.0 %all-to-all-start.1 = ((bf16[1,16,242,256]{3,2,0,1:T(8,128)(2,1)}), bf16[1,16,242,256]{3,2,0,1:T(8,128)(2,1)S(1)}, u32[]{:S(2)}, u32[]{:S(2)}) async-start(bf16[1,16,242,256]{3,2,0,1:T(8,128)(2,1)} %bitcast.76), calls=%async_computation.1 | async-start | bytes 4063232 | tf_op jit(solution)/shard_map/all_to_all | solution.py:72
  345.9 41.0 %all-to-all-done.1 = bf16[1,16,242,256]{3,2,0,1:T(8,128)(2,1)S(1)} async-done(((bf16[1,16,242,256]{3,2,0,1:T(8,128)(2,1)}), bf16[1,16,242,256]{3,2,0,1:T(8,128)(2,1)S(1)}, u32[]{:S(2)}, u32[]{:S(2)}) %all-to-all-start.1) | async-done | bytes 1982496 | tf_op jit(solution)/shard_map/all_to_all | solution.py:72
  386.9 3.4 maximum_convert_fusion
  390.4 0.5 fusion.29
  390.9 1.4 copy.18
  (27 shorter events, 0.2 us)
Async XLA Ops:
  0.0 191.9 %copy-start = (bf16[2048,256]{1,0:T(8,128)(2,1)S(1)}, bf16[2048,256]{1,0:T(8,128)(2,1)}, u32[]{:S(2)}) copy-start(bf16[2048,256]{1,0:T(8,128)(2,1)} %param.11) | copy-start | bytes 3145732
  0.0 8.7 %copy-start.3 = (bf16[3,9,2048]{2,0,1:T(4,128)(2,1)S(1)}, bf16[3,9,2048]{2,0,1:T(4,128)(2,1)}, u32[]{:S(2)}) copy-start(bf16[3,9,2048]{2,0,1:T(4,128)(2,1)} %param.9) | copy-start | bytes 331780
  0.0 186.5 %all-to-all-start = ((bf16[16,144,2048]{2,1,0:T(8,128)(2,1)}), bf16[16,144,2048]{2,1,0:T(8,128)(2,1)}, u32[]{:S(2)}, u32[]{:S(2)}) async-start(bf16[16,144,2048]{2,1,0:T(8,128)(2,1)} %param.8), calls=%async_computation | async-start | bytes 18874368 | tf_op jit(solution)/shard_map/all_to_all | solution.py:51
  8.5 183.1 %copy-start.2 = (bf16[2048,256]{1,0:T(8,128)(2,1)S(1)}, bf16[2048,256]{1,0:T(8,128)(2,1)}, u32[]{:S(2)}) copy-start(bf16[2048,256]{1,0:T(8,128)(2,1)} %param.12) | copy-start | bytes 3145732
  242.9 20.3 %copy-start.6 = (bf16[2304,1280]{0,1:T(8,128)(2,1)S(1)}, bf16[2304,1280]{0,1:T(8,128)(2,1)}, u32[]{:S(2)}) copy-start(bf16[2304,1280]{0,1:T(8,128)(2,1)} %fusion.24) | copy-start | bytes 17694724
  242.9 20.3 %copy-start.7 = (bf16[3,2048,256]{2,1,0:T(8,128)(2,1)S(1)}, bf16[3,2048,256]{2,1,0:T(8,128)(2,1)}, u32[]{:S(2)}) copy-start(bf16[3,2048,256]{2,1,0:T(8,128)(2,1)} %param.10) | copy-start | bytes 9437188
  282.5 3.1 copy-start.8
  288.7 57.2 %copy-start.5 = (bf16[9,256]{1,0:T(8,128)(2,1)S(1)}, bf16[9,256]{1,0:T(8,128)(2,1)}, u32[]{:S(2)}) copy-start(bf16[9,256]{1,0:T(8,128)(2,1)} %param.14) | copy-start | bytes 13828
  301.0 89.3 %copy-start.4 = (bf16[256,256]{1,0:T(8,128)(2,1)S(1)}, bf16[256,256]{1,0:T(8,128)(2,1)}, u32[]{:S(2)}) copy-start(bf16[256,256]{1,0:T(8,128)(2,1)} %param.15) | copy-start | bytes 393220
  303.8 88.5 %copy-start.1 = (bf16[2048,256]{1,0:T(8,128)(2,1)S(1)}, bf16[2048,256]{1,0:T(8,128)(2,1)}, u32[]{:S(2)}) copy-start(bf16[2048,256]{1,0:T(8,128)(2,1)} %param.11) | copy-start | bytes 3145732
  303.8 83.1 %all-to-all-start.1 = ((bf16[1,16,242,256]{3,2,0,1:T(8,128)(2,1)}), bf16[1,16,242,256]{3,2,0,1:T(8,128)(2,1)S(1)}, u32[]{:S(2)}, u32[]{:S(2)}) async-start(bf16[1,16,242,256]{3,2,0,1:T(8,128)(2,1)} %bitcast.76), calls=%async_computation.1 | async-start | bytes 4063232 | tf_op jit(solution)/shard_map/all_to_all | solution.py:72
where the time goes:
time: 396 us; the launch traced here: 392 us
  waiting for transfers between devices  219 us (55%)
  other arithmetic  81.4 us (21%)
  starting transfers between devices  50.5 us (13%)
  matrix products  23.5 us (6%)
  local copies, waits for them, and re-layouts  18.1 us (5%)
    all_to_all x1, waiting for transfers between devices, body(): lax.all_to_all(features, 'space', split_axis=0, concat_axis=1, tiled=True)  178 us
    convert_element_type x3, other arithmetic, depthwise(): return jax.nn.relu(total).astype(jnp.bfloat16)  72.6 us
    all_to_all x1, starting transfers between devices, body(): lax.all_to_all(windows, 'space', split_axis=1, concat_axis=0, tiled=True)  42 us
    all_to_all x1, waiting for transfers between devices, body(): lax.all_to_all(windows, 'space', split_axis=1, concat_axis=0, tiled=True)  41 us
    dot_general x6, matrix products, pointwise(): product = jnp.dot(flat, weight, preferred_element_type=jnp.float32)  23.3 us
    gather x2, local copies, waits for them, and re-layouts, body(): windows = flat_context[:, window_index]  15.1 us
    all_to_all x1, starting transfers between devices, body(): lax.all_to_all(features, 'space', split_axis=0, concat_axis=1, tiled=True)  8.49 us
  transfers between devices with their start and end apart: 2, of which 2 were waited for; matrix products, arithmetic and copies ran while one was open for 0% of the time, Pallas kernels for 0%

commit v1 on v0

v1 whole, which is shorter than its diff:
```python
import functools

import jax
import jax.numpy as jnp
from jax import lax
from jax.experimental import pallas as pl
from jax.experimental.pallas import tpu as pltpu
from jax.sharding import PartitionSpec as P

ROWS = 48
COLS = 48
RATE = 12
BANDS = ROWS // RATE
CLASSES = 4
CLASS_ROWS = RATE // CLASSES
BLOCK = CLASS_ROWS * COLS
TILE = 512
HALF = 256
WINDOW = 4
ORDER = (0, 1, 3, 2)
HOPS = (2, 3, 1, 0)
F32 = jnp.float32
BF16 = jnp.bfloat16


def load_tile(info, x_refs, plain, shifted, raw):
    width = plain.shape[-1]

    @pl.when(pl.program_id(0) == 0)
    def _():
        shifted[:, :, 0:8, :] = jnp.zeros((BANDS, CLASS_ROWS, 8, width), F32)
        shifted[:, :, 48:56, :] = jnp.zeros((BANDS, CLASS_ROWS, 8, width), F32)

    for hop in range(BANDS):
        band = jnp.bitwise_xor(info[0], hop)
        block = x_refs[hop][...]
        raw[band] = block
        wide = block.astype(F32).reshape(CLASS_ROWS, COLS, width)
        plain[band] = wide
        shifted[band, :, 4:52, :] = wide


def spread_rows(plain, shifted, taps, spread, row, lane):
    lanes = pl.ds(lane, HALF)
    for branch in range(3):
        weights = [taps[9 * branch + tap, :, lanes] for tap in range(9)]
        for band in range(BANDS):
            tiles = []
            for tile in range(COLS // 8):
                total = None
                for up in (-1, 0, 1):
                    source = band + up * (branch + 1)
                    if not 0 <= source < BANDS:
                        continue
                    for side in (-1, 0, 1):
                        shift = side * RATE * (branch + 1)
                        if 8 * tile + shift + 7 < 0 or 8 * tile + shift >= COLS:
                            continue
                        if shift % 8 == 0:
                            value = plain[source, row, 8 * tile + shift:8 * tile + shift + 8, lanes]
                        else:
                            start = 8 * tile + shift + 4
                            value = shifted[source, row, start:start + 8, lanes]
                        term = value * weights[3 * (up + 1) + (side + 1)]
                        total = term if total is None else total + term
                tiles.append(jnp.maximum(total, 0.0))
            sums = jnp.concatenate(tiles, axis=0).astype(BF16)
            spread[branch, band, pl.ds(pl.multiple_of(row * COLS, COLS), COLS), lanes] = sums


def pyramid_tile(info, x_refs, taps, point, branch, plain, shifted, raw, spread, sums):
    width = plain.shape[-1]
    load_tile(info, x_refs, plain, shifted, raw)

    def step(index, carry):
        spread_rows(plain, shifted, taps, spread, index // (width // HALF),
                    pl.multiple_of((index % (width // HALF)) * HALF, HALF))
        return carry

    lax.fori_loop(0, CLASS_ROWS * (width // HALF), step, 0)
    cells = BANDS * BLOCK
    parts = [jnp.dot(raw[...].reshape(cells, width), branch[...], preferred_element_type=F32)]
    for index in range(3):
        parts.append(
            jnp.dot(spread[index].reshape(cells, width), point[index], preferred_element_type=F32)
        )

    @pl.when(pl.program_id(0) == 0)
    def _():
        for index in range(4):
            sums[index] = parts[index]

    @pl.when(pl.program_id(0) > 0)
    def _():
        for index in range(4):
            sums[index] += parts[index]


def channel_sum(plain):
    width = plain.shape[-1]
    total = jnp.sum(plain[...].reshape(BANDS * BLOCK // 8, 8, width), axis=0)
    return total


def project(sums, weight):
    total = None
    for index in range(4):
        joined = jnp.maximum(sums[index], 0.0).astype(BF16)
        term = jnp.dot(
            joined, weight[HALF * index:HALF * (index + 1), :], preferred_element_type=F32
        )
        total = term if total is None else total + term
    return total


def class_kernel(info, x0, x1, x2, x3, taps, point, branch, weight, out, channel, plain, shifted,
                 raw, spread, sums):
    pyramid_tile(info, (x0, x1, x2, x3), taps, point, branch, plain, shifted, raw, spread, sums)
    channel[...] = channel_sum(plain)

    @pl.when(pl.program_id(0) == pl.num_programs(0) - 1)
    def _():
        out[...] = project(sums, weight)


def last_kernel(info, x0, x1, x2, x3, taps, point, branch, weight, pooling, channel0, channel1,
                channel2, pre0, pre1, pre2, refine_taps, refine_point, out, plain, shifted, raw,
                spread, sums, pool, context, rows):
    pyramid_tile(info, (x0, x1, x2, x3), taps, point, branch, plain, shifted, raw, spread, sums)
    total = channel0[...] + channel1[...] + channel2[...] + channel_sum(plain)
    mean = jnp.sum(total, axis=0, keepdims=True) * (1.0 / (ROWS * COLS))
    mean = jnp.broadcast_to(mean, (16, mean.shape[1])).astype(BF16)
    term = jnp.dot(mean, pooling[...], preferred_element_type=F32)

    @pl.when(pl.program_id(0) == 0)
    def _():
        pool[...] = term
        context[...] = jnp.zeros(context.shape, F32)

    @pl.when(pl.program_id(0) > 0)
    def _():
        pool[...] += term

    @pl.when(pl.program_id(0) == pl.num_programs(0) - 1)
    def _():
        vector = jnp.maximum(pool[...], 0.0).astype(BF16)
        bias = jnp.dot(vector, weight[4 * HALF:5 * HALF, :], preferred_element_type=F32)[0:1, :]
        pres = (pre0[...], pre1[...], pre2[...], project(sums, weight))
        for index, pre in enumerate(pres):
            first = CLASS_ROWS * jnp.bitwise_xor(info[1], ORDER[index])
            value = jnp.maximum(pre + bias, 0.0).astype(BF16).astype(F32)
            value = value.reshape(BANDS, CLASS_ROWS, COLS, HALF)
            for band in range(BANDS):
                for row in range(CLASS_ROWS):
                    context[RATE * band + first + row + 1, 8:56, :] = value[band, row]

        def step(row, carry):
            total = None
            for up in range(3):
                for side in range(3):
                    term = context[row + up, 7 + side:7 + side + COLS, :] * jnp.concatenate(
                        [refine_taps[3 * up + side]] * (COLS // 8), axis=0
                    )
                    total = term if total is None else total + term
            rows[pl.ds(pl.multiple_of(row * COLS, COLS), COLS), :] = jnp.maximum(total, 0.0).astype(BF16)
            return carry

        lax.fori_loop(0, ROWS, step, 0)
        product = jnp.dot(rows[...], refine_point[...], preferred_element_type=F32)
        out[...] = jnp.maximum(product, 0.0).astype(BF16)


def whole(shape):
    return pl.BlockSpec(shape, lambda i, info: (0,) * len(shape))


def pyramid_specs(channels):
    specs = [pl.BlockSpec((BLOCK, TILE), lambda i, info: (0, i)) for _ in range(BANDS)]
    specs.append(pl.BlockSpec((27, 8, TILE), lambda i, info: (0, 0, i)))
    specs.append(pl.BlockSpec((3, TILE, HALF), lambda i, info: (0, i, 0)))
    specs.append(pl.BlockSpec((TILE, HALF), lambda i, info: (i, 0)))
    specs.append(whole((5 * HALF, HALF)))
    return specs


def pyramid_scratch():
    return [
        pltpu.VMEM((BANDS, CLASS_ROWS, COLS, TILE), F32),
        pltpu.VMEM((BANDS, CLASS_ROWS, COLS + 8, TILE), F32),
        pltpu.VMEM((BANDS, BLOCK, TILE), BF16),
        pltpu.VMEM((3, BANDS, BLOCK, TILE), BF16),
        pltpu.VMEM((4, BANDS * BLOCK, HALF), F32),
    ]


PARAMS = pltpu.CompilerParams(
    dimension_semantics=("arbitrary",), vmem_limit_bytes=52 * 1024 * 1024
)


def class_call(info, blocks, taps, point, branch, weight):
    channels = blocks[0].shape[1]
    return pl.pallas_call(
        class_kernel,
        grid_spec=pltpu.PrefetchScalarGridSpec(
            num_scalar_prefetch=1,
            grid=(channels // TILE,),
            in_specs=pyramid_specs(channels),
            out_specs=[
                whole((BANDS * BLOCK, HALF)),
                pl.BlockSpec((8, TILE), lambda i, info: (0, i)),
            ],
            scratch_shapes=pyramid_scratch(),
        ),
        out_shape=[
            jax.ShapeDtypeStruct((BANDS * BLOCK, HALF), F32),
            jax.ShapeDtypeStruct((8, channels), F32),
        ],
        compiler_params=PARAMS,
        name="pyramid_class",
    )(info, *blocks, taps, point, branch, weight)


def last_call(info, blocks, taps, point, branch, weight, pooling, channel, pres, refine_taps, refine_point):
    channels = blocks[0].shape[1]
    specs = pyramid_specs(channels)
    specs.append(pl.BlockSpec((TILE, HALF), lambda i, info: (i, 0)))
    specs += [pl.BlockSpec((8, TILE), lambda i, info: (0, i)) for _ in range(3)]
    specs += [whole((BANDS * BLOCK, HALF)) for _ in range(3)]
    specs += [whole((9, 8, HALF)), whole((HALF, HALF))]
    return pl.pallas_call(
        last_kernel,
        grid_spec=pltpu.PrefetchScalarGridSpec(
            num_scalar_prefetch=1,
            grid=(channels // TILE,),
            in_specs=specs,
            out_specs=whole((ROWS * COLS, HALF)),
            scratch_shapes=pyramid_scratch() + [
                pltpu.VMEM((16, HALF), F32),
                pltpu.VMEM((ROWS + 2, COLS + 16, HALF), F32),
                pltpu.VMEM((ROWS * COLS, HALF), BF16),
            ],
        ),
        out_shape=jax.ShapeDtypeStruct((ROWS * COLS, HALF), BF16),
        compiler_params=PARAMS,
        name="pyramid_last",
    )(info, *blocks, taps, point, branch, weight, pooling, *channel, *pres, refine_taps, refine_point)


def exchange(features):
    parts = lax.axis_size("space")
    block = features.shape[1]
    channels = features.shape[2]
    sub = BLOCK // block
    me = lax.axis_index("space").astype(jnp.int32)
    sent = []
    classes = []
    for kind in ORDER:
        blocks = {}
        for hop in HOPS:
            pieces = []
            for piece in range(sub):
                distance = (hop * CLASSES + kind) * sub + piece
                target = jnp.bitwise_xor(me, distance)
                if distance and len(sent) >= WINDOW:
                    target, _ = lax.optimization_barrier((target, sent[len(sent) - WINDOW]))
                value = lax.dynamic_slice_in_dim(features, target, 1, 0)
                if distance:
                    value = lax.ppermute(value, "space", [(i, i ^ distance) for i in range(parts)])
                    sent.append(value)
                pieces.append(value.reshape(block, channels))
            if sub == 1:
                blocks[hop] = pieces[0]
            else:
                joined = jnp.zeros((BLOCK, channels), features.dtype)
                for piece in range(sub):
                    start = jnp.bitwise_xor(me % sub, piece) * block
                    joined = lax.dynamic_update_slice(joined, pieces[piece], (start, 0))
                blocks[hop] = joined
        classes.append([blocks[hop] for hop in range(BANDS)])
    return me, sub, classes


def body(
    features,
    depth_weights,
    point_weights,
    branch_weight,
    pooling_weight,
    project_weight,
    refine_depth,
    refine_point,
):
    parts = lax.axis_size("space")
    assert features.shape[0] == parts
    block = features.shape[1]
    channels = features.shape[2]
    taps = jnp.broadcast_to(depth_weights.reshape(27, 1, channels).astype(F32), (27, 8, channels))
    refine_taps = jnp.broadcast_to(refine_depth.reshape(9, 1, HALF).astype(F32), (9, 8, HALF))
    me, sub, classes = exchange(features)
    info = jnp.stack([me // (CLASSES * sub), (me // sub) % CLASSES])
    shared = (taps, point_weights, branch_weight, project_weight)
    pres = []
    channel = []
    for blocks in classes[:3]:
        pre, total = class_call(info, blocks, *shared)
        pres.append(pre)
        channel.append(total)
    refined = last_call(
        info, classes[3], *shared, pooling_weight, channel, pres, refine_taps, refine_point
    )
    return lax.all_to_all(refined.reshape(parts, block, HALF), "space", 0, 0, tiled=True)


def solution(mesh):
    return jax.shard_map(
        body,
        mesh=mesh,
        in_specs=(P("dp", "space", None), P(), P(), P(), P(), P(), P(), P()),
        out_specs=P("dp", "space", None),
        check_vma=False,
    )
```

time: 396 us -> 306 us (0.77)
  other arithmetic: 81.4 us -> 0.07 us
  waiting for transfers between devices: 219 us -> 144 us
  Pallas kernels: 0 us -> 59.1 us
  blocking collectives: 0 us -> 55.5 us
  starting transfers between devices: 50.5 us -> 26.2 us
  matrix products: 23.5 us -> 0 us
    all_to_all x2 -> x0, waiting for transfers between devices: 219 us -> none  [the longest x1 178 us: body(): lax.all_to_all(features, 'space', split_axis=0, concat_axis=1, tiled=True)]
    ppermute x0 -> x15, waiting for transfers between devices: none -> 144 us  [exchange(): lax.ppermute(value, 'space', [(i, i ^ distance) for i in range(parts)])]
    convert_element_type x10 -> x0, other arithmetic: 76.2 us -> none  [the longest x3 72.6 us: depthwise(): return jax.nn.relu(total).astype(jnp.bfloat16)]
    pallas_call x0 -> x4, Pallas kernels: none -> 59.1 us  [the longest x3 38.7 us: class_call(): pl.pallas_call(class_kernel, grid_spec=pltpu.PrefetchScalarGridSpec(num_s...]
    all_to_all x0 -> x1, blocking collectives: none -> 55.5 us  [body(): lax.all_to_all(refined.reshape(parts, block, HALF), 'space', 0, 0, tiled=...]
    all_to_all x2 -> x0, starting transfers between devices: 50.5 us -> none  [the longest x1 42 us: body(): lax.all_to_all(windows, 'space', split_axis=1, concat_axis=0, tiled=True)]
    ppermute x0 -> x15, starting transfers between devices: none -> 26.2 us  [exchange(): lax.ppermute(value, 'space', [(i, i ^ distance) for i in range(parts)])]
    dot_general x7 -> x0, matrix products: 23.5 us -> none  [the longest x6 23.3 us: pointwise(): product = jnp.dot(flat, weight, preferred_element_type=jnp.float32)]
  transfers between devices with their start and end apart: 2 -> 15, of which waited for: 2 -> 8; matrix products, arithmetic and copies ran while one was open for 0% -> 3% of each run, Pallas kernels for 0% -> 13%
where the time goes in v1:
time: 306 us
  waiting for transfers between devices  144 us (47%)
  Pallas kernels  59.1 us (19%)
  blocking collectives  55.5 us (18%)
  starting transfers between devices  26.2 us (9%)
  local copies, waits for them, and re-layouts  21.2 us (7%)
    ppermute x15, waiting for transfers between devices, exchange(): lax.ppermute(value, 'space', [(i, i ^ distance) for i in range(parts)])  144 us
    all_to_all x1, blocking collectives, body(): lax.all_to_all(refined.reshape(parts, block, HALF), 'space', 0, 0, tiled=...  55.5 us
    pallas_call x3, Pallas kernels, class_call(): pl.pallas_call(class_kernel, grid_spec=pltpu.PrefetchScalarGridSpec(num_s...  38.7 us
    ppermute x15, starting transfers between devices, exchange(): lax.ppermute(value, 'space', [(i, i ^ distance) for i in range(parts)])  26.2 us
    pallas_call x1, Pallas kernels, last_call(): pl.pallas_call(last_kernel, grid_spec=pltpu.PrefetchScalarGridSpec(num_sc...  20.3 us
    dynamic_slice x4, local copies, waits for them, and re-layouts, exchange(): value = lax.dynamic_slice_in_dim(features, target, 1, 0)  9.37 us
  transfers between devices with their start and end apart: 15, of which 8 were waited for; matrix products, arithmetic and copies ran while one was open for 3% of the time, Pallas kernels for 13%

profile of v1, /device:TPU:0, one launch (start us, length us, event | category | flops | bytes accessed | tf_op | source)
XLA Modules:
  0.0 305.7 jit_solution(10010062246164307861)
XLA Ops:
  1.3 5.1 %collective-permute-start.4 = (bf16[1,144,2048]{2,1,0:T(8,128)(2,1)S(1)}, bf16[1,144,2048]{2,1,0:T(8,128)(2,1)S(1)}, u32[]{:S(2)}, u32[]{:S(2)}) collective-permute-start(bf16[1,144,2048]{2,1,0:T(8,128)(2,1)S(1)} %get-tuple-element.52), channel_id=1, source_target_pairs={{0,12},{1,13},{2,14},{3,15},{4,8},{5,9},{6,10},{7,11},{8,4},{9,5},... | collective-permute-start | bytes 1769480 | tf_op jit(solution)/shard_map/ppermute | solution.py:269
  6.4 14.2 %collective-permute-done.4 = bf16[1,144,2048]{2,1,0:T(8,128)(2,1)S(1)} collective-permute-done((bf16[1,144,2048]{2,1,0:T(8,128)(2,1)S(1)}, bf16[1,144,2048]{2,1,0:T(8,128)(2,1)S(1)}, u32[]{:S(2)}, u32[]{:S(2)}) %collective-permute-start.4) | collective-permute-done | bytes 589856 | tf_op jit(solution)/shard_map/ppermute | solution.py:269
  20.7 11.8 %collective-permute-done = bf16[1,144,2048]{2,1,0:T(8,128)(2,1)S(1)} collective-permute-done((bf16[1,144,2048]{2,1,0:T(8,128)(2,1)S(1)}, bf16[1,144,2048]{2,1,0:T(8,128)(2,1)S(1)}, u32[]{:S(2)}, u32[]{:S(2)}) %collective-permute-start) | collective-permute-done | bytes 589856 | tf_op jit(solution)/shard_map/ppermute | solution.py:269
  32.5 2.9 constant_dynamic-slice_fusion.3
  36.2 3.0 collective-permute-start.8
  42.4 34.8 %collective-permute-done.11 = bf16[1,144,2048]{2,1,0:T(8,128)(2,1)S(1)} collective-permute-done((bf16[1,144,2048]{2,1,0:T(8,128)(2,1)}, bf16[1,144,2048]{2,1,0:T(8,128)(2,1)S(1)}, u32[]{:S(2)}, u32[]{:S(2)}) %collective-permute-start.11) | collective-permute-done | bytes 589856 | tf_op jit(solution)/shard_map/ppermute | solution.py:269
  77.2 13.4 %collective-permute-done.8 = bf16[1,144,2048]{2,1,0:T(8,128)(2,1)S(1)} collective-permute-done((bf16[1,144,2048]{2,1,0:T(8,128)(2,1)}, bf16[1,144,2048]{2,1,0:T(8,128)(2,1)S(1)}, u32[]{:S(2)}, u32[]{:S(2)}) %collective-permute-start.8) | collective-permute-done | bytes 589856 | tf_op jit(solution)/shard_map/ppermute | solution.py:269
  90.6 3.3 %constant_dynamic-slice_fusion.2 = (bf16[1,144,2048]{2,1,0:T(8,128)(2,1)}, bf16[1,144,2048]{2,1,0:T(8,128)(2,1)}, bf16[1,144,2048]{2,1,0:T(8,128)(2,1)}, bf16[1,144,2048]{2,1,0:T(8,128)(2,1)}) fusion(bf16[16,144,2048]{2,1,0:T(8,128)(2,1)} %param.8, s32[]{:T(128)S(6)} %select_n.74, s32[]{:T(128)S(6)} %select_n.71, s32[]{:T(128)S(6)} %select_n.68, s32[]{:T(128)S(6)} %select_n.64), kind=kLoop, calls=%fused_computation.3 | loop fusion | bytes 4718608 | tf_op jit(solution)/shard_map/dynamic_slice | solution.py:267
  94.5 5.5 %collective-permute-start.6 = (bf16[1,144,2048]{2,1,0:T(8,128)(2,1)}, bf16[1,144,2048]{2,1,0:T(8,128)(2,1)S(1)}, u32[]{:S(2)}, u32[]{:S(2)}) collective-permute-start(bf16[1,144,2048]{2,1,0:T(8,128)(2,1)} %get-tuple-element.46), channel_id=1, source_target_pairs={{0,7},{1,6},{2,5},{3,4},{4,3},{5,2},{6,1},{7,0},{8,15},{9,14},{10,... | collective-permute-start | bytes 1769480 | tf_op jit(solution)/shard_map/ppermute | solution.py:269
  100.0 2.4 collective-permute-start.2
  102.5 10.8 %collective-permute-done.12 = bf16[1,144,2048]{2,1,0:T(8,128)(2,1)} collective-permute-done((bf16[1,144,2048]{2,1,0:T(8,128)(2,1)}, bf16[1,144,2048]{2,1,0:T(8,128)(2,1)}, u32[]{:S(2)}, u32[]{:S(2)}) %collective-permute-start.12) | collective-permute-done | bytes 589856 | tf_op jit(solution)/shard_map/ppermute | solution.py:269
  113.3 41.9 %collective-permute-done.9 = bf16[1,144,2048]{2,1,0:T(8,128)(2,1)S(1)} collective-permute-done((bf16[1,144,2048]{2,1,0:T(8,128)(2,1)}, bf16[1,144,2048]{2,1,0:T(8,128)(2,1)S(1)}, u32[]{:S(2)}, u32[]{:S(2)}) %collective-permute-start.9) | collective-permute-done | bytes 589856 | tf_op jit(solution)/shard_map/ppermute | solution.py:269
  156.0 3.3 %dynamic-slice_bitcast_fusion = (bf16[144,2048]{1,0:T(8,128)(2,1)S(1)}, bf16[1,144,2048]{2,1,0:T(8,128)(2,1)}, bf16[1,144,2048]{2,1,0:T(8,128)(2,1)}, bf16[1,144,2048]{2,1,0:T(8,128)(2,1)}, bf16[1,144,2048]{2,1,0:T(8,128)(2,1)}) fusion(bf16[16,144,2048]{2,1,0:T(8,128)(2,1)} %param.8, s32[]{:T(128)S(6)} %select_n.77, s32[]{:T(128)S(6)} %select_n.75, ...), kind=kLoop, calls=%fused_computation | loop fusion | bytes 5898260 | tf_op jit(solution)/shard_map/reshape | solution.py:271
  159.3 2.4 collective-permute-start.13
  164.8 16.5 %collective-permute-done.13 = bf16[1,144,2048]{2,1,0:T(8,128)(2,1)} collective-permute-done((bf16[1,144,2048]{2,1,0:T(8,128)(2,1)}, bf16[1,144,2048]{2,1,0:T(8,128)(2,1)}, u32[]{:S(2)}, u32[]{:S(2)}) %collective-permute-start.13) | collective-permute-done | bytes 589856 | tf_op jit(solution)/shard_map/ppermute | solution.py:269
  181.3 1.9 constant_dynamic-slice_fusion
  183.2 1.8 copy.9
  185.0 1.7 reshape.81
  186.8 2.4 broadcast_in_dim.4.taps
  189.2 12.9 %pyramid_class.4 = (f32[576,256]{1,0:T(8,128)S(1)}, f32[8,2048]{1,0:T(8,128)S(1)}) custom-call(s32[2]{0:T(128)S(1)} %pad_add_fusion.info, bf16[144,2048]{1,0:T(8,128)(2,1)S(1)} %bitcast.22, bf16[144,2048]{1,0:T(8,128)(2,1)S(1)} %bitcast.21, bf16[144,2048]{1,0:T(8,128)(2,1)} %bitcast.28, bf16[144,2048]{1,0:T(8,128)(2,1)} %bitcast.13.x3, ...), custom_call_target="tpu_custom_call" | custom-call | tf_op jit(solution)/shard_map/pyramid_class/pallas_call | solution.py:203
  202.1 12.9 %pyramid_class.3 = (f32[576,256]{1,0:T(8,128)S(1)}, f32[8,2048]{1,0:T(8,128)S(1)}) custom-call(s32[2]{0:T(128)S(1)} %pad_add_fusion.info, bf16[144,2048]{1,0:T(8,128)(2,1)S(1)} %get-tuple-element.39.x0, bf16[144,2048]{1,0:T(8,128)(2,1)S(1)} %bitcast.20, bf16[144,2048]{1,0:T(8,128)(2,1)} %bitcast.27, bf16[144,2048]{1,0:T(8,128)(2,1)} %bitcast.26, ...), custom_call_target="tpu_custom_call" | custom-call | tf_op jit(solution)/shard_map/pyramid_class/pallas_call | solution.py:203
  215.1 12.9 %pyramid_class.5 = (f32[576,256]{1,0:T(8,128)S(1)}, f32[8,2048]{1,0:T(8,128)S(1)}) custom-call(s32[2]{0:T(128)S(1)} %pad_add_fusion.info, bf16[144,2048]{1,0:T(8,128)(2,1)S(1)} %bitcast.24, bf16[144,2048]{1,0:T(8,128)(2,1)S(1)} %bitcast.23, bf16[144,2048]{1,0:T(8,128)(2,1)} %bitcast.29, bf16[144,2048]{1,0:T(8,128)(2,1)} %bitcast.17.x3, ...), custom_call_target="tpu_custom_call" | custom-call | tf_op jit(solution)/shard_map/pyramid_class/pallas_call | solution.py:203
  228.9 20.3 %pyramid_last.1 = bf16[2304,256]{1,0:T(8,128)(2,1)} custom-call(s32[2]{0:T(128)S(1)} %pad_add_fusion.info, bf16[144,2048]{1,0:T(8,128)(2,1)} %bitcast.2.x0, bf16[144,2048]{1,0:T(8,128)(2,1)} %bitcast.3.x1, bf16[144,2048]{1,0:T(8,128)(2,1)} %bitcast.4.x2, bf16[144,2048]{1,0:T(8,128)(2,1)} %bitcast.5.x3, f32[27,8,2048]{2,1,0:T(8,128)} %broadcast_in_dim.4.taps, ...), custom_call_target="tpu_custom_call" | custom-call | tf_op jit(solution)/shard_map/pyramid_last/pallas_call | solution.py:231
  249.3 55.5 %all_to_all.5 = bf16[16,144,256]{2,1,0:T(8,128)(2,1)S(1)} all-to-all(bf16[16,144,256]{2,1,0:T(8,128)(2,1)} %bitcast.25), channel_id=1, replica_groups=mesh['dp'=2,'space'=16] {'space'}, dimensions={0} | all-to-all | bytes 2359296 | tf_op jit(solution)/shard_map/all_to_all | solution.py:312
  (40 shorter events, 11.9 us)
Async XLA Ops:
  1.3 19.4 %collective-permute-start.4 = (bf16[1,144,2048]{2,1,0:T(8,128)(2,1)S(1)}, bf16[1,144,2048]{2,1,0:T(8,128)(2,1)S(1)}, u32[]{:S(2)}, u32[]{:S(2)}) collective-permute-start(bf16[1,144,2048]{2,1,0:T(8,128)(2,1)S(1)} %get-tuple-element.52), channel_id=1, source_target_pairs={{0,12},{1,13},{2,14},{3,15},{4,8},{5,9},{6,10},{7,11},{8,4},{9,5},... | collective-permute-start | bytes 1769480 | tf_op jit(solution)/shard_map/ppermute | solution.py:269
  6.4 26.1 %collective-permute-start = (bf16[1,144,2048]{2,1,0:T(8,128)(2,1)S(1)}, bf16[1,144,2048]{2,1,0:T(8,128)(2,1)S(1)}, u32[]{:S(2)}, u32[]{:S(2)}) collective-permute-start(bf16[1,144,2048]{2,1,0:T(8,128)(2,1)S(1)} %get-tuple-element.53), channel_id=1, source_target_pairs={{0,4},{1,5},{2,6},{3,7},{4,0},{5,1},{6,2},{7,3},{8,12},{9,13},{10,... | collective-permute-start | bytes 1769480 | tf_op jit(solution)/shard_map/ppermute | solution.py:269
  20.7 18.5 %copy-start.4 = (bf16[1,144,2048]{2,1,0:T(8,128)(2,1)}, bf16[1,144,2048]{2,1,0:T(8,128)(2,1)S(1)}, u32[]{:S(2)}) copy-start(bf16[1,144,2048]{2,1,0:T(8,128)(2,1)S(1)} %collective-permute-done.4) | copy-start | bytes 1769476
  35.4 41.8 %collective-permute-start.11 = (bf16[1,144,2048]{2,1,0:T(8,128)(2,1)}, bf16[1,144,2048]{2,1,0:T(8,128)(2,1)S(1)}, u32[]{:S(2)}, u32[]{:S(2)}) collective-permute-start(bf16[1,144,2048]{2,1,0:T(8,128)(2,1)} %get-tuple-element.48), channel_id=1, source_target_pairs={{0,8},{1,9},{2,10},{3,11},{4,12},{5,13},{6,14},{7,15},{8,0},{9,1},... | collective-permute-start | bytes 1769480 | tf_op jit(solution)/shard_map/ppermute | solution.py:269
  36.2 54.4 %collective-permute-start.8 = (bf16[1,144,2048]{2,1,0:T(8,128)(2,1)}, bf16[1,144,2048]{2,1,0:T(8,128)(2,1)S(1)}, u32[]{:S(2)}, u32[]{:S(2)}) collective-permute-start(bf16[1,144,2048]{2,1,0:T(8,128)(2,1)} %get-tuple-element.49), channel_id=1, source_target_pairs={{0,9},{1,8},{2,11},{3,10},{4,13},{5,12},{6,15},{7,14},{8,1},{9,0},... | collective-permute-start | bytes 1769480 | tf_op jit(solution)/shard_map/ppermute | solution.py:269
  39.2 51.4 %collective-permute-start.5 = (bf16[1,144,2048]{2,1,0:T(8,128)(2,1)}, bf16[1,144,2048]{2,1,0:T(8,128)(2,1)S(1)}, u32[]{:S(2)}, u32[]{:S(2)}) collective-permute-start(bf16[1,144,2048]{2,1,0:T(8,128)(2,1)} %get-tuple-element.50), channel_id=1, source_target_pairs={{0,5},{1,4},{2,7},{3,6},{4,1},{5,0},{6,3},{7,2},{8,13},{9,12},{10,... | collective-permute-start | bytes 1769480 | tf_op jit(solution)/shard_map/ppermute | solution.py:269
  40.9 49.7 %collective-permute-start.1 = (bf16[1,144,2048]{2,1,0:T(8,128)(2,1)S(1)}, bf16[1,144,2048]{2,1,0:T(8,128)(2,1)S(1)}, u32[]{:S(2)}, u32[]{:S(2)}) collective-permute-start(bf16[1,144,2048]{2,1,0:T(8,128)(2,1)S(1)} %get-tuple-element.51), channel_id=1, source_target_pairs={{0,1},{1,0},{2,3},{3,2},{4,5},{5,4},{6,7},{7,6},{8,9},{9,8},{10,11... | collective-permute-start | bytes 1769480 | tf_op jit(solution)/shard_map/ppermute | solution.py:269
  77.2 17.3 %copy-start.5 = (bf16[1,144,2048]{2,1,0:T(8,128)(2,1)}, bf16[1,144,2048]{2,1,0:T(8,128)(2,1)S(1)}, u32[]{:S(2)}) copy-start(bf16[1,144,2048]{2,1,0:T(8,128)(2,1)S(1)} %collective-permute-done.11) | copy-start | bytes 1769476
  90.6 9.5 %copy-start.6 = (bf16[1,144,2048]{2,1,0:T(8,128)(2,1)}, bf16[1,144,2048]{2,1,0:T(8,128)(2,1)S(1)}, u32[]{:S(2)}) copy-start(bf16[1,144,2048]{2,1,0:T(8,128)(2,1)S(1)} %collective-permute-done.8) | copy-start | bytes 1769476
  93.9 19.4 %collective-permute-start.12 = (bf16[1,144,2048]{2,1,0:T(8,128)(2,1)}, bf16[1,144,2048]{2,1,0:T(8,128)(2,1)}, u32[]{:S(2)}, u32[]{:S(2)}) collective-permute-start(bf16[1,144,2048]{2,1,0:T(8,128)(2,1)} %get-tuple-element.44), channel_id=1, source_target_pairs={{0,13},{1,12},{2,15},{3,14},{4,9},{5,8},{6,11},{7,10},{8,5},{9,4},... | collective-permute-start | bytes 1769480 | tf_op jit(solution)/shard_map/ppermute | solution.py:269
  94.5 60.7 %collective-permute-start.9 = (bf16[1,144,2048]{2,1,0:T(8,128)(2,1)}, bf16[1,144,2048]{2,1,0:T(8,128)(2,1)S(1)}, u32[]{:S(2)}, u32[]{:S(2)}) collective-permute-start(bf16[1,144,2048]{2,1,0:T(8,128)(2,1)} %get-tuple-element.45), channel_id=1, source_target_pairs={{0,11},{1,10},{2,9},{3,8},{4,15},{5,14},{6,13},{7,12},{8,3},{9,2},... | collective-permute-start | bytes 1769480 | tf_op jit(solution)/shard_map/ppermute | solution.py:269
  94.5 60.7 %collective-permute-start.6 = (bf16[1,144,2048]{2,1,0:T(8,128)(2,1)}, bf16[1,144,2048]{2,1,0:T(8,128)(2,1)S(1)}, u32[]{:S(2)}, u32[]{:S(2)}) collective-permute-start(bf16[1,144,2048]{2,1,0:T(8,128)(2,1)} %get-tuple-element.46), channel_id=1, source_target_pairs={{0,7},{1,6},{2,5},{3,4},{4,3},{5,2},{6,1},{7,0},{8,15},{9,14},{10,... | collective-permute-start | bytes 1769480 | tf_op jit(solution)/shard_map/ppermute | solution.py:269
  100.0 55.1 %collective-permute-start.2 = (bf16[1,144,2048]{2,1,0:T(8,128)(2,1)}, bf16[1,144,2048]{2,1,0:T(8,128)(2,1)S(1)}, u32[]{:S(2)}, u32[]{:S(2)}) collective-permute-start(bf16[1,144,2048]{2,1,0:T(8,128)(2,1)} %get-tuple-element.47), channel_id=1, source_target_pairs={{0,3},{1,2},{2,1},{3,0},{4,7},{5,6},{6,5},{7,4},{8,11},{9,10},{10,... | collective-permute-start | bytes 1769480 | tf_op jit(solution)/shard_map/ppermute | solution.py:269
  155.2 0.8 copy-start.7
  159.3 22.0 %collective-permute-start.13 = (bf16[1,144,2048]{2,1,0:T(8,128)(2,1)}, bf16[1,144,2048]{2,1,0:T(8,128)(2,1)}, u32[]{:S(2)}, u32[]{:S(2)}) collective-permute-start(bf16[1,144,2048]{2,1,0:T(8,128)(2,1)} %get-tuple-element.40), channel_id=1, source_target_pairs={{0,15},{1,14},{2,13},{3,12},{4,11},{5,10},{6,9},{7,8},{8,7},{9,6},... | collective-permute-start | bytes 1769480 | tf_op jit(solution)/shard_map/ppermute | solution.py:269
  161.7 67.2 %collective-permute-start.10 = (bf16[1,144,2048]{2,1,0:T(8,128)(2,1)}, bf16[1,144,2048]{2,1,0:T(8,128)(2,1)}, u32[]{:S(2)}, u32[]{:S(2)}) collective-permute-start(bf16[1,144,2048]{2,1,0:T(8,128)(2,1)} %get-tuple-element.41), channel_id=1, source_target_pairs={{0,10},{1,11},{2,8},{3,9},{4,14},{5,15},{6,12},{7,13},{8,2},{9,3},... | collective-permute-start | bytes 1769480 | tf_op jit(solution)/shard_map/ppermute | solution.py:269
  161.7 67.2 %collective-permute-start.7 = (bf16[1,144,2048]{2,1,0:T(8,128)(2,1)}, bf16[1,144,2048]{2,1,0:T(8,128)(2,1)}, u32[]{:S(2)}, u32[]{:S(2)}) collective-permute-start(bf16[1,144,2048]{2,1,0:T(8,128)(2,1)} %get-tuple-element.42), channel_id=1, source_target_pairs={{0,6},{1,7},{2,4},{3,5},{4,2},{5,3},{6,0},{7,1},{8,14},{9,15},{10,... | collective-permute-start | bytes 1769480 | tf_op jit(solution)/shard_map/ppermute | solution.py:269
  163.4 65.5 %collective-permute-start.3 = (bf16[1,144,2048]{2,1,0:T(8,128)(2,1)}, bf16[1,144,2048]{2,1,0:T(8,128)(2,1)}, u32[]{:S(2)}, u32[]{:S(2)}) collective-permute-start(bf16[1,144,2048]{2,1,0:T(8,128)(2,1)} %get-tuple-element.43), channel_id=1, source_target_pairs={{0,2},{1,3},{2,0},{3,1},{4,6},{5,7},{6,4},{7,5},{8,10},{9,11},{10,... | collective-permute-start | bytes 1769480 | tf_op jit(solution)/shard_map/ppermute | solution.py:269
  183.2 45.7 %collective-permute-start.14 = (bf16[1,144,2048]{2,1,0:T(8,128)(2,1)}, bf16[1,144,2048]{2,1,0:T(8,128)(2,1)}, u32[]{:S(2)}, u32[]{:S(2)}) collective-permute-start(bf16[1,144,2048]{2,1,0:T(8,128)(2,1)} %constant_dynamic-slice_fusion), channel_id=1, source_target_pairs={{0,14},{1,15},{2,12},{3,13},{4,10},{5,11},{6,8},{7,9},{8,6},{9,7},... | collective-permute-start | bytes 1769480 | tf_op jit(solution)/shard_map/ppermute | solution.py:269
  202.1 25.9 %copy-start = (f32[576,256]{1,0:T(8,128)}, f32[576,256]{1,0:T(8,128)S(1)}, u32[]{:S(2)}) copy-start(f32[576,256]{1,0:T(8,128)S(1)} %get-tuple-element.37.pre1) | copy-start | bytes 1769476
  202.1 26.8 %copy-start.8 = (bf16[9,256]{1,0:T(8,128)(2,1)S(1)}, bf16[9,256]{1,0:T(8,128)(2,1)}, u32[]{:S(2)}) copy-start(bf16[9,256]{1,0:T(8,128)(2,1)} %param.14) | copy-start | bytes 13828
  202.1 26.8 %copy-start.3 = (bf16[256,256]{1,0:T(8,128)(2,1)S(1)}, bf16[256,256]{1,0:T(8,128)(2,1)}, u32[]{:S(2)}) copy-start(bf16[256,256]{1,0:T(8,128)(2,1)} %refine_point.1) | copy-start | bytes 393220
  215.1 13.8 %copy-start.1 = (f32[576,256]{1,0:T(8,128)}, f32[576,256]{1,0:T(8,128)S(1)}, u32[]{:S(2)}) copy-start(f32[576,256]{1,0:T(8,128)S(1)} %get-tuple-element.36.pre0) | copy-start | bytes 1769476
  228.0 0.8 copy-start.2

commit v2 on v1

--- a/solution.py
+++ b/solution.py
@@ -247,25 +247,42 @@
     )(info, *blocks, taps, point, branch, weight, pooling, *channel, *pres, refine_taps, refine_point)
 
 
-def exchange(features):
+def exchange(features, consume):
     parts = lax.axis_size("space")
     block = features.shape[1]
     channels = features.shape[2]
     sub = BLOCK // block
     me = lax.axis_index("space").astype(jnp.int32)
+    first = None
+    values = {}
+    for kind in ORDER:
+        origin = me
+        if first is not None:
+            origin, _ = lax.optimization_barrier((me, first))
+        for hop in HOPS:
+            for piece in range(sub):
+                distance = (hop * CLASSES + kind) * sub + piece
+                target = jnp.bitwise_xor(origin, distance)
+                values[distance] = lax.dynamic_slice_in_dim(features, target, 1, 0)
+        if first is None:
+            first = values[HOPS[0] * CLASSES * sub]
     sent = []
-    classes = []
-    for kind in ORDER:
+    results = []
+    for index, kind in enumerate(ORDER):
         blocks = {}
-        for hop in HOPS:
+        for order, hop in enumerate(HOPS):
             pieces = []
             for piece in range(sub):
                 distance = (hop * CLASSES + kind) * sub + piece
-                target = jnp.bitwise_xor(me, distance)
-                if distance and len(sent) >= WINDOW:
-                    target, _ = lax.optimization_barrier((target, sent[len(sent) - WINDOW]))
-                value = lax.dynamic_slice_in_dim(features, target, 1, 0)
+                value = values[distance]
                 if distance:
+                    before = []
+                    if len(sent) >= WINDOW:
+                        before.append(sent[len(sent) - WINDOW])
+                    if order == 0 and index >= 2:
+                        before.append(results[index - 2])
+                    if before:
+                        value, _ = lax.optimization_barrier((value, before))
                     value = lax.ppermute(value, "space", [(i, i ^ distance) for i in range(parts)])
                     sent.append(value)
                 pieces.append(value.reshape(block, channels))
@@ -277,8 +294,8 @@
                     start = jnp.bitwise_xor(me % sub, piece) * block
                     joined = lax.dynamic_update_slice(joined, pieces[piece], (start, 0))
                 blocks[hop] = joined
-        classes.append([blocks[hop] for hop in range(BANDS)])
-    return me, sub, classes
+        results.append(consume(index, [blocks[hop] for hop in range(BANDS)]))
+    return results
 
 
 def body(
@@ -297,18 +314,22 @@
     channels = features.shape[2]
     taps = jnp.broadcast_to(depth_weights.reshape(27, 1, channels).astype(F32), (27, 8, channels))
     refine_taps = jnp.broadcast_to(refine_depth.reshape(9, 1, HALF).astype(F32), (9, 8, HALF))
-    me, sub, classes = exchange(features)
+    me = lax.axis_index("space").astype(jnp.int32)
+    sub = BLOCK // block
     info = jnp.stack([me // (CLASSES * sub), (me // sub) % CLASSES])
     shared = (taps, point_weights, branch_weight, project_weight)
-    pres = []
-    channel = []
-    for blocks in classes[:3]:
-        pre, total = class_call(info, blocks, *shared)
-        pres.append(pre)
-        channel.append(total)
-    refined = last_call(
-        info, classes[3], *shared, pooling_weight, channel, pres, refine_taps, refine_point
-    )
+    done = []
+
+    def consume(index, blocks):
+        if index < 3:
+            done.append(class_call(info, blocks, *shared))
+            return done[-1]
+        return last_call(
+            info, blocks, *shared, pooling_weight, [item[1] for item in done],
+            [item[0] for item in done], refine_taps, refine_point
+        )
+
+    refined = exchange(features, consume)[-1]
     return lax.all_to_all(refined.reshape(parts, block, HALF), "space", 0, 0, tiled=True)
 
 

time: 306 us -> 287 us (0.938)
  starting transfers between devices: 26.2 us -> 112 us
  waiting for transfers between devices: 144 us -> 64.2 us
  blocking collectives: 55.5 us -> 37.5 us
  local copies, waits for them, and re-layouts: 21.2 us -> 12.9 us
    ppermute x15, starting transfers between devices: 26.2 us -> 112 us  [exchange(): lax.ppermute(value, 'space', [(i, i ^ distance) for i in range(parts)])]
    ppermute x15, waiting for transfers between devices: 144 us -> 64.2 us  [exchange(): lax.ppermute(value, 'space', [(i, i ^ distance) for i in range(parts)])]
    all_to_all x1, blocking collectives: 55.5 us -> 37.5 us  [body(): lax.all_to_all(refined.reshape(parts, block, HALF), 'space', 0, 0, tiled=...]
    convert_element_type x2, local copies, waits for them, and re-layouts: 3.49 us -> 0.13 us  [body(): depth_weights.reshape(27, 1, channels).astype(F32)]
    reshape x1 -> x0, local copies, waits for them, and re-layouts: 3.31 us -> none  [exchange(): pieces.append(value.reshape(block, channels))]
    dynamic_slice x4 -> x2, local copies, waits for them, and re-layouts: 9.37 us -> 7.72 us  [exchange(): values[distance] = lax.dynamic_slice_in_dim(features, target, 1, 0)]
  transfers between devices with their start and end apart: 15 -> 15, of which waited for: 8 -> 6; matrix products, arithmetic and copies ran while one was open for 3% -> 3% of each run, Pallas kernels for 13% -> 14%
where the time goes in v2:
time: 287 us; the launch traced here: 286 us
  starting transfers between devices  112 us (39%)
  waiting for transfers between devices  64.2 us (22%)
  Pallas kernels  59.2 us (21%)
  blocking collectives  37.5 us (13%)
  local copies, waits for them, and re-layouts  12.9 us (4%)
    ppermute x15, starting transfers between devices, exchange(): lax.ppermute(value, 'space', [(i, i ^ distance) for i in range(parts)])  112 us
    ppermute x15, waiting for transfers between devices, exchange(): lax.ppermute(value, 'space', [(i, i ^ distance) for i in range(parts)])  64.2 us
    pallas_call x3, Pallas kernels, class_call(): pl.pallas_call(class_kernel, grid_spec=pltpu.PrefetchScalarGridSpec(num_s...  38.9 us
    all_to_all x1, blocking collectives, body(): lax.all_to_all(refined.reshape(parts, block, HALF), 'space', 0, 0, tiled=...  37.5 us
    pallas_call x1, Pallas kernels, last_call(): pl.pallas_call(last_kernel, grid_spec=pltpu.PrefetchScalarGridSpec(num_sc...  20.3 us
    dynamic_slice x2, local copies, waits for them, and re-layouts, exchange(): values[distance] = lax.dynamic_slice_in_dim(features, target, 1, 0)  7.72 us
  transfers between devices with their start and end apart: 15, of which 6 were waited for; matrix products, arithmetic and copies ran while one was open for 3% of the time, Pallas kernels for 14%

profile of v2, /device:TPU:0, one launch (start us, length us, event | category | flops | bytes accessed | tf_op | source)
XLA Modules:
  0.0 286.4 jit_solution(17133467428659065977)
XLA Ops:
  1.1 4.1 %collective-permute-start.9 = (bf16[1,144,2048]{2,1,0:T(8,128)(2,1)S(1)}, bf16[1,144,2048]{2,1,0:T(8,128)(2,1)S(1)}, u32[]{:S(2)}, u32[]{:S(2)}) collective-permute-start(bf16[1,144,2048]{2,1,0:T(8,128)(2,1)S(1)} %constant_dynamic-slice_fusion.14), channel_id=1, source_target_pairs={{0,8},{1,9},{2,10},{3,11},{4,12},{5,13},{6,14},{7,15},{8,0},{9,1},... | collective-permute-start | bytes 1769480 | tf_op jit(solution)/shard_map/ppermute | solution.py:286
  5.2 6.6 %constant_dynamic-slice_fusion = (bf16[1,144,2048]{2,1,0:T(8,128)(2,1)}, bf16[1,144,2048]{2,1,0:T(8,128)(2,1)}, bf16[144,2048]{1,0:T(8,128)(2,1)S(1)}, bf16[1,14...) fusion(bf16[16,144,2048]{2,1,0:T(8,128)(2,1)} %param.8, ...), kind=kLoop, calls=%fused_computation.1 | loop fusion | bytes 17694780 | tf_op jit(solution)/shard_map/dynamic_slice | solution.py:266
  13.5 3.7 %collective-permute-start.8 = (bf16[1,144,2048]{2,1,0:T(8,128)(2,1)}, bf16[1,144,2048]{2,1,0:T(8,128)(2,1)}, u32[]{:S(2)}, u32[]{:S(2)}) collective-permute-start(bf16[1,144,2048]{2,1,0:T(8,128)(2,1)} %get-tuple-element.44), channel_id=1, source_target_pairs={{0,9},{1,8},{2,11},{3,10},{4,13},{5,12},{6,15},{7,14},{8,1},{9,0},... | collective-permute-start | bytes 1769480 | tf_op jit(solution)/shard_map/ppermute | solution.py:286
  17.2 28.4 %collective-permute-done.9 = bf16[1,144,2048]{2,1,0:T(8,128)(2,1)S(1)} collective-permute-done((bf16[1,144,2048]{2,1,0:T(8,128)(2,1)S(1)}, bf16[1,144,2048]{2,1,0:T(8,128)(2,1)S(1)}, u32[]{:S(2)}, u32[]{:S(2)}) %collective-permute-start.9) | collective-permute-done | bytes 589856 | tf_op jit(solution)/shard_map/ppermute | solution.py:286
  45.5 4.1 %collective-permute-start.11 = (bf16[1,144,2048]{2,1,0:T(8,128)(2,1)}, bf16[1,144,2048]{2,1,0:T(8,128)(2,1)}, u32[]{:S(2)}, u32[]{:S(2)}) collective-permute-start(bf16[1,144,2048]{2,1,0:T(8,128)(2,1)} %get-tuple-element.33), channel_id=1, source_target_pairs={{0,13},{1,12},{2,15},{3,14},{4,9},{5,8},{6,11},{7,10},{8,5},{9,4},... | collective-permute-start | bytes 1769480 | tf_op jit(solution)/shard_map/ppermute | solution.py:286
  49.6 34.9 %collective-permute-start.5 = (bf16[1,144,2048]{2,1,0:T(8,128)(2,1)}, bf16[1,144,2048]{2,1,0:T(8,128)(2,1)S(1)}, u32[]{:S(2)}, u32[]{:S(2)}) collective-permute-start(bf16[1,144,2048]{2,1,0:T(8,128)(2,1)} %get-tuple-element.27), channel_id=1, source_target_pairs={{0,5},{1,4},{2,7},{3,6},{4,1},{5,0},{6,3},{7,2},{8,13},{9,12},{10,... | collective-permute-start | bytes 1769480 | tf_op jit(solution)/shard_map/ppermute | solution.py:286
  84.9 1.4 broadcast_in_dim.4.taps
  86.3 13.0 %pyramid_class.3 = (f32[576,256]{1,0:T(8,128)S(1)}, f32[8,2048]{1,0:T(8,128)S(1)}) custom-call(s32[2]{0:T(128)S(1)} %pad_add_fusion.info, bf16[144,2048]{1,0:T(8,128)(2,1)S(1)} %get-tuple-element.43.x0, bf16[144,2048]{1,0:T(8,128)(2,1)S(1)} %bitcast.22, bf16[144,2048]{1,0:T(8,128)(2,1)} %bitcast.28, bf16[144,2048]{1,0:T(8,128)(2,1)} %bitcast.29, ...), custom_call_target="tpu_custom_call" | custom-call | tf_op jit(solution)/shard_map/pyramid_class/pallas_call | solution.py:203
  100.2 3.1 %collective-permute-start.10 = (bf16[1,144,2048]{2,1,0:T(8,128)(2,1)S(1)}, bf16[1,144,2048]{2,1,0:T(8,128)(2,1)S(1)}, u32[]{:S(2)}, u32[]{:S(2)}) collective-permute-start(bf16[1,144,2048]{2,1,0:T(8,128)(2,1)S(1)} %copy-done.12), channel_id=1, source_target_pairs={{0,11},{1,10},{2,9},{3,8},{4,15},{5,14},{6,13},{7,12},{8,3},{9,2},... | collective-permute-start | bytes 1769480 | tf_op jit(solution)/shard_map/ppermute | solution.py:286
  103.4 2.2 collective-permute-start.13
  105.6 2.5 collective-permute-done.5
  108.1 33.2 %collective-permute-start.6 = (bf16[1,144,2048]{2,1,0:T(8,128)(2,1)S(1)}, bf16[1,144,2048]{2,1,0:T(8,128)(2,1)S(1)}, u32[]{:S(2)}, u32[]{:S(2)}) collective-permute-start(bf16[1,144,2048]{2,1,0:T(8,128)(2,1)S(1)} %copy-done.10), channel_id=1, source_target_pairs={{0,7},{1,6},{2,5},{3,4},{4,3},{5,2},{6,1},{7,0},{8,15},{9,14},{10,... | collective-permute-start | bytes 1769480 | tf_op jit(solution)/shard_map/ppermute | solution.py:286
  141.3 2.4 collective-permute-start.2
  143.8 13.0 %pyramid_class.4 = (f32[576,256]{1,0:T(8,128)S(1)}, f32[8,2048]{1,0:T(8,128)S(1)}) custom-call(s32[2]{0:T(128)S(1)} %pad_add_fusion.info, bf16[144,2048]{1,0:T(8,128)(2,1)S(1)} %bitcast.21, bf16[144,2048]{1,0:T(8,128)(2,1)S(1)} %bitcast.20, bf16[144,2048]{1,0:T(8,128)(2,1)} %bitcast.10.x2, bf16[144,2048]{1,0:T(8,128)(2,1)} %bitcast.11.x3, ...), custom_call_target="tpu_custom_call" | custom-call | tf_op jit(solution)/shard_map/pyramid_class/pallas_call | solution.py:203
  157.7 1.5 collective-permute-start.14
  159.2 3.4 %collective-permute-done.6 = bf16[1,144,2048]{2,1,0:T(8,128)(2,1)S(1)} collective-permute-done((bf16[1,144,2048]{2,1,0:T(8,128)(2,1)S(1)}, bf16[1,144,2048]{2,1,0:T(8,128)(2,1)S(1)}, u32[]{:S(2)}, u32[]{:S(2)}) %collective-permute-start.6) | collective-permute-done | bytes 589856 | tf_op jit(solution)/shard_map/ppermute | solution.py:286
  162.6 18.8 %collective-permute-start.7 = (bf16[1,144,2048]{2,1,0:T(8,128)(2,1)S(1)}, bf16[1,144,2048]{2,1,0:T(8,128)(2,1)S(1)}, u32[]{:S(2)}, u32[]{:S(2)}) collective-permute-start(bf16[1,144,2048]{2,1,0:T(8,128)(2,1)S(1)} %copy-done.6), channel_id=1, source_target_pairs={{0,6},{1,7},{2,4},{3,5},{4,2},{5,3},{6,0},{7,1},{8,14},{9,15},{10,... | collective-permute-start | bytes 1769480 | tf_op jit(solution)/shard_map/ppermute | solution.py:286
  181.4 2.6 collective-permute-start.3
  184.0 12.9 %pyramid_class.5 = (f32[576,256]{1,0:T(8,128)S(1)}, f32[8,2048]{1,0:T(8,128)S(1)}) custom-call(s32[2]{0:T(128)S(1)} %pad_add_fusion.info, bf16[144,2048]{1,0:T(8,128)(2,1)S(1)} %bitcast.24, bf16[144,2048]{1,0:T(8,128)(2,1)S(1)} %bitcast.23, bf16[144,2048]{1,0:T(8,128)(2,1)} %bitcast.30, bf16[144,2048]{1,0:T(8,128)(2,1)} %bitcast.31, ...), custom_call_target="tpu_custom_call" | custom-call | tf_op jit(solution)/shard_map/pyramid_class/pallas_call | solution.py:203
  197.8 9.5 %collective-permute-done.12 = bf16[1,144,2048]{2,1,0:T(8,128)(2,1)S(1)} collective-permute-done((bf16[1,144,2048]{2,1,0:T(8,128)(2,1)S(1)}, bf16[1,144,2048]{2,1,0:T(8,128)(2,1)S(1)}, u32[]{:S(2)}, u32[]{:S(2)}) %collective-permute-start.12) | collective-permute-done | bytes 589856 | tf_op jit(solution)/shard_map/ppermute | solution.py:286
  207.2 7.9 %collective-permute-done.7 = bf16[1,144,2048]{2,1,0:T(8,128)(2,1)S(1)} collective-permute-done((bf16[1,144,2048]{2,1,0:T(8,128)(2,1)S(1)}, bf16[1,144,2048]{2,1,0:T(8,128)(2,1)S(1)}, u32[]{:S(2)}, u32[]{:S(2)}) %collective-permute-start.7) | collective-permute-done | bytes 589856 | tf_op jit(solution)/shard_map/ppermute | solution.py:286
  215.1 12.5 %collective-permute-done.3 = bf16[1,144,2048]{2,1,0:T(8,128)(2,1)S(1)} collective-permute-done((bf16[1,144,2048]{2,1,0:T(8,128)(2,1)S(1)}, bf16[1,144,2048]{2,1,0:T(8,128)(2,1)S(1)}, u32[]{:S(2)}, u32[]{:S(2)}) %collective-permute-start.3) | collective-permute-done | bytes 589856 | tf_op jit(solution)/shard_map/ppermute | solution.py:286
  227.7 20.3 %pyramid_last.1 = bf16[2304,256]{1,0:T(8,128)(2,1)} custom-call(s32[2]{0:T(128)S(1)} %pad_add_fusion.info, bf16[144,2048]{1,0:T(8,128)(2,1)S(1)} %bitcast.26, bf16[144,2048]{1,0:T(8,128)(2,1)S(1)} %bitcast.25, bf16[144,2048]{1,0:T(8,128)(2,1)} %bitcast.32, bf16[144,2048]{1,0:T(8,128)(2,1)} %bitcast.33, f32[27,8,2048]{2,1,0:T(8,128)} %broadcast_in_dim.4.taps, ...), custom_call_target="tpu_custom_call" | custom-call | tf_op jit(solution)/shard_map/pyramid_last/pallas_call | solution.py:231
  247.9 37.5 %all_to_all.5 = bf16[16,144,256]{2,1,0:T(8,128)(2,1)S(1)} all-to-all(bf16[16,144,256]{2,1,0:T(8,128)(2,1)} %bitcast.27), channel_id=1, replica_groups=mesh['dp'=2,'space'=16] {'space'}, dimensions={0} | all-to-all | bytes 2359296 | tf_op jit(solution)/shard_map/all_to_all | solution.py:333
  (59 shorter events, 6.9 us)
Async XLA Ops:
  1.1 44.4 %collective-permute-start.9 = (bf16[1,144,2048]{2,1,0:T(8,128)(2,1)S(1)}, bf16[1,144,2048]{2,1,0:T(8,128)(2,1)S(1)}, u32[]{:S(2)}, u32[]{:S(2)}) collective-permute-start(bf16[1,144,2048]{2,1,0:T(8,128)(2,1)S(1)} %constant_dynamic-slice_fusion.14), channel_id=1, source_target_pairs={{0,8},{1,9},{2,10},{3,11},{4,12},{5,13},{6,14},{7,15},{8,0},{9,1},... | collective-permute-start | bytes 1769480 | tf_op jit(solution)/shard_map/ppermute | solution.py:286
  5.2 79.4 %copy-start.18 = (bf16[3,9,2048]{2,0,1:T(4,128)(2,1)S(1)}, bf16[3,9,2048]{2,0,1:T(4,128)(2,1)}, u32[]{:S(2)}) copy-start(bf16[3,9,2048]{2,0,1:T(4,128)(2,1)} %param.9) | copy-start | bytes 331780
  11.8 37.8 %collective-permute-start.4 = (bf16[1,144,2048]{2,1,0:T(8,128)(2,1)S(1)}, bf16[1,144,2048]{2,1,0:T(8,128)(2,1)S(1)}, u32[]{:S(2)}, u32[]{:S(2)}) collective-permute-start(bf16[1,144,2048]{2,1,0:T(8,128)(2,1)S(1)} %get-tuple-element.47), channel_id=1, source_target_pairs={{0,12},{1,13},{2,14},{3,15},{4,8},{5,9},{6,10},{7,11},{8,4},{9,5},... | collective-permute-start | bytes 1769480 | tf_op jit(solution)/shard_map/ppermute | solution.py:286
  13.2 71.3 %collective-permute-start = (bf16[1,144,2048]{2,1,0:T(8,128)(2,1)S(1)}, bf16[1,144,2048]{2,1,0:T(8,128)(2,1)S(1)}, u32[]{:S(2)}, u32[]{:S(2)}) collective-permute-start(bf16[1,144,2048]{2,1,0:T(8,128)(2,1)S(1)} %get-tuple-element.51), channel_id=1, source_target_pairs={{0,4},{1,5},{2,6},{3,7},{4,0},{5,1},{6,2},{7,3},{8,12},{9,13},{10,... | collective-permute-start | bytes 1769480 | tf_op jit(solution)/shard_map/ppermute | solution.py:286
  13.5 86.7 %collective-permute-start.8 = (bf16[1,144,2048]{2,1,0:T(8,128)(2,1)}, bf16[1,144,2048]{2,1,0:T(8,128)(2,1)}, u32[]{:S(2)}, u32[]{:S(2)}) collective-permute-start(bf16[1,144,2048]{2,1,0:T(8,128)(2,1)} %get-tuple-element.44), channel_id=1, source_target_pairs={{0,9},{1,8},{2,11},{3,10},{4,13},{5,12},{6,15},{7,14},{8,1},{9,0},... | collective-permute-start | bytes 1769480 | tf_op jit(solution)/shard_map/ppermute | solution.py:286
  45.5 57.8 %collective-permute-start.11 = (bf16[1,144,2048]{2,1,0:T(8,128)(2,1)}, bf16[1,144,2048]{2,1,0:T(8,128)(2,1)}, u32[]{:S(2)}, u32[]{:S(2)}) collective-permute-start(bf16[1,144,2048]{2,1,0:T(8,128)(2,1)} %get-tuple-element.33), channel_id=1, source_target_pairs={{0,13},{1,12},{2,15},{3,14},{4,9},{5,8},{6,11},{7,10},{8,5},{9,4},... | collective-permute-start | bytes 1769480 | tf_op jit(solution)/shard_map/ppermute | solution.py:286
  49.6 34.9 %copy-start.13 = (bf16[1,144,2048]{2,1,0:T(8,128)(2,1)}, bf16[1,144,2048]{2,1,0:T(8,128)(2,1)S(1)}, u32[]{:S(2)}) copy-start(bf16[1,144,2048]{2,1,0:T(8,128)(2,1)S(1)} %collective-permute-done.4) | copy-start | bytes 1769476
  49.6 58.6 %collective-permute-start.5 = (bf16[1,144,2048]{2,1,0:T(8,128)(2,1)}, bf16[1,144,2048]{2,1,0:T(8,128)(2,1)S(1)}, u32[]{:S(2)}, u32[]{:S(2)}) collective-permute-start(bf16[1,144,2048]{2,1,0:T(8,128)(2,1)} %get-tuple-element.27), channel_id=1, source_target_pairs={{0,5},{1,4},{2,7},{3,6},{4,1},{5,0},{6,3},{7,2},{8,13},{9,12},{10,... | collective-permute-start | bytes 1769480 | tf_op jit(solution)/shard_map/ppermute | solution.py:286
  84.5 56.9 %collective-permute-start.1 = (bf16[1,144,2048]{2,1,0:T(8,128)(2,1)}, bf16[1,144,2048]{2,1,0:T(8,128)(2,1)S(1)}, u32[]{:S(2)}, u32[]{:S(2)}) collective-permute-start(bf16[1,144,2048]{2,1,0:T(8,128)(2,1)} %get-tuple-element.24), channel_id=1, source_target_pairs={{0,1},{1,0},{2,3},{3,2},{4,5},{5,4},{6,7},{7,6},{8,9},{9,8},{10,11... | collective-permute-start | bytes 1769480 | tf_op jit(solution)/shard_map/ppermute | solution.py:286
  86.3 21.8 %copy-start.10 = (bf16[1,144,2048]{2,1,0:T(8,128)(2,1)S(1)}, bf16[1,144,2048]{2,1,0:T(8,128)(2,1)}, u32[]{:S(2)}) copy-start(bf16[1,144,2048]{2,1,0:T(8,128)(2,1)} %get-tuple-element.28) | copy-start | bytes 1769476
  86.3 55.0 %copy-start.9 = (bf16[1,144,2048]{2,1,0:T(8,128)(2,1)S(1)}, bf16[1,144,2048]{2,1,0:T(8,128)(2,1)}, u32[]{:S(2)}) copy-start(bf16[1,144,2048]{2,1,0:T(8,128)(2,1)} %get-tuple-element.25) | copy-start | bytes 1769476
  100.2 57.4 %collective-permute-start.10 = (bf16[1,144,2048]{2,1,0:T(8,128)(2,1)S(1)}, bf16[1,144,2048]{2,1,0:T(8,128)(2,1)S(1)}, u32[]{:S(2)}, u32[]{:S(2)}) collective-permute-start(bf16[1,144,2048]{2,1,0:T(8,128)(2,1)S(1)} %copy-done.12), channel_id=1, source_target_pairs={{0,11},{1,10},{2,9},{3,8},{4,15},{5,14},{6,13},{7,12},{8,3},{9,2},... | collective-permute-start | bytes 1769480 | tf_op jit(solution)/shard_map/ppermute | solution.py:286
  103.4 54.3 %collective-permute-start.13 = (bf16[1,144,2048]{2,1,0:T(8,128)(2,1)S(1)}, bf16[1,144,2048]{2,1,0:T(8,128)(2,1)S(1)}, u32[]{:S(2)}, u32[]{:S(2)}) collective-permute-start(bf16[1,144,2048]{2,1,0:T(8,128)(2,1)S(1)} %copy-done.11), channel_id=1, source_target_pairs={{0,15},{1,14},{2,13},{3,12},{4,11},{5,10},{6,9},{7,8},{8,7},{9,6},... | collective-permute-start | bytes 1769480 | tf_op jit(solution)/shard_map/ppermute | solution.py:286
  108.1 54.5 %collective-permute-start.6 = (bf16[1,144,2048]{2,1,0:T(8,128)(2,1)S(1)}, bf16[1,144,2048]{2,1,0:T(8,128)(2,1)S(1)}, u32[]{:S(2)}, u32[]{:S(2)}) collective-permute-start(bf16[1,144,2048]{2,1,0:T(8,128)(2,1)S(1)} %copy-done.10), channel_id=1, source_target_pairs={{0,7},{1,6},{2,5},{3,4},{4,3},{5,2},{6,1},{7,0},{8,15},{9,14},{10,... | collective-permute-start | bytes 1769480 | tf_op jit(solution)/shard_map/ppermute | solution.py:286
  141.3 40.1 %collective-permute-start.2 = (bf16[1,144,2048]{2,1,0:T(8,128)(2,1)S(1)}, bf16[1,144,2048]{2,1,0:T(8,128)(2,1)S(1)}, u32[]{:S(2)}, u32[]{:S(2)}) collective-permute-start(bf16[1,144,2048]{2,1,0:T(8,128)(2,1)S(1)} %copy-done.9), channel_id=1, source_target_pairs={{0,3},{1,2},{2,1},{3,0},{4,7},{5,6},{6,5},{7,4},{8,11},{9,10},{10,... | collective-permute-start | bytes 1769480 | tf_op jit(solution)/shard_map/ppermute | solution.py:286
  143.8 37.6 %copy-start.5 = (bf16[1,144,2048]{2,1,0:T(8,128)(2,1)S(1)}, bf16[1,144,2048]{2,1,0:T(8,128)(2,1)}, u32[]{:S(2)}) copy-start(bf16[1,144,2048]{2,1,0:T(8,128)(2,1)} %get-tuple-element.26) | copy-start | bytes 1769476
  157.6 26.4 %copy-start.14 = (bf16[1,144,2048]{2,1,0:T(8,128)(2,1)}, bf16[1,144,2048]{2,1,0:T(8,128)(2,1)S(1)}, u32[]{:S(2)}) copy-start(bf16[1,144,2048]{2,1,0:T(8,128)(2,1)S(1)} %collective-permute-done.10) | copy-start | bytes 1769476
  157.6 49.6 %collective-permute-start.12 = (bf16[1,144,2048]{2,1,0:T(8,128)(2,1)S(1)}, bf16[1,144,2048]{2,1,0:T(8,128)(2,1)S(1)}, u32[]{:S(2)}, u32[]{:S(2)}) collective-permute-start(bf16[1,144,2048]{2,1,0:T(8,128)(2,1)S(1)} %copy-done.8), channel_id=1, source_target_pairs={{0,10},{1,11},{2,8},{3,9},{4,14},{5,15},{6,12},{7,13},{8,2},{9,3},... | collective-permute-start | bytes 1769480 | tf_op jit(solution)/shard_map/ppermute | solution.py:286
  157.7 26.3 %copy-start.15 = (bf16[1,144,2048]{2,1,0:T(8,128)(2,1)}, bf16[1,144,2048]{2,1,0:T(8,128)(2,1)S(1)}, u32[]{:S(2)}) copy-start(bf16[1,144,2048]{2,1,0:T(8,128)(2,1)S(1)} %collective-permute-done.13) | copy-start | bytes 1769476
  157.7 49.5 %collective-permute-start.14 = (bf16[1,144,2048]{2,1,0:T(8,128)(2,1)S(1)}, bf16[1,144,2048]{2,1,0:T(8,128)(2,1)S(1)}, u32[]{:S(2)}, u32[]{:S(2)}) collective-permute-start(bf16[1,144,2048]{2,1,0:T(8,128)(2,1)S(1)} %copy-done.7), channel_id=1, source_target_pairs={{0,14},{1,15},{2,12},{3,13},{4,10},{5,11},{6,8},{7,9},{8,6},{9,7},... | collective-permute-start | bytes 1769480 | tf_op jit(solution)/shard_map/ppermute | solution.py:286
  162.6 52.5 %collective-permute-start.7 = (bf16[1,144,2048]{2,1,0:T(8,128)(2,1)S(1)}, bf16[1,144,2048]{2,1,0:T(8,128)(2,1)S(1)}, u32[]{:S(2)}, u32[]{:S(2)}) collective-permute-start(bf16[1,144,2048]{2,1,0:T(8,128)(2,1)S(1)} %copy-done.6), channel_id=1, source_target_pairs={{0,6},{1,7},{2,4},{3,5},{4,2},{5,3},{6,0},{7,1},{8,14},{9,15},{10,... | collective-permute-start | bytes 1769480 | tf_op jit(solution)/shard_map/ppermute | solution.py:286
  181.4 46.2 %collective-permute-start.3 = (bf16[1,144,2048]{2,1,0:T(8,128)(2,1)S(1)}, bf16[1,144,2048]{2,1,0:T(8,128)(2,1)S(1)}, u32[]{:S(2)}, u32[]{:S(2)}) collective-permute-start(bf16[1,144,2048]{2,1,0:T(8,128)(2,1)S(1)} %copy-done.5), channel_id=1, source_target_pairs={{0,2},{1,3},{2,0},{3,1},{4,6},{5,7},{6,4},{7,5},{8,10},{9,11},{10,... | collective-permute-start | bytes 1769480 | tf_op jit(solution)/shard_map/ppermute | solution.py:286
  184.0 43.6 %copy-start.19 = (bf16[9,256]{1,0:T(8,128)(2,1)S(1)}, bf16[9,256]{1,0:T(8,128)(2,1)}, u32[]{:S(2)}) copy-start(bf16[9,256]{1,0:T(8,128)(2,1)} %param.14) | copy-start | bytes 13828
  184.0 43.7 %copy-start.3 = (bf16[256,256]{1,0:T(8,128)(2,1)S(1)}, bf16[256,256]{1,0:T(8,128)(2,1)}, u32[]{:S(2)}) copy-start(bf16[256,256]{1,0:T(8,128)(2,1)} %refine_point.1) | copy-start | bytes 393220
  (11 other events, 125.1 us)

commit v3 on v1

v3 whole, which is shorter than its diff:
```python
import jax
import jax.numpy as jnp
from jax import lax
from jax.experimental import pallas as pl
from jax.experimental.pallas import tpu as pltpu
from jax.sharding import PartitionSpec as P

ROWS = 48
COLS = 48
RATE = 12
BANDS = ROWS // RATE
CLASSES = 4
CLASS_ROWS = RATE // CLASSES
BLOCK = CLASS_ROWS * COLS
TILE = 512
HALF = 256
LATE = 512
ORDER = (0, 1, 3, 2)
NEAR = (1, 0)
FAR = (2, 3)
F32 = jnp.float32
BF16 = jnp.bfloat16


def load_tile(info, x_refs, depth, plain, shifted, raw, taps):
    width = plain.shape[-1]
    for index in range(3):
        taps[index] = depth[index].astype(F32)

    @pl.when(pl.program_id(0) == 0)
    def _():
        shifted[:, :, 0:8, :] = jnp.zeros((BANDS, CLASS_ROWS, 8, width), F32)
        shifted[:, :, 48:56, :] = jnp.zeros((BANDS, CLASS_ROWS, 8, width), F32)

    for hop in range(BANDS):
        band = jnp.bitwise_xor(info[0], hop)
        block = x_refs[hop][...]
        raw[band] = block
        wide = block.astype(F32).reshape(CLASS_ROWS, COLS, width)
        plain[band] = wide
        shifted[band, :, 4:52, :] = wide


def spread_rows(plain, shifted, taps, spread, row, lane):
    lanes = pl.ds(lane, HALF)
    for branch in range(3):
        weights = [
            jnp.broadcast_to(taps[branch, tap:tap + 1, lanes], (8, HALF)) for tap in range(9)
        ]
        for band in range(BANDS):
            tiles = []
            for tile in range(COLS // 8):
                total = None
                for up in (-1, 0, 1):
                    source = band + up * (branch + 1)
                    if not 0 <= source < BANDS:
                        continue
                    for side in (-1, 0, 1):
                        shift = side * RATE * (branch + 1)
                        if 8 * tile + shift + 7 < 0 or 8 * tile + shift >= COLS:
                            continue
                        if shift % 8 == 0:
                            value = plain[source, row, 8 * tile + shift:8 * tile + shift + 8, lanes]
                        else:
                            start = 8 * tile + shift + 4
                            value = shifted[source, row, start:start + 8, lanes]
                        term = value * weights[3 * (up + 1) + (side + 1)]
                        total = term if total is None else total + term
                tiles.append(jnp.maximum(total, 0.0))
            sums = jnp.concatenate(tiles, axis=0).astype(BF16)
            spread[branch, band, pl.ds(pl.multiple_of(row * COLS, COLS), COLS), lanes] = sums


def pyramid_tile(info, x_refs, depth, point, branch, plain, shifted, raw, spread, taps):
    width = plain.shape[-1]
    load_tile(info, x_refs, depth, plain, shifted, raw, taps)

    def step(index, carry):
        spread_rows(plain, shifted, taps, spread, index // (width // HALF),
                    pl.multiple_of((index % (width // HALF)) * HALF, HALF))
        return carry

    lax.fori_loop(0, CLASS_ROWS * (width // HALF), step, 0)
    cells = BANDS * BLOCK
    parts = [jnp.dot(raw[...].reshape(cells, width), branch[...], preferred_element_type=F32)]
    for index in range(3):
        parts.append(
            jnp.dot(spread[index].reshape(cells, width), point[index], preferred_element_type=F32)
        )
    return parts


def accumulate(sums, parts):
    @pl.when(pl.program_id(0) == 0)
    def _():
        for index in range(4):
            sums[index] = parts[index]

    @pl.when(pl.program_id(0) > 0)
    def _():
        for index in range(4):
            sums[index] += parts[index]


def channel_sum(plain):
    width = plain.shape[-1]
    return jnp.sum(plain[...].reshape(BANDS * BLOCK // 8, 8, width), axis=0)


def pool_term(channels, pooling):
    total = channels[0]
    for item in channels[1:]:
        total = total + item
    mean = jnp.sum(total, axis=0, keepdims=True) * (1.0 / (ROWS * COLS))
    mean = jnp.broadcast_to(mean, (16, mean.shape[1])).astype(BF16)
    return jnp.dot(mean, pooling[...], preferred_element_type=F32)


def project(sums, weight):
    total = None
    for index in range(4):
        joined = jnp.maximum(sums[index], 0.0).astype(BF16)
        term = jnp.dot(
            joined, weight[HALF * index:HALF * (index + 1), :], preferred_element_type=F32
        )
        total = term if total is None else total + term
    return total


def class_kernel(info, x0, x1, x2, x3, depth, point, branch, weight, out, channel, plain, shifted,
                 raw, spread, taps, sums):
    accumulate(sums, pyramid_tile(info, (x0, x1, x2, x3), depth, point, branch, plain, shifted,
                                  raw, spread, taps))
    channel[...] = channel_sum(plain)

    @pl.when(pl.program_id(0) == pl.num_programs(0) - 1)
    def _():
        out[...] = project(sums, weight)


def early_kernel(info, x0, x1, x2, x3, depth, point, branch, pooling, channel0, channel1, channel2,
                 sums, pool, plain, shifted, raw, spread, taps):
    accumulate(sums, pyramid_tile(info, (x0, x1, x2, x3), depth, point, branch, plain, shifted,
                                  raw, spread, taps))
    term = pool_term([channel0[...], channel1[...], channel2[...], channel_sum(plain)], pooling)

    @pl.when(pl.program_id(0) == 0)
    def _():
        pool[...] = term

    @pl.when(pl.program_id(0) > 0)
    def _():
        pool[...] += term


def last_kernel(info, x0, x1, x2, x3, depth, point, branch, weight, pooling, channel0, channel1,
                channel2, sums, pool, pre0, pre1, pre2, refine_depth, refine_point, out, plain,
                shifted, raw, spread, taps, context, rows):
    parts = pyramid_tile(info, (x0, x1, x2, x3), depth, point, branch, plain, shifted, raw, spread,
                         taps)
    parts = [sums[index] + parts[index] for index in range(4)]
    term = pool_term([channel0[...], channel1[...], channel2[...], channel_sum(plain)], pooling)
    vector = jnp.maximum(pool[...] + term, 0.0).astype(BF16)
    bias = jnp.dot(vector, weight[4 * HALF:5 * HALF, :], preferred_element_type=F32)[0:1, :]
    context[0] = jnp.zeros((COLS, HALF), F32)
    context[ROWS + 1] = jnp.zeros((COLS, HALF), F32)
    pres = (pre0[...], pre1[...], pre2[...], project(parts, weight))
    for index, pre in enumerate(pres):
        first = CLASS_ROWS * jnp.bitwise_xor(info[1], ORDER[index])
        value = jnp.maximum(pre + bias, 0.0).astype(BF16).astype(F32)
        value = value.reshape(BANDS, CLASS_ROWS, COLS, HALF)
        for band in range(BANDS):
            for row in range(CLASS_ROWS):
                context[RATE * band + first + row + 1] = value[band, row]
    column = lax.broadcasted_iota(jnp.int32, (COLS, HALF), 0)
    wide = refine_depth[...].astype(F32)

    def step(row, carry):
        lines = [context[row + up] for up in range(3)]
        sides = []
        for side in range(3):
            total = None
            for up in range(3):
                term = lines[up] * wide[3 * up + side:3 * up + side + 1, :]
                total = term if total is None else total + term
            sides.append(total)
        left = jnp.where(column == 0, 0.0, pltpu.roll(sides[0], 1, 0))
        right = jnp.where(column == COLS - 1, 0.0, pltpu.roll(sides[2], COLS - 1, 0))
        total = jnp.maximum(sides[1] + left + right, 0.0).astype(BF16)
        rows[pl.ds(pl.multiple_of(row * COLS, COLS), COLS), :] = total
        return carry

    lax.fori_loop(0, ROWS, step, 0)
    product = jnp.dot(rows[...], refine_point[...], preferred_element_type=F32)
    out[...] = jnp.maximum(product, 0.0).astype(BF16)


def whole(shape):
    return pl.BlockSpec(shape, lambda i, info: (0,) * len(shape))


def pyramid_specs(blocks, start, channels):
    offset = start // TILE
    full = max(item.shape[1] for item in blocks)
    specs = []
    for item in blocks:
        first = offset if item.shape[1] == full else 0
        specs.append(pl.BlockSpec((BLOCK, TILE), lambda i, info, first=first: (0, first + i)))
    specs.append(pl.BlockSpec((3, 9, TILE), lambda i, info: (0, 0, offset + i)))
    specs.append(pl.BlockSpec((3, TILE, HALF), lambda i, info: (0, offset + i, 0)))
    specs.append(pl.BlockSpec((TILE, HALF), lambda i, info: (offset + i, 0)))
    return specs


def channel_specs(start):
    offset = start // TILE
    specs = [pl.BlockSpec((TILE, HALF), lambda i, info: (offset + i, 0))]
    return specs + [pl.BlockSpec((8, TILE), lambda i, info: (0, offset + i)) for _ in range(3)]


def pyramid_scratch():
    return [
        pltpu.VMEM((BANDS, CLASS_ROWS, COLS, TILE), F32),
        pltpu.VMEM((BANDS, CLASS_ROWS, COLS + 8, TILE), F32),
        pltpu.VMEM((BANDS, BLOCK, TILE), BF16),
        pltpu.VMEM((3, BANDS, BLOCK, TILE), BF16),
        pltpu.VMEM((3, 9, TILE), F32),
    ]


PARAMS = pltpu.CompilerParams(
    dimension_semantics=("arbitrary",), vmem_limit_bytes=52 * 1024 * 1024
)


def class_call(info, blocks, depth, point, branch, weight):
    channels = depth.shape[2]
    return pl.pallas_call(
        class_kernel,
        grid_spec=pltpu.PrefetchScalarGridSpec(
            num_scalar_prefetch=1,
            grid=(channels // TILE,),
            in_specs=pyramid_specs(blocks, 0, channels) + [whole((5 * HALF, HALF))],
            out_specs=[
                whole((BANDS * BLOCK, HALF)),
                pl.BlockSpec((8, TILE), lambda i, info: (0, i)),
            ],
            scratch_shapes=pyramid_scratch() + [pltpu.VMEM((4, BANDS * BLOCK, HALF), F32)],
        ),
        out_shape=[
            jax.ShapeDtypeStruct((BANDS * BLOCK, HALF), F32),
            jax.ShapeDtypeStruct((8, channels), F32),
        ],
        compiler_params=PARAMS,
        name="pyramid_class",
    )(info, *blocks, depth, point, branch, weight)


def early_call(info, blocks, depth, point, branch, pooling, channel):
    channels = depth.shape[2] - LATE
    return pl.pallas_call(
        early_kernel,
        grid_spec=pltpu.PrefetchScalarGridSpec(
            num_scalar_prefetch=1,
            grid=(channels // TILE,),
            in_specs=pyramid_specs(blocks, 0, channels) + channel_specs(0),
            out_specs=[whole((4, BANDS * BLOCK, HALF)), whole((16, HALF))],
            scratch_shapes=pyramid_scratch(),
        ),
        out_shape=[
            jax.ShapeDtypeStruct((4, BANDS * BLOCK, HALF), F32),
            jax.ShapeDtypeStruct((16, HALF), F32),
        ],
        compiler_params=PARAMS,
        name="pyramid_early",
    )(info, *blocks, depth, point, branch, pooling, *channel)


def last_call(info, blocks, depth, point, branch, weight, pooling, channel, sums, pool, pres,
              refine_depth, refine_point):
    start = depth.shape[2] - LATE
    specs = pyramid_specs(blocks, start, LATE) + [whole((5 * HALF, HALF))] + channel_specs(start)
    specs += [whole((4, BANDS * BLOCK, HALF)), whole((16, HALF))]
    specs += [whole((BANDS * BLOCK, HALF)) for _ in range(3)]
    specs += [whole((9, HALF)), whole((HALF, HALF))]
    return pl.pallas_call(
        last_kernel,
        grid_spec=pltpu.PrefetchScalarGridSpec(
            num_scalar_prefetch=1,
            grid=(1,),
            in_specs=specs,
            out_specs=whole((ROWS * COLS, HALF)),
            scratch_shapes=pyramid_scratch() + [
                pltpu.VMEM((ROWS + 2, COLS, HALF), F32),
                pltpu.VMEM((ROWS * COLS, HALF), BF16),
            ],
        ),
        out_shape=jax.ShapeDtypeStruct((ROWS * COLS, HALF), BF16),
        compiler_params=PARAMS,
        name="pyramid_last",
    )(info, *blocks, depth, point, branch, weight, pooling, *channel, sums, pool, *pres,
      refine_depth, refine_point)


class Sender:
    def __init__(self, features):
        self.features = features
        self.parts = lax.axis_size("space")
        self.sub = BLOCK // features.shape[1]
        self.me = lax.axis_index("space").astype(jnp.int32)
        self.values = {}
        self.far = []
        self.near = []

    def cut(self, origin, hop, kind, start, size):
        for piece in range(self.sub):
            distance = (hop * CLASSES + kind) * self.sub + piece
            target = jnp.bitwise_xor(origin, distance)
            self.values[distance, start] = lax.dynamic_slice(
                self.features, (target, 0, start), (1, self.features.shape[1], size)
            )

    def send(self, hop, kind, start, after):
        chain = self.far if hop in FAR else self.near
        got = []
        for piece in range(self.sub):
            distance = (hop * CLASSES + kind) * self.sub + piece
            value = self.values[distance, start]
            if distance:
                before = [chain[-2][piece]] if len(chain) >= 2 else []
                before += after
                if before:
                    value, _ = lax.optimization_barrier((value, before))
                value = lax.ppermute(
                    value, "space", [(i, i ^ distance) for i in range(self.parts)]
                )
            got.append(value)
        if hop or kind:
            chain.append(got)
        block, size = got[0].shape[1:]
        if self.sub == 1:
            return got[0].reshape(block, size)
        joined = jnp.zeros((BLOCK, size), value.dtype)
        for piece in range(self.sub):
            row = jnp.bitwise_xor(self.me % self.sub, piece) * block
            joined = lax.dynamic_update_slice(joined, got[piece].reshape(block, size), (row, 0))
        return joined


def body(
    features,
    depth_weights,
    point_weights,
    branch_weight,
    pooling_weight,
    project_weight,
    refine_depth,
    refine_point,
):
    parts = lax.axis_size("space")
    assert features.shape[0] == parts
    block = features.shape[1]
    channels = features.shape[2]
    send = Sender(features)
    me = send.me
    info = jnp.stack([me // (CLASSES * send.sub), (me // send.sub) % CLASSES])
    early = channels - LATE
    for hop in (2, 3, 1):
        send.cut(me, hop, ORDER[0], 0, channels)
    origin, _ = lax.optimization_barrier((me, list(send.values.values())))
    send.cut(origin, 0, ORDER[0], 0, channels)
    for kind in ORDER[1:3]:
        for hop in FAR + NEAR:
            send.cut(origin, hop, kind, 0, channels)
    for hop in FAR:
        send.cut(origin, hop, ORDER[3], 0, early)
        send.cut(origin, hop, ORDER[3], early, LATE)
    for hop in NEAR:
        send.cut(origin, hop, ORDER[3], 0, channels)
    shared = (depth_weights, point_weights, branch_weight)
    done = []
    for index in range(3):
        after = [done[index - 2]] if index >= 2 else []
        blocks = {}
        for hop in FAR + NEAR:
            blocks[hop] = send.send(hop, ORDER[index], 0, after if hop == FAR[0] else [])
        blocks = [blocks[hop] for hop in range(BANDS)]
        done.append(class_call(info, blocks, *shared, project_weight))
    pres = [item[0] for item in done]
    channel = [item[1] for item in done]
    blocks = {}
    for hop in FAR + NEAR:
        blocks[hop] = send.send(hop, ORDER[3], 0, [done[1]] if hop == FAR[0] else [])
    late = dict(blocks)
    for hop in FAR:
        late[hop] = send.send(hop, ORDER[3], early, [done[2]] if hop == FAR[0] else [])
    blocks = [blocks[hop] for hop in range(BANDS)]
    late = [late[hop] for hop in range(BANDS)]
    sums, pool = early_call(info, blocks, *shared, pooling_weight, channel)
    refined = last_call(
        info, late, *shared, project_weight, pooling_weight, channel, sums, pool, pres,
        refine_depth, refine_point
    )
    return lax.all_to_all(refined.reshape(parts, block, HALF), "space", 0, 0, tiled=True)


def solution(mesh):
    return jax.shard_map(
        body,
        mesh=mesh,
        in_specs=(P("dp", "space", None), P(), P(), P(), P(), P(), P(), P()),
        out_specs=P("dp", "space", None),
        check_vma=False,
    )
```

time: 306 us -> 279 us (0.912)
  waiting for transfers between devices: 144 us -> 99.5 us
  starting transfers between devices: 26.2 us -> 66.5 us
  blocking collectives: 55.5 us -> 37.2 us
  local copies, waits for them, and re-layouts: 21.2 us -> 15.3 us
    ppermute x15 -> x17, waiting for transfers between devices: 144 us -> 99.5 us  [send(): lax.ppermute(value, 'space', [(i, i ^ distance) for i in range(self.parts)])]
    ppermute x15 -> x17, starting transfers between devices: 26.2 us -> 66.5 us  [send(): lax.ppermute(value, 'space', [(i, i ^ distance) for i in range(self.parts)])]
    all_to_all x1, blocking collectives: 55.5 us -> 37.2 us  [body(): lax.all_to_all(refined.reshape(parts, block, HALF), 'space', 0, 0, tiled=...]
    pallas_call x0 -> x1, Pallas kernels: none -> 11.2 us  [early_call(): pl.pallas_call(early_kernel, grid_spec=pltpu.PrefetchScalarGridSpec(num_s...]
    pallas_call x1, Pallas kernels: 20.3 us -> 10.4 us  [last_call(): pl.pallas_call(last_kernel, grid_spec=pltpu.PrefetchScalarGridSpec(num_sc...]
    convert_element_type x2 -> x0, local copies, waits for them, and re-layouts: 3.49 us -> none  [body(): depth_weights.reshape(27, 1, channels).astype(F32)]
    reshape x1 -> x0, local copies, waits for them, and re-layouts: 3.31 us -> none  [exchange(): pieces.append(value.reshape(block, channels))]
  transfers between devices with their start and end apart: 15 -> 17, of which waited for: 8 -> 4; matrix products, arithmetic and copies ran while one was open for 3% -> 3% of each run, Pallas kernels for 13% -> 18%
where the time goes in v3:
time: 279 us
  waiting for transfers between devices  99.5 us (36%)
  starting transfers between devices  66.5 us (24%)
  Pallas kernels  59.8 us (21%)
  blocking collectives  37.2 us (13%)
  local copies, waits for them, and re-layouts  15.3 us (5%)
    ppermute x17, waiting for transfers between devices, send(): lax.ppermute(value, 'space', [(i, i ^ distance) for i in range(self.parts)])  99.5 us
    ppermute x17, starting transfers between devices, send(): lax.ppermute(value, 'space', [(i, i ^ distance) for i in range(self.parts)])  66.5 us
    pallas_call x3, Pallas kernels, class_call(): pl.pallas_call(class_kernel, grid_spec=pltpu.PrefetchScalarGridSpec(num_s...  38.2 us
    all_to_all x1, blocking collectives, body(): lax.all_to_all(refined.reshape(parts, block, HALF), 'space', 0, 0, tiled=...  37.2 us
    pallas_call x1, Pallas kernels, early_call(): pl.pallas_call(early_kernel, grid_spec=pltpu.PrefetchScalarGridSpec(num_s...  11.2 us
    pallas_call x1, Pallas kernels, last_call(): pl.pallas_call(last_kernel, grid_spec=pltpu.PrefetchScalarGridSpec(num_sc...  10.4 us
    dynamic_slice x4, local copies, waits for them, and re-layouts, cut(): lax.dynamic_slice(self.features, (target, 0, start), (1, self.features.sh...  9.92 us
  transfers between devices with their start and end apart: 17, of which 4 were waited for; matrix products, arithmetic and copies ran while one was open for 3% of the time, Pallas kernels for 18%

profile of v3, /device:TPU:0, one launch (start us, length us, event | category | flops | bytes accessed | tf_op | source)
XLA Modules:
  0.0 278.5 jit_solution(4956386894690838343)
XLA Ops:
  0.0 2.8 constant_dynamic-slice_fusion.14
  2.8 5.0 %collective-permute-start.9 = (bf16[1,144,2048]{2,1,0:T(8,128)(2,1)}, bf16[1,144,2048]{2,1,0:T(8,128)(2,1)S(1)}, u32[]{:S(2)}, u32[]{:S(2)}) collective-permute-start(bf16[1,144,2048]{2,1,0:T(8,128)(2,1)} %get-tuple-element.65), channel_id=1, source_target_pairs={{0,12},{1,13},{2,14},{3,15},{4,8},{5,9},{6,10},{7,11},{8,4},{9,5},... | collective-permute-start | bytes 1769480 | tf_op jit(solution)/shard_map/ppermute | solution.py:334
  8.4 5.0 %constant_dynamic-slice_fusion.2 = (bf16[1,144,2048]{2,1,0:T(8,128)(2,1)}, bf16[1,144,2048]{2,1,0:T(8,128)(2,1)}, bf16[144,2048]{1,0:T(8,128)(2,1)S(1)}, bf16[1,...) fusion(bf16[16,144,2048]{2,1,0:T(8,128)(2,1)} %param.8, ...), kind=kLoop, calls=%fused_computation.3 | loop fusion | bytes 12976172 | tf_op jit(solution)/shard_map/dynamic_slice | solution.py:319
  13.3 2.4 collective-permute-start.4
  15.7 6.6 %collective-permute-done.9 = bf16[1,144,2048]{2,1,0:T(8,128)(2,1)S(1)} collective-permute-done((bf16[1,144,2048]{2,1,0:T(8,128)(2,1)}, bf16[1,144,2048]{2,1,0:T(8,128)(2,1)S(1)}, u32[]{:S(2)}, u32[]{:S(2)}) %collective-permute-start.9) | collective-permute-done | bytes 589856 | tf_op jit(solution)/shard_map/ppermute | solution.py:334
  22.3 4.7 %collective-permute-start.11 = (bf16[1,144,2048]{2,1,0:T(8,128)(2,1)}, bf16[1,144,2048]{2,1,0:T(8,128)(2,1)}, u32[]{:S(2)}, u32[]{:S(2)}) collective-permute-start(bf16[1,144,2048]{2,1,0:T(8,128)(2,1)} %get-tuple-element.37), channel_id=1, source_target_pairs={{0,13},{1,12},{2,15},{3,14},{4,9},{5,8},{6,11},{7,10},{8,5},{9,4},... | collective-permute-start | bytes 1769480 | tf_op jit(solution)/shard_map/ppermute | solution.py:334
  27.1 33.3 %collective-permute-done.7 = bf16[1,144,2048]{2,1,0:T(8,128)(2,1)} collective-permute-done((bf16[1,144,2048]{2,1,0:T(8,128)(2,1)}, bf16[1,144,2048]{2,1,0:T(8,128)(2,1)}, u32[]{:S(2)}, u32[]{:S(2)}) %collective-permute-start.7) | collective-permute-done | bytes 589856 | tf_op jit(solution)/shard_map/ppermute | solution.py:334
  60.6 1.5 collective-permute-start.1
  62.3 4.0 %collective-permute-start.5 = (bf16[1,144,2048]{2,1,0:T(8,128)(2,1)}, bf16[1,144,2048]{2,1,0:T(8,128)(2,1)}, u32[]{:S(2)}, u32[]{:S(2)}) collective-permute-start(bf16[1,144,2048]{2,1,0:T(8,128)(2,1)} %get-tuple-element.31), channel_id=1, source_target_pairs={{0,7},{1,6},{2,5},{3,4},{4,3},{5,2},{6,1},{7,0},{8,15},{9,14},{10,... | collective-permute-start | bytes 1769480 | tf_op jit(solution)/shard_map/ppermute | solution.py:334
  66.3 12.7 %pyramid_class.3 = (f32[576,256]{1,0:T(8,128)S(1)}, f32[8,2048]{1,0:T(8,128)S(1)}) custom-call(s32[2]{0:T(128)S(1)} %pad_add_fusion.info, bf16[144,2048]{1,0:T(8,128)(2,1)S(1)} %get-tuple-element.55.x0, bf16[144,2048]{1,0:T(8,128)(2,1)} %bitcast.5.x1, bf16[144,2048]{1,0:T(8,128)(2,1)} %bitcast.6.x2, bf16[144,2048]{1,0:T(8,128)(2,1)} %bitcast.33, ...), custom_call_target="tpu_custom_call" | custom-call | tf_op jit(solution)/shard_map/pyramid_class/pallas_call | solution.py:238
  79.9 1.9 collective-permute-start.13
  81.8 50.5 %collective-permute-done.8 = bf16[1,144,2048]{2,1,0:T(8,128)(2,1)} collective-permute-done((bf16[1,144,2048]{2,1,0:T(8,128)(2,1)}, bf16[1,144,2048]{2,1,0:T(8,128)(2,1)}, u32[]{:S(2)}, u32[]{:S(2)}) %collective-permute-start.8) | collective-permute-done | bytes 589856 | tf_op jit(solution)/shard_map/ppermute | solution.py:334
  133.8 1.2 constant_dynamic-slice_fusion
  135.0 21.9 %collective-permute-start.6 = (bf16[1,144,2048]{2,1,0:T(8,128)(2,1)S(1)}, bf16[1,144,2048]{2,1,0:T(8,128)(2,1)S(1)}, u32[]{:S(2)}, u32[]{:S(2)}) collective-permute-start(bf16[1,144,2048]{2,1,0:T(8,128)(2,1)S(1)} %get-tuple-element.32), channel_id=1, source_target_pairs={{0,6},{1,7},{2,4},{3,5},{4,2},{5,3},{6,0},{7,1},{8,14},{9,15},{10,... | collective-permute-start | bytes 1769480 | tf_op jit(solution)/shard_map/ppermute | solution.py:334
  156.9 12.7 %pyramid_class.4 = (f32[576,256]{1,0:T(8,128)S(1)}, f32[8,2048]{1,0:T(8,128)S(1)}) custom-call(s32[2]{0:T(128)S(1)} %pad_add_fusion.info, bf16[144,2048]{1,0:T(8,128)(2,1)S(1)} %bitcast.26, bf16[144,2048]{1,0:T(8,128)(2,1)} %bitcast.9.x1, bf16[144,2048]{1,0:T(8,128)(2,1)} %bitcast.10.x2, bf16[144,2048]{1,0:T(8,128)(2,1)} %bitcast.11.x3, ...), custom_call_target="tpu_custom_call" | custom-call | tf_op jit(solution)/shard_map/pyramid_class/pallas_call | solution.py:238
  170.4 9.1 %collective-permute-done.10 = bf16[1,144,2048]{2,1,0:T(8,128)(2,1)} collective-permute-done((bf16[1,144,2048]{2,1,0:T(8,128)(2,1)}, bf16[1,144,2048]{2,1,0:T(8,128)(2,1)}, u32[]{:S(2)}, u32[]{:S(2)}) %collective-permute-start.10) | collective-permute-done | bytes 589856 | tf_op jit(solution)/shard_map/ppermute | solution.py:334
  180.1 7.0 %collective-permute-start.12 = (bf16[1,144,1536]{2,1,0:T(8,128)(2,1)S(1)}, bf16[1,144,1536]{2,1,0:T(8,128)(2,1)S(1)}, u32[]{:S(2)}, u32[]{:S(2)}) collective-permute-start(bf16[1,144,1536]{2,1,0:T(8,128)(2,1)S(1)} %get-tuple-element.40), channel_id=1, source_target_pairs={{0,10},{1,11},{2,8},{3,9},{4,14},{5,15},{6,12},{7,13},{8,2},{9,3},... | collective-permute-start | bytes 1327112 | tf_op jit(solution)/shard_map/ppermute | solution.py:334
  188.2 12.7 %pyramid_class.5 = (f32[576,256]{1,0:T(8,128)S(1)}, f32[8,2048]{1,0:T(8,128)S(1)}) custom-call(s32[2]{0:T(128)S(1)} %pad_add_fusion.info, bf16[144,2048]{1,0:T(8,128)(2,1)S(1)} %bitcast.27, bf16[144,2048]{1,0:T(8,128)(2,1)} %bitcast.13.x1, bf16[144,2048]{1,0:T(8,128)(2,1)} %bitcast.14.x2, bf16[144,2048]{1,0:T(8,128)(2,1)} %bitcast.15.x3, ...), custom_call_target="tpu_custom_call" | custom-call | tf_op jit(solution)/shard_map/pyramid_class/pallas_call | solution.py:238
  201.7 15.1 %collective-permute-start.16 = (bf16[1,144,512]{2,1,0:T(8,128)(2,1)S(1)}, bf16[1,144,512]{2,1,0:T(8,128)(2,1)S(1)}, u32[]{:S(2)}, u32[]{:S(2)}) collective-permute-start(bf16[1,144,512]{2,1,0:T(8,128)(2,1)S(1)} %get-tuple-element.46), channel_id=1, source_target_pairs={{0,14},{1,15},{2,12},{3,13},{4,10},{5,11},{6,8},{7,9},{8,6},{9,7},... | collective-permute-start | bytes 442376 | tf_op jit(solution)/shard_map/ppermute | solution.py:334
  217.6 11.2 %pyramid_early.1 = (f32[4,576,256]{2,1,0:T(8,128)}, f32[16,256]{1,0:T(8,128)S(1)}) custom-call(s32[2]{0:T(128)S(1)} %pad_add_fusion.info, bf16[144,2048]{1,0:T(8,128)(2,1)S(1)} %bitcast.24, bf16[144,2048]{1,0:T(8,128)(2,1)} %bitcast.22, bf16[144,1536]{1,0:T(8,128)(2,1)S(1)} %bitcast.29, bf16[144,1536]{1,0:T(8,128)(2,1)S(1)} %bitcast.28, ...), custom_call_target="tpu_custom_call" | custom-call | tf_op jit(solution)/shard_map/pyramid_early/pallas_call | solution.py:261
  228.9 1.1 copy-done.1
  230.0 10.4 %pyramid_last.1 = bf16[2304,256]{1,0:T(8,128)(2,1)} custom-call(s32[2]{0:T(128)S(1)} %pad_add_fusion.info, bf16[144,2048]{1,0:T(8,128)(2,1)S(1)} %bitcast.25, bf16[144,2048]{1,0:T(8,128)(2,1)S(1)} %bitcast.23, bf16[144,512]{1,0:T(8,128)(2,1)S(1)} %bitcast.31, bf16[144,512]{1,0:T(8,128)(2,1)S(1)} %bitcast.30, bf16[3,9,2048]{2,1,0:T(8,128)(2,1)S(1)} %copy.9.depth, ...), custom_call_target="tpu_custom_call" | custom-call | tf_op jit(solution)/shard_map/pyramid_last/pallas_call | solution.py:286
  240.3 37.2 %all_to_all.5 = bf16[16,144,256]{2,1,0:T(8,128)(2,1)S(1)} all-to-all(bf16[16,144,256]{2,1,0:T(8,128)(2,1)} %bitcast.32), channel_id=1, replica_groups=mesh['dp'=2,'space'=16] {'space'}, dimensions={0} | all-to-all | bytes 2359296 | tf_op jit(solution)/shard_map/all_to_all | solution.py:404
  277.5 1.0 copy.15
  (41 shorter events, 7.3 us)
Async XLA Ops:
  0.0 62.1 %copy-start.8 = (bf16[3,9,2048]{2,0,1:T(4,128)(2,1)S(1)}, bf16[3,9,2048]{2,0,1:T(4,128)(2,1)}, u32[]{:S(2)}) copy-start(bf16[3,9,2048]{2,0,1:T(4,128)(2,1)} %param.9) | copy-start | bytes 331780
  2.8 19.6 %collective-permute-start.9 = (bf16[1,144,2048]{2,1,0:T(8,128)(2,1)}, bf16[1,144,2048]{2,1,0:T(8,128)(2,1)S(1)}, u32[]{:S(2)}, u32[]{:S(2)}) collective-permute-start(bf16[1,144,2048]{2,1,0:T(8,128)(2,1)} %get-tuple-element.65), channel_id=1, source_target_pairs={{0,12},{1,13},{2,14},{3,15},{4,8},{5,9},{6,10},{7,11},{8,4},{9,5},... | collective-permute-start | bytes 1769480 | tf_op jit(solution)/shard_map/ppermute | solution.py:334
  7.8 52.6 %collective-permute-start.7 = (bf16[1,144,2048]{2,1,0:T(8,128)(2,1)}, bf16[1,144,2048]{2,1,0:T(8,128)(2,1)}, u32[]{:S(2)}, u32[]{:S(2)}) collective-permute-start(bf16[1,144,2048]{2,1,0:T(8,128)(2,1)} %get-tuple-element.66), channel_id=1, source_target_pairs={{0,8},{1,9},{2,10},{3,11},{4,12},{5,13},{6,14},{7,15},{8,0},{9,1},... | collective-permute-start | bytes 1769480 | tf_op jit(solution)/shard_map/ppermute | solution.py:334
  7.8 52.8 %collective-permute-start = (bf16[1,144,2048]{2,1,0:T(8,128)(2,1)}, bf16[1,144,2048]{2,1,0:T(8,128)(2,1)}, u32[]{:S(2)}, u32[]{:S(2)}) collective-permute-start(bf16[1,144,2048]{2,1,0:T(8,128)(2,1)} %get-tuple-element.64), channel_id=1, source_target_pairs={{0,4},{1,5},{2,6},{3,7},{4,0},{5,1},{6,2},{7,3},{8,12},{9,13},{10,... | collective-permute-start | bytes 1769480 | tf_op jit(solution)/shard_map/ppermute | solution.py:334
  13.3 49.0 %collective-permute-start.4 = (bf16[1,144,2048]{2,1,0:T(8,128)(2,1)}, bf16[1,144,2048]{2,1,0:T(8,128)(2,1)}, u32[]{:S(2)}, u32[]{:S(2)}) collective-permute-start(bf16[1,144,2048]{2,1,0:T(8,128)(2,1)} %get-tuple-element.58), channel_id=1, source_target_pairs={{0,5},{1,4},{2,7},{3,6},{4,1},{5,0},{6,3},{7,2},{8,13},{9,12},{10,... | collective-permute-start | bytes 1769480 | tf_op jit(solution)/shard_map/ppermute | solution.py:334
  22.3 38.3 %copy-start.7 = (bf16[1,144,2048]{2,1,0:T(8,128)(2,1)}, bf16[1,144,2048]{2,1,0:T(8,128)(2,1)S(1)}, u32[]{:S(2)}) copy-start(bf16[1,144,2048]{2,1,0:T(8,128)(2,1)S(1)} %collective-permute-done.9) | copy-start | bytes 1769476
  22.3 57.5 %collective-permute-start.11 = (bf16[1,144,2048]{2,1,0:T(8,128)(2,1)}, bf16[1,144,2048]{2,1,0:T(8,128)(2,1)}, u32[]{:S(2)}, u32[]{:S(2)}) collective-permute-start(bf16[1,144,2048]{2,1,0:T(8,128)(2,1)} %get-tuple-element.37), channel_id=1, source_target_pairs={{0,13},{1,12},{2,15},{3,14},{4,9},{5,8},{6,11},{7,10},{8,5},{9,4},... | collective-permute-start | bytes 1769480 | tf_op jit(solution)/shard_map/ppermute | solution.py:334
  60.4 71.9 %collective-permute-start.8 = (bf16[1,144,2048]{2,1,0:T(8,128)(2,1)}, bf16[1,144,2048]{2,1,0:T(8,128)(2,1)}, u32[]{:S(2)}, u32[]{:S(2)}) collective-permute-start(bf16[1,144,2048]{2,1,0:T(8,128)(2,1)} %get-tuple-element.33), channel_id=1, source_target_pairs={{0,9},{1,8},{2,11},{3,10},{4,13},{5,12},{6,15},{7,14},{8,1},{9,0},... | collective-permute-start | bytes 1769480 | tf_op jit(solution)/shard_map/ppermute | solution.py:334
  60.6 72.1 %collective-permute-start.1 = (bf16[1,144,2048]{2,1,0:T(8,128)(2,1)}, bf16[1,144,2048]{2,1,0:T(8,128)(2,1)S(1)}, u32[]{:S(2)}, u32[]{:S(2)}) collective-permute-start(bf16[1,144,2048]{2,1,0:T(8,128)(2,1)} %get-tuple-element.28), channel_id=1, source_target_pairs={{0,1},{1,0},{2,3},{3,2},{4,5},{5,4},{6,7},{7,6},{8,9},{9,8},{10,11... | collective-permute-start | bytes 1769480 | tf_op jit(solution)/shard_map/ppermute | solution.py:334
  62.3 72.6 %collective-permute-start.5 = (bf16[1,144,2048]{2,1,0:T(8,128)(2,1)}, bf16[1,144,2048]{2,1,0:T(8,128)(2,1)}, u32[]{:S(2)}, u32[]{:S(2)}) collective-permute-start(bf16[1,144,2048]{2,1,0:T(8,128)(2,1)} %get-tuple-element.31), channel_id=1, source_target_pairs={{0,7},{1,6},{2,5},{3,4},{4,3},{5,2},{6,1},{7,0},{8,15},{9,14},{10,... | collective-permute-start | bytes 1769480 | tf_op jit(solution)/shard_map/ppermute | solution.py:334
  79.9 90.6 %collective-permute-start.13 = (bf16[1,144,2048]{2,1,0:T(8,128)(2,1)}, bf16[1,144,2048]{2,1,0:T(8,128)(2,1)}, u32[]{:S(2)}, u32[]{:S(2)}) collective-permute-start(bf16[1,144,2048]{2,1,0:T(8,128)(2,1)} %get-tuple-element.41), channel_id=1, source_target_pairs={{0,15},{1,14},{2,13},{3,12},{4,11},{5,10},{6,9},{7,8},{8,7},{9,6},... | collective-permute-start | bytes 1769480 | tf_op jit(solution)/shard_map/ppermute | solution.py:334
  132.3 47.3 %collective-permute-start.10 = (bf16[1,144,2048]{2,1,0:T(8,128)(2,1)}, bf16[1,144,2048]{2,1,0:T(8,128)(2,1)}, u32[]{:S(2)}, u32[]{:S(2)}) collective-permute-start(bf16[1,144,2048]{2,1,0:T(8,128)(2,1)} %get-tuple-element.36), channel_id=1, source_target_pairs={{0,11},{1,10},{2,9},{3,8},{4,15},{5,14},{6,13},{7,12},{8,3},{9,2},... | collective-permute-start | bytes 1769480 | tf_op jit(solution)/shard_map/ppermute | solution.py:334
  132.8 46.8 %collective-permute-start.2 = (bf16[1,144,2048]{2,1,0:T(8,128)(2,1)S(1)}, bf16[1,144,2048]{2,1,0:T(8,128)(2,1)S(1)}, u32[]{:S(2)}, u32[]{:S(2)}) collective-permute-start(bf16[1,144,2048]{2,1,0:T(8,128)(2,1)S(1)} %get-tuple-element.29), channel_id=1, source_target_pairs={{0,3},{1,2},{2,1},{3,0},{4,7},{5,6},{6,5},{7,4},{8,11},{9,10},{10,... | collective-permute-start | bytes 1769480 | tf_op jit(solution)/shard_map/ppermute | solution.py:334
  135.0 81.8 %collective-permute-start.6 = (bf16[1,144,2048]{2,1,0:T(8,128)(2,1)S(1)}, bf16[1,144,2048]{2,1,0:T(8,128)(2,1)S(1)}, u32[]{:S(2)}, u32[]{:S(2)}) collective-permute-start(bf16[1,144,2048]{2,1,0:T(8,128)(2,1)S(1)} %get-tuple-element.32), channel_id=1, source_target_pairs={{0,6},{1,7},{2,4},{3,5},{4,2},{5,3},{6,0},{7,1},{8,14},{9,15},{10,... | collective-permute-start | bytes 1769480 | tf_op jit(solution)/shard_map/ppermute | solution.py:334
  169.6 0.8 copy-start.3
  170.4 58.4 %copy-start.5 = (bf16[256,256]{1,0:T(8,128)(2,1)S(1)}, bf16[256,256]{1,0:T(8,128)(2,1)}, u32[]{:S(2)}) copy-start(bf16[256,256]{1,0:T(8,128)(2,1)} %refine_point.1) | copy-start | bytes 393220
  170.4 58.5 %copy-start.6 = (bf16[9,256]{1,0:T(8,128)(2,1)S(1)}, bf16[9,256]{1,0:T(8,128)(2,1)}, u32[]{:S(2)}) copy-start(bf16[9,256]{1,0:T(8,128)(2,1)} %refine_depth.1) | copy-start | bytes 13828
  170.4 31.3 %collective-permute-start.15 = (bf16[1,144,1536]{2,1,0:T(8,128)(2,1)S(1)}, bf16[1,144,1536]{2,1,0:T(8,128)(2,1)S(1)}, u32[]{:S(2)}, u32[]{:S(2)}) collective-permute-start(bf16[1,144,1536]{2,1,0:T(8,128)(2,1)S(1)} %get-tuple-element.45), channel_id=1, source_target_pairs={{0,14},{1,15},{2,12},{3,13},{4,10},{5,11},{6,8},{7,9},{8,6},{9,7},... | collective-permute-start | bytes 1327112 | tf_op jit(solution)/shard_map/ppermute | solution.py:334
  179.5 37.3 %collective-permute-start.3 = (bf16[1,144,2048]{2,1,0:T(8,128)(2,1)S(1)}, bf16[1,144,2048]{2,1,0:T(8,128)(2,1)S(1)}, u32[]{:S(2)}, u32[]{:S(2)}) collective-permute-start(bf16[1,144,2048]{2,1,0:T(8,128)(2,1)S(1)} %get-tuple-element.30), channel_id=1, source_target_pairs={{0,2},{1,3},{2,0},{3,1},{4,6},{5,7},{6,4},{7,5},{8,10},{9,11},{10,... | collective-permute-start | bytes 1769480 | tf_op jit(solution)/shard_map/ppermute | solution.py:334
  180.1 36.7 %collective-permute-start.12 = (bf16[1,144,1536]{2,1,0:T(8,128)(2,1)S(1)}, bf16[1,144,1536]{2,1,0:T(8,128)(2,1)S(1)}, u32[]{:S(2)}, u32[]{:S(2)}) collective-permute-start(bf16[1,144,1536]{2,1,0:T(8,128)(2,1)S(1)} %get-tuple-element.40), channel_id=1, source_target_pairs={{0,10},{1,11},{2,8},{3,9},{4,14},{5,15},{6,12},{7,13},{8,2},{9,3},... | collective-permute-start | bytes 1327112 | tf_op jit(solution)/shard_map/ppermute | solution.py:334
  201.7 27.1 %collective-permute-start.16 = (bf16[1,144,512]{2,1,0:T(8,128)(2,1)S(1)}, bf16[1,144,512]{2,1,0:T(8,128)(2,1)S(1)}, u32[]{:S(2)}, u32[]{:S(2)}) collective-permute-start(bf16[1,144,512]{2,1,0:T(8,128)(2,1)S(1)} %get-tuple-element.46), channel_id=1, source_target_pairs={{0,14},{1,15},{2,12},{3,13},{4,10},{5,11},{6,8},{7,9},{8,6},{9,7},... | collective-permute-start | bytes 442376 | tf_op jit(solution)/shard_map/ppermute | solution.py:334
  216.8 12.0 %collective-permute-start.14 = (bf16[1,144,512]{2,1,0:T(8,128)(2,1)S(1)}, bf16[1,144,512]{2,1,0:T(8,128)(2,1)S(1)}, u32[]{:S(2)}, u32[]{:S(2)}) collective-permute-start(bf16[1,144,512]{2,1,0:T(8,128)(2,1)S(1)} %get-tuple-element.44), channel_id=1, source_target_pairs={{0,10},{1,11},{2,8},{3,9},{4,14},{5,15},{6,12},{7,13},{8,2},{9,3},... | collective-permute-start | bytes 442376 | tf_op jit(solution)/shard_map/ppermute | solution.py:334
  216.8 0.8 copy-start
  228.9 1.1 copy-start.1
  (2 other events, 1.6 us)

commit v4 on v3

--- a/solution.py
+++ b/solution.py
@@ -18,6 +18,8 @@
 ORDER = (0, 1, 3, 2)
 NEAR = (1, 0)
 FAR = (2, 3)
+FAR_LAG = 3
+NEAR_LAG = 3
 F32 = jnp.float32
 BF16 = jnp.bfloat16
 
@@ -41,49 +43,42 @@
         shifted[band, :, 4:52, :] = wide
 
 
-def spread_rows(plain, shifted, taps, spread, row, lane):
+def spread_branch(plain, shifted, taps, spread, branch, row, lane):
     lanes = pl.ds(lane, HALF)
-    for branch in range(3):
-        weights = [
-            jnp.broadcast_to(taps[branch, tap:tap + 1, lanes], (8, HALF)) for tap in range(9)
-        ]
-        for band in range(BANDS):
-            tiles = []
-            for tile in range(COLS // 8):
-                total = None
-                for up in (-1, 0, 1):
-                    source = band + up * (branch + 1)
-                    if not 0 <= source < BANDS:
+    weights = [jnp.broadcast_to(taps[branch, tap:tap + 1, lanes], (8, HALF)) for tap in range(9)]
+    for band in range(BANDS):
+        tiles = []
+        for tile in range(COLS // 8):
+            total = None
+            for up in (-1, 0, 1):
+                source = band + up * (branch + 1)
+                if not 0 <= source < BANDS:
+                    continue
+                for side in (-1, 0, 1):
+                    shift = side * RATE * (branch + 1)
+                    if 8 * tile + shift + 7 < 0 or 8 * tile + shift >= COLS:
                         continue
-                    for side in (-1, 0, 1):
-                        shift = side * RATE * (branch + 1)
-                        if 8 * tile + shift + 7 < 0 or 8 * tile + shift >= COLS:
-                            continue
-                        if shift % 8 == 0:
-                            value = plain[source, row, 8 * tile + shift:8 * tile + shift + 8, lanes]
-                        else:
-                            start = 8 * tile + shift + 4
-                            value = shifted[source, row, start:start + 8, lanes]
-                        term = value * weights[3 * (up + 1) + (side + 1)]
-                        total = term if total is None else total + term
-                tiles.append(jnp.maximum(total, 0.0))
-            sums = jnp.concatenate(tiles, axis=0).astype(BF16)
-            spread[branch, band, pl.ds(pl.multiple_of(row * COLS, COLS), COLS), lanes] = sums
+                    if shift % 8 == 0:
+                        value = plain[source, row, 8 * tile + shift:8 * tile + shift + 8, lanes]
+                    else:
+                        start = 8 * tile + shift + 4
+                        value = shifted[source, row, start:start + 8, lanes]
+                    term = value * weights[3 * (up + 1) + (side + 1)]
+                    total = term if total is None else total + term
+            tiles.append(jnp.maximum(total, 0.0))
+        sums = jnp.concatenate(tiles, axis=0).astype(BF16)
+        spread[branch, band, row * COLS:(row + 1) * COLS, lanes] = sums
 
 
 def pyramid_tile(info, x_refs, depth, point, branch, plain, shifted, raw, spread, taps):
     width = plain.shape[-1]
     load_tile(info, x_refs, depth, plain, shifted, raw, taps)
-
-    def step(index, carry):
-        spread_rows(plain, shifted, taps, spread, index // (width // HALF),
-                    pl.multiple_of((index % (width // HALF)) * HALF, HALF))
-        return carry
-
-    lax.fori_loop(0, CLASS_ROWS * (width // HALF), step, 0)
     cells = BANDS * BLOCK
     parts = [jnp.dot(raw[...].reshape(cells, width), branch[...], preferred_element_type=F32)]
     for index in range(3):
+        for row in range(CLASS_ROWS):
+            for lane in range(0, width, HALF):
+                spread_branch(plain, shifted, taps, spread, index, row, lane)
         parts.append(
             jnp.dot(spread[index].reshape(cells, width), point[index], preferred_element_type=F32)
         )
@@ -91,15 +86,9 @@
 
 
 def accumulate(sums, parts):
-    @pl.when(pl.program_id(0) == 0)
-    def _():
-        for index in range(4):
-            sums[index] = parts[index]
-
-    @pl.when(pl.program_id(0) > 0)
-    def _():
-        for index in range(4):
-            sums[index] += parts[index]
+    first = pl.program_id(0) == 0
+    for index in range(4):
+        sums[index] = jnp.where(first, 0.0, sums[index]) + parts[index]
 
 
 def channel_sum(plain):
@@ -190,7 +179,7 @@
         rows[pl.ds(pl.multiple_of(row * COLS, COLS), COLS), :] = total
         return carry
 
-    lax.fori_loop(0, ROWS, step, 0)
+    lax.fori_loop(0, ROWS, step, 0, unroll=4)
     product = jnp.dot(rows[...], refine_point[...], preferred_element_type=F32)
     out[...] = jnp.maximum(product, 0.0).astype(BF16)
 
@@ -327,7 +316,8 @@
             distance = (hop * CLASSES + kind) * self.sub + piece
             value = self.values[distance, start]
             if distance:
-                before = [chain[-2][piece]] if len(chain) >= 2 else []
+                lag = FAR_LAG if hop in FAR else NEAR_LAG
+                before = [chain[-lag][piece]] if len(chain) >= lag else []
                 before += after
                 if before:
                     value, _ = lax.optimization_barrier((value, before))
@@ -393,7 +383,7 @@
         blocks[hop] = send.send(hop, ORDER[3], 0, [done[1]] if hop == FAR[0] else [])
     late = dict(blocks)
     for hop in FAR:
-        late[hop] = send.send(hop, ORDER[3], early, [done[2]] if hop == FAR[0] else [])
+        late[hop] = send.send(hop, ORDER[3], early, [done[2]] if hop == FAR[1] else [])
     blocks = [blocks[hop] for hop in range(BANDS)]
     late = [late[hop] for hop in range(BANDS)]
     sums, pool = early_call(info, blocks, *shared, pooling_weight, channel)

time: 279 us -> 266 us (0.953)
  waiting for transfers between devices: 99.5 us -> 44 us
  starting transfers between devices: 66.5 us -> 118 us
  Pallas kernels: 59.8 us -> 49.3 us
    ppermute x17, waiting for transfers between devices: 99.5 us -> 44 us  [send(): lax.ppermute(value, 'space', [(i, i ^ distance) for i in range(self.parts)])]
    ppermute x17, starting transfers between devices: 66.5 us -> 118 us  [send(): lax.ppermute(value, 'space', [(i, i ^ distance) for i in range(self.parts)])]
    pallas_call x3, Pallas kernels: 38.2 us -> 30.3 us  [class_call(): pl.pallas_call(class_kernel, grid_spec=pltpu.PrefetchScalarGridSpec(num_s...]
    reshape x0 -> x1, local copies, waits for them, and re-layouts: none -> 5.01 us  [send(): return got[0].reshape(block, size)]
    dynamic_slice x4 -> x3, local copies, waits for them, and re-layouts: 9.92 us -> 4.95 us  [cut(): lax.dynamic_slice(self.features, (target, 0, start), (1, self.features.sh...]
    unnamed x20 -> x22, local copies, waits for them, and re-layouts: 5.39 us -> 6.26 us
  transfers between devices with their start and end apart: 17 -> 17, of which waited for: 4 -> 5; matrix products, arithmetic and copies ran while one was open for 3% -> 3% of each run, Pallas kernels for 18% -> 15%
where the time goes in v4:
time: 266 us; the launch traced here: 265 us
  starting transfers between devices  118 us (44%)
  Pallas kernels  49.3 us (19%)
  waiting for transfers between devices  44 us (17%)
  blocking collectives  37.5 us (14%)
  local copies, waits for them, and re-layouts  16.2 us (6%)
    ppermute x17, starting transfers between devices, send(): lax.ppermute(value, 'space', [(i, i ^ distance) for i in range(self.parts)])  118 us
    ppermute x17, waiting for transfers between devices, send(): lax.ppermute(value, 'space', [(i, i ^ distance) for i in range(self.parts)])  44 us
    all_to_all x1, blocking collectives, body(): lax.all_to_all(refined.reshape(parts, block, HALF), 'space', 0, 0, tiled=...  37.5 us
    pallas_call x3, Pallas kernels, class_call(): pl.pallas_call(class_kernel, grid_spec=pltpu.PrefetchScalarGridSpec(num_s...  30.3 us
    pallas_call x1, Pallas kernels, last_call(): pl.pallas_call(last_kernel, grid_spec=pltpu.PrefetchScalarGridSpec(num_sc...  9.9 us
    pallas_call x1, Pallas kernels, early_call(): pl.pallas_call(early_kernel, grid_spec=pltpu.PrefetchScalarGridSpec(num_s...  9.07 us
    unnamed x22, local copies, waits for them, and re-layouts  6.26 us
  transfers between devices with their start and end apart: 17, of which 5 were waited for; matrix products, arithmetic and copies ran while one was open for 3% of the time, Pallas kernels for 15%

profile of v4, /device:TPU:0, one launch (start us, length us, event | category | flops | bytes accessed | tf_op | source)
XLA Modules:
  0.0 265.5 jit_solution(18422204284442245812)
XLA Ops:
  0.0 2.7 %constant_dynamic-slice_fusion.14 = (bf16[1,144,2048]{2,1,0:T(8,128)(2,1)}, bf16[1,144,2048]{2,1,0:T(8,128)(2,1)}, bf16[1,144,2048]{2,1,0:T(8,128)(2,1)}) fusion(bf16[16,144,2048]{2,1,0:T(8,128)(2,1)} %param.8, s32[]{:T(128)S(6)} %select_n.66, s32[]{:T(128)S(6)} %select_n.65, s32[]{:T(128)S(6)} %select_n.64), kind=kLoop, calls=%fused_computation.15 | loop fusion | bytes 3538956 | tf_op jit(solution)/shard_map/dynamic_slice | solution.py:308
  2.7 3.0 %collective-permute-start = (bf16[1,144,2048]{2,1,0:T(8,128)(2,1)}, bf16[1,144,2048]{2,1,0:T(8,128)(2,1)S(1)}, u32[]{:S(2)}, u32[]{:S(2)}) collective-permute-start(bf16[1,144,2048]{2,1,0:T(8,128)(2,1)} %get-tuple-element.60), channel_id=1, source_target_pairs={{0,4},{1,5},{2,6},{3,7},{4,0},{5,1},{6,2},{7,3},{8,12},{9,13},{10,... | collective-permute-start | bytes 1769480 | tf_op jit(solution)/shard_map/ppermute | solution.py:324
  5.8 2.6 collective-permute-start.8
  8.4 5.0 %dynamic-slice_bitcast_fusion = (bf16[144,2048]{1,0:T(8,128)(2,1)S(1)}, bf16[1,144,2048]{2,1,0:T(8,128)(2,1)}, bf16[1,144,2048]{2,1,0:T(8,128)(2,1)S(1)}, bf16[1...) fusion(bf16[16,144,2048]{2,1,0:T(8,128)(2,1)} %param.8, ...), kind=kLoop, calls=%fused_computation | loop fusion | bytes 12976172 | tf_op jit(solution)/shard_map/reshape | solution.py:332
  13.4 2.8 %collective-permute-start.5 = (bf16[1,144,2048]{2,1,0:T(8,128)(2,1)}, bf16[1,144,2048]{2,1,0:T(8,128)(2,1)}, u32[]{:S(2)}, u32[]{:S(2)}) collective-permute-start(bf16[1,144,2048]{2,1,0:T(8,128)(2,1)} %get-tuple-element.52), channel_id=1, source_target_pairs={{0,9},{1,8},{2,11},{3,10},{4,13},{5,12},{6,15},{7,14},{8,1},{9,0},... | collective-permute-start | bytes 1769480 | tf_op jit(solution)/shard_map/ppermute | solution.py:324
  16.2 2.4 collective-permute-start.10
  18.7 13.3 %collective-permute-done = bf16[1,144,2048]{2,1,0:T(8,128)(2,1)S(1)} collective-permute-done((bf16[1,144,2048]{2,1,0:T(8,128)(2,1)}, bf16[1,144,2048]{2,1,0:T(8,128)(2,1)S(1)}, u32[]{:S(2)}, u32[]{:S(2)}) %collective-permute-start) | collective-permute-done | bytes 589856 | tf_op jit(solution)/shard_map/ppermute | solution.py:324
  32.8 2.0 collective-permute-start.3
  35.0 26.2 %collective-permute-done.8 = bf16[1,144,2048]{2,1,0:T(8,128)(2,1)} collective-permute-done((bf16[1,144,2048]{2,1,0:T(8,128)(2,1)}, bf16[1,144,2048]{2,1,0:T(8,128)(2,1)}, u32[]{:S(2)}, u32[]{:S(2)}) %collective-permute-start.8) | collective-permute-done | bytes 589856 | tf_op jit(solution)/shard_map/ppermute | solution.py:324
  61.2 3.4 %collective-permute-start.9 = (bf16[1,144,2048]{2,1,0:T(8,128)(2,1)}, bf16[1,144,2048]{2,1,0:T(8,128)(2,1)}, u32[]{:S(2)}, u32[]{:S(2)}) collective-permute-start(bf16[1,144,2048]{2,1,0:T(8,128)(2,1)} %get-tuple-element.31), channel_id=1, source_target_pairs={{0,13},{1,12},{2,15},{3,14},{4,9},{5,8},{6,11},{7,10},{8,5},{9,4},... | collective-permute-start | bytes 1769480 | tf_op jit(solution)/shard_map/ppermute | solution.py:324
  64.6 24.3 %collective-permute-start.1 = (bf16[1,144,2048]{2,1,0:T(8,128)(2,1)}, bf16[1,144,2048]{2,1,0:T(8,128)(2,1)}, u32[]{:S(2)}, u32[]{:S(2)}) collective-permute-start(bf16[1,144,2048]{2,1,0:T(8,128)(2,1)} %get-tuple-element.26), channel_id=1, source_target_pairs={{0,7},{1,6},{2,5},{3,4},{4,3},{5,2},{6,1},{7,0},{8,15},{9,14},{10,... | collective-permute-start | bytes 1769480 | tf_op jit(solution)/shard_map/ppermute | solution.py:324
  88.9 10.1 %pyramid_class.4 = (f32[576,256]{1,0:T(8,128)S(1)}, f32[8,2048]{1,0:T(8,128)S(1)}) custom-call(s32[2]{0:T(128)S(1)} %pad_add_fusion.info, bf16[144,2048]{1,0:T(8,128)(2,1)S(1)} %get-tuple-element.47.x0, bf16[144,2048]{1,0:T(8,128)(2,1)} %bitcast.33, bf16[144,2048]{1,0:T(8,128)(2,1)} %bitcast.13.x2, bf16[144,2048]{1,0:T(8,128)(2,1)} %bitcast.14.x3, ...), custom_call_target="tpu_custom_call" | custom-call | tf_op jit(solution)/shard_map/pyramid_class/pallas_call | solution.py:227
  100.9 2.6 collective-permute-start.6
  103.5 1.9 collective-permute-start.12
  106.6 32.9 %collective-permute-start.4 = (bf16[1,144,2048]{2,1,0:T(8,128)(2,1)S(1)}, bf16[1,144,2048]{2,1,0:T(8,128)(2,1)S(1)}, u32[]{:S(2)}, u32[]{:S(2)}) collective-permute-start(bf16[1,144,2048]{2,1,0:T(8,128)(2,1)S(1)} %get-tuple-element.28), channel_id=1, source_target_pairs={{0,6},{1,7},{2,4},{3,5},{4,2},{5,3},{6,0},{7,1},{8,14},{9,15},{10,... | collective-permute-start | bytes 1769480 | tf_op jit(solution)/shard_map/ppermute | solution.py:324
  139.5 10.1 %pyramid_class.3 = (f32[576,256]{1,0:T(8,128)S(1)}, f32[8,2048]{1,0:T(8,128)S(1)}) custom-call(s32[2]{0:T(128)S(1)} %pad_add_fusion.info, bf16[144,2048]{1,0:T(8,128)(2,1)S(1)} %bitcast.26, bf16[144,2048]{1,0:T(8,128)(2,1)} %bitcast.6.x1, bf16[144,2048]{1,0:T(8,128)(2,1)} %bitcast.7.x2, bf16[144,2048]{1,0:T(8,128)(2,1)} %bitcast.8.x3, ...), custom_call_target="tpu_custom_call" | custom-call | tf_op jit(solution)/shard_map/pyramid_class/pallas_call | solution.py:227
  151.0 2.6 collective-permute-done.14
  153.7 6.8 %collective-permute-start.16 = (bf16[1,144,1536]{2,1,0:T(8,128)(2,1)S(1)}, bf16[1,144,1536]{2,1,0:T(8,128)(2,1)S(1)}, u32[]{:S(2)}, u32[]{:S(2)}) collective-permute-start(bf16[1,144,1536]{2,1,0:T(8,128)(2,1)S(1)} %get-tuple-element.42), channel_id=1, source_target_pairs={{0,14},{1,15},{2,12},{3,13},{4,10},{5,11},{6,8},{7,9},{8,6},{9,7},... | collective-permute-start | bytes 1327112 | tf_op jit(solution)/shard_map/ppermute | solution.py:324
  161.4 28.3 %collective-permute-start.7 = (bf16[1,144,512]{2,1,0:T(8,128)(2,1)S(1)}, bf16[1,144,512]{2,1,0:T(8,128)(2,1)S(1)}, u32[]{:S(2)}, u32[]{:S(2)}) collective-permute-start(bf16[1,144,512]{2,1,0:T(8,128)(2,1)S(1)} %get-tuple-element.30), channel_id=1, source_target_pairs={{0,10},{1,11},{2,8},{3,9},{4,14},{5,15},{6,12},{7,13},{8,2},{9,3},... | collective-permute-start | bytes 442376 | tf_op jit(solution)/shard_map/ppermute | solution.py:324
  189.7 10.1 %pyramid_class.5 = (f32[576,256]{1,0:T(8,128)S(1)}, f32[8,2048]{1,0:T(8,128)S(1)}) custom-call(s32[2]{0:T(128)S(1)} %pad_add_fusion.info, bf16[144,2048]{1,0:T(8,128)(2,1)S(1)} %bitcast.27, bf16[144,2048]{1,0:T(8,128)(2,1)} %bitcast.10.x1, bf16[144,2048]{1,0:T(8,128)(2,1)} %bitcast.34, bf16[144,2048]{1,0:T(8,128)(2,1)} %bitcast.16.x3, ...), custom_call_target="tpu_custom_call" | custom-call | tf_op jit(solution)/shard_map/pyramid_class/pallas_call | solution.py:227
  200.6 3.8 %collective-permute-start.15 = (bf16[1,144,512]{2,1,0:T(8,128)(2,1)S(1)}, bf16[1,144,512]{2,1,0:T(8,128)(2,1)S(1)}, u32[]{:S(2)}, u32[]{:S(2)}) collective-permute-start(bf16[1,144,512]{2,1,0:T(8,128)(2,1)S(1)} %get-tuple-element.41), channel_id=1, source_target_pairs={{0,14},{1,15},{2,12},{3,13},{4,10},{5,11},{6,8},{7,9},{8,6},{9,7},... | collective-permute-start | bytes 442376 | tf_op jit(solution)/shard_map/ppermute | solution.py:324
  205.3 9.1 %pyramid_early.1 = (f32[4,576,256]{2,1,0:T(8,128)}, f32[16,256]{1,0:T(8,128)S(1)}) custom-call(s32[2]{0:T(128)S(1)} %pad_add_fusion.info, bf16[144,2048]{1,0:T(8,128)(2,1)S(1)} %bitcast.24, bf16[144,2048]{1,0:T(8,128)(2,1)} %bitcast.22, bf16[144,1536]{1,0:T(8,128)(2,1)S(1)} %bitcast.28, bf16[144,1536]{1,0:T(8,128)(2,1)S(1)} %bitcast.29, ...), custom_call_target="tpu_custom_call" | custom-call | tf_op jit(solution)/shard_map/pyramid_early/pallas_call | solution.py:250
  217.1 9.9 %pyramid_last.1 = bf16[2304,256]{1,0:T(8,128)(2,1)} custom-call(s32[2]{0:T(128)S(1)} %pad_add_fusion.info, bf16[144,2048]{1,0:T(8,128)(2,1)S(1)} %bitcast.25, bf16[144,2048]{1,0:T(8,128)(2,1)S(1)} %bitcast.23, bf16[144,512]{1,0:T(8,128)(2,1)S(1)} %bitcast.30, bf16[144,512]{1,0:T(8,128)(2,1)S(1)} %bitcast.31, bf16[3,9,2048]{2,1,0:T(8,128)(2,1)S(1)} %copy.9.depth, ...), custom_call_target="tpu_custom_call" | custom-call | tf_op jit(solution)/shard_map/pyramid_last/pallas_call | solution.py:275
  227.0 37.5 %all_to_all.5 = bf16[16,144,256]{2,1,0:T(8,128)(2,1)S(1)} all-to-all(bf16[16,144,256]{2,1,0:T(8,128)(2,1)} %bitcast.32), channel_id=1, replica_groups=mesh['dp'=2,'space'=16] {'space'}, dimensions={0} | all-to-all | bytes 2359296 | tf_op jit(solution)/shard_map/all_to_all | solution.py:394
  (43 shorter events, 11.8 us)
Async XLA Ops:
  0.0 34.8 %copy-start.9 = (bf16[3,9,2048]{2,0,1:T(4,128)(2,1)S(1)}, bf16[3,9,2048]{2,0,1:T(4,128)(2,1)}, u32[]{:S(2)}) copy-start(bf16[3,9,2048]{2,0,1:T(4,128)(2,1)} %param.9) | copy-start | bytes 331780
  2.7 29.3 %collective-permute-start = (bf16[1,144,2048]{2,1,0:T(8,128)(2,1)}, bf16[1,144,2048]{2,1,0:T(8,128)(2,1)S(1)}, u32[]{:S(2)}, u32[]{:S(2)}) collective-permute-start(bf16[1,144,2048]{2,1,0:T(8,128)(2,1)} %get-tuple-element.60), channel_id=1, source_target_pairs={{0,4},{1,5},{2,6},{3,7},{4,0},{5,1},{6,2},{7,3},{8,12},{9,13},{10,... | collective-permute-start | bytes 1769480 | tf_op jit(solution)/shard_map/ppermute | solution.py:324
  5.8 55.4 %collective-permute-start.8 = (bf16[1,144,2048]{2,1,0:T(8,128)(2,1)}, bf16[1,144,2048]{2,1,0:T(8,128)(2,1)}, u32[]{:S(2)}, u32[]{:S(2)}) collective-permute-start(bf16[1,144,2048]{2,1,0:T(8,128)(2,1)} %get-tuple-element.62), channel_id=1, source_target_pairs={{0,8},{1,9},{2,10},{3,11},{4,12},{5,13},{6,14},{7,15},{8,0},{9,1},... | collective-permute-start | bytes 1769480 | tf_op jit(solution)/shard_map/ppermute | solution.py:324
  8.4 56.2 %collective-permute-start.13 = (bf16[1,144,2048]{2,1,0:T(8,128)(2,1)}, bf16[1,144,2048]{2,1,0:T(8,128)(2,1)}, u32[]{:S(2)}, u32[]{:S(2)}) collective-permute-start(bf16[1,144,2048]{2,1,0:T(8,128)(2,1)} %get-tuple-element.61), channel_id=1, source_target_pairs={{0,12},{1,13},{2,14},{3,15},{4,8},{5,9},{6,10},{7,11},{8,4},{9,5},... | collective-permute-start | bytes 1769480 | tf_op jit(solution)/shard_map/ppermute | solution.py:324
  13.4 86.7 %collective-permute-start.5 = (bf16[1,144,2048]{2,1,0:T(8,128)(2,1)}, bf16[1,144,2048]{2,1,0:T(8,128)(2,1)}, u32[]{:S(2)}, u32[]{:S(2)}) collective-permute-start(bf16[1,144,2048]{2,1,0:T(8,128)(2,1)} %get-tuple-element.52), channel_id=1, source_target_pairs={{0,9},{1,8},{2,11},{3,10},{4,13},{5,12},{6,15},{7,14},{8,1},{9,0},... | collective-permute-start | bytes 1769480 | tf_op jit(solution)/shard_map/ppermute | solution.py:324
  16.2 84.7 %collective-permute-start.10 = (bf16[1,144,2048]{2,1,0:T(8,128)(2,1)}, bf16[1,144,2048]{2,1,0:T(8,128)(2,1)}, u32[]{:S(2)}, u32[]{:S(2)}) collective-permute-start(bf16[1,144,2048]{2,1,0:T(8,128)(2,1)} %get-tuple-element.50), channel_id=1, source_target_pairs={{0,5},{1,4},{2,7},{3,6},{4,1},{5,0},{6,3},{7,2},{8,13},{9,12},{10,... | collective-permute-start | bytes 1769480 | tf_op jit(solution)/shard_map/ppermute | solution.py:324
  32.8 70.6 %collective-permute-start.3 = (bf16[1,144,2048]{2,1,0:T(8,128)(2,1)}, bf16[1,144,2048]{2,1,0:T(8,128)(2,1)S(1)}, u32[]{:S(2)}, u32[]{:S(2)}) collective-permute-start(bf16[1,144,2048]{2,1,0:T(8,128)(2,1)} %get-tuple-element.54), channel_id=1, source_target_pairs={{0,1},{1,0},{2,3},{3,2},{4,5},{5,4},{6,7},{7,6},{8,9},{9,8},{10,11... | collective-permute-start | bytes 1769480 | tf_op jit(solution)/shard_map/ppermute | solution.py:324
  61.2 45.4 %collective-permute-start.9 = (bf16[1,144,2048]{2,1,0:T(8,128)(2,1)}, bf16[1,144,2048]{2,1,0:T(8,128)(2,1)}, u32[]{:S(2)}, u32[]{:S(2)}) collective-permute-start(bf16[1,144,2048]{2,1,0:T(8,128)(2,1)} %get-tuple-element.31), channel_id=1, source_target_pairs={{0,13},{1,12},{2,15},{3,14},{4,9},{5,8},{6,11},{7,10},{8,5},{9,4},... | collective-permute-start | bytes 1769480 | tf_op jit(solution)/shard_map/ppermute | solution.py:324
  64.6 85.9 %collective-permute-start.1 = (bf16[1,144,2048]{2,1,0:T(8,128)(2,1)}, bf16[1,144,2048]{2,1,0:T(8,128)(2,1)}, u32[]{:S(2)}, u32[]{:S(2)}) collective-permute-start(bf16[1,144,2048]{2,1,0:T(8,128)(2,1)} %get-tuple-element.26), channel_id=1, source_target_pairs={{0,7},{1,6},{2,5},{3,4},{4,3},{5,2},{6,1},{7,0},{8,15},{9,14},{10,... | collective-permute-start | bytes 1769480 | tf_op jit(solution)/shard_map/ppermute | solution.py:324
  99.0 0.8 copy-start.2
  100.0 53.6 %collective-permute-start.14 = (bf16[1,144,2048]{2,1,0:T(8,128)(2,1)}, bf16[1,144,2048]{2,1,0:T(8,128)(2,1)S(1)}, u32[]{:S(2)}, u32[]{:S(2)}) collective-permute-start(bf16[1,144,2048]{2,1,0:T(8,128)(2,1)} %get-tuple-element.38), channel_id=1, source_target_pairs={{0,11},{1,10},{2,9},{3,8},{4,15},{5,14},{6,13},{7,12},{8,3},{9,2},... | collective-permute-start | bytes 1769480 | tf_op jit(solution)/shard_map/ppermute | solution.py:324
  100.9 52.8 %collective-permute-start.6 = (bf16[1,144,2048]{2,1,0:T(8,128)(2,1)}, bf16[1,144,2048]{2,1,0:T(8,128)(2,1)}, u32[]{:S(2)}, u32[]{:S(2)}) collective-permute-start(bf16[1,144,2048]{2,1,0:T(8,128)(2,1)} %get-tuple-element.29), channel_id=1, source_target_pairs={{0,15},{1,14},{2,13},{3,12},{4,11},{5,10},{6,9},{7,8},{8,7},{9,6},... | collective-permute-start | bytes 1769480 | tf_op jit(solution)/shard_map/ppermute | solution.py:324
  103.5 58.0 %collective-permute-start.12 = (bf16[1,144,2048]{2,1,0:T(8,128)(2,1)S(1)}, bf16[1,144,2048]{2,1,0:T(8,128)(2,1)S(1)}, u32[]{:S(2)}, u32[]{:S(2)}) collective-permute-start(bf16[1,144,2048]{2,1,0:T(8,128)(2,1)S(1)} %get-tuple-element.35), channel_id=1, source_target_pairs={{0,3},{1,2},{2,1},{3,0},{4,7},{5,6},{6,5},{7,4},{8,11},{9,10},{10,... | collective-permute-start | bytes 1769480 | tf_op jit(solution)/shard_map/ppermute | solution.py:324
  106.6 97.9 %collective-permute-start.4 = (bf16[1,144,2048]{2,1,0:T(8,128)(2,1)S(1)}, bf16[1,144,2048]{2,1,0:T(8,128)(2,1)S(1)}, u32[]{:S(2)}, u32[]{:S(2)}) collective-permute-start(bf16[1,144,2048]{2,1,0:T(8,128)(2,1)S(1)} %get-tuple-element.28), channel_id=1, source_target_pairs={{0,6},{1,7},{2,4},{3,5},{4,2},{5,3},{6,0},{7,1},{8,14},{9,15},{10,... | collective-permute-start | bytes 1769480 | tf_op jit(solution)/shard_map/ppermute | solution.py:324
  149.6 0.8 copy-start.3
  150.5 65.5 %copy-start.5 = (bf16[256,256]{1,0:T(8,128)(2,1)S(1)}, bf16[256,256]{1,0:T(8,128)(2,1)}, u32[]{:S(2)}) copy-start(bf16[256,256]{1,0:T(8,128)(2,1)} %refine_point.1) | copy-start | bytes 393220
  150.5 65.5 %copy-start.6 = (bf16[9,256]{1,0:T(8,128)(2,1)S(1)}, bf16[9,256]{1,0:T(8,128)(2,1)}, u32[]{:S(2)}) copy-start(bf16[9,256]{1,0:T(8,128)(2,1)} %refine_depth.1) | copy-start | bytes 13828
  150.5 54.0 %collective-permute-start.2 = (bf16[1,144,2048]{2,1,0:T(8,128)(2,1)S(1)}, bf16[1,144,2048]{2,1,0:T(8,128)(2,1)S(1)}, u32[]{:S(2)}, u32[]{:S(2)}) collective-permute-start(bf16[1,144,2048]{2,1,0:T(8,128)(2,1)S(1)} %get-tuple-element.27), channel_id=1, source_target_pairs={{0,2},{1,3},{2,0},{3,1},{4,6},{5,7},{6,4},{7,5},{8,10},{9,11},{10,... | collective-permute-start | bytes 1769480 | tf_op jit(solution)/shard_map/ppermute | solution.py:324
  153.6 36.1 %copy-start.8 = (bf16[1,144,2048]{2,1,0:T(8,128)(2,1)}, bf16[1,144,2048]{2,1,0:T(8,128)(2,1)S(1)}, u32[]{:S(2)}) copy-start(bf16[1,144,2048]{2,1,0:T(8,128)(2,1)S(1)} %collective-permute-done.14) | copy-start | bytes 1769476
  153.7 47.0 %collective-permute-start.11 = (bf16[1,144,1536]{2,1,0:T(8,128)(2,1)S(1)}, bf16[1,144,1536]{2,1,0:T(8,128)(2,1)S(1)}, u32[]{:S(2)}, u32[]{:S(2)}) collective-permute-start(bf16[1,144,1536]{2,1,0:T(8,128)(2,1)S(1)} %get-tuple-element.34), channel_id=1, source_target_pairs={{0,10},{1,11},{2,8},{3,9},{4,14},{5,15},{6,12},{7,13},{8,2},{9,3},... | collective-permute-start | bytes 1327112 | tf_op jit(solution)/shard_map/ppermute | solution.py:324
  153.7 50.8 %collective-permute-start.16 = (bf16[1,144,1536]{2,1,0:T(8,128)(2,1)S(1)}, bf16[1,144,1536]{2,1,0:T(8,128)(2,1)S(1)}, u32[]{:S(2)}, u32[]{:S(2)}) collective-permute-start(bf16[1,144,1536]{2,1,0:T(8,128)(2,1)S(1)} %get-tuple-element.42), channel_id=1, source_target_pairs={{0,14},{1,15},{2,12},{3,13},{4,10},{5,11},{6,8},{7,9},{8,6},{9,7},... | collective-permute-start | bytes 1327112 | tf_op jit(solution)/shard_map/ppermute | solution.py:324
  161.4 54.5 %collective-permute-start.7 = (bf16[1,144,512]{2,1,0:T(8,128)(2,1)S(1)}, bf16[1,144,512]{2,1,0:T(8,128)(2,1)S(1)}, u32[]{:S(2)}, u32[]{:S(2)}) collective-permute-start(bf16[1,144,512]{2,1,0:T(8,128)(2,1)S(1)} %get-tuple-element.30), channel_id=1, source_target_pairs={{0,10},{1,11},{2,8},{3,9},{4,14},{5,15},{6,12},{7,13},{8,2},{9,3},... | collective-permute-start | bytes 442376 | tf_op jit(solution)/shard_map/ppermute | solution.py:324
  200.6 15.4 %collective-permute-start.15 = (bf16[1,144,512]{2,1,0:T(8,128)(2,1)S(1)}, bf16[1,144,512]{2,1,0:T(8,128)(2,1)S(1)}, u32[]{:S(2)}, u32[]{:S(2)}) collective-permute-start(bf16[1,144,512]{2,1,0:T(8,128)(2,1)S(1)} %get-tuple-element.41), channel_id=1, source_target_pairs={{0,14},{1,15},{2,12},{3,13},{4,10},{5,11},{6,8},{7,9},{8,6},{9,7},... | collective-permute-start | bytes 442376 | tf_op jit(solution)/shard_map/ppermute | solution.py:324
  216.0 1.1 copy-start.1
  (3 other events, 2.5 us)

commit v5 on v4

--- a/solution.py
+++ b/solution.py
@@ -16,6 +16,7 @@
 HALF = 256
 LATE = 512
 ORDER = (0, 1, 3, 2)
+READY = RATE - CLASS_ROWS - 2
 NEAR = (1, 0)
 FAR = (2, 3)
 FAR_LAG = 3
@@ -91,20 +92,6 @@
         sums[index] = jnp.where(first, 0.0, sums[index]) + parts[index]
 
 
-def channel_sum(plain):
-    width = plain.shape[-1]
-    return jnp.sum(plain[...].reshape(BANDS * BLOCK // 8, 8, width), axis=0)
-
-
-def pool_term(channels, pooling):
-    total = channels[0]
-    for item in channels[1:]:
-        total = total + item
-    mean = jnp.sum(total, axis=0, keepdims=True) * (1.0 / (ROWS * COLS))
-    mean = jnp.broadcast_to(mean, (16, mean.shape[1])).astype(BF16)
-    return jnp.dot(mean, pooling[...], preferred_element_type=F32)
-
-
 def project(sums, weight):
     total = None
     for index in range(4):
@@ -116,55 +103,30 @@
     return total
 
 
-def class_kernel(info, x0, x1, x2, x3, depth, point, branch, weight, out, channel, plain, shifted,
-                 raw, spread, taps, sums):
-    accumulate(sums, pyramid_tile(info, (x0, x1, x2, x3), depth, point, branch, plain, shifted,
-                                  raw, spread, taps))
-    channel[...] = channel_sum(plain)
-
-    @pl.when(pl.program_id(0) == pl.num_programs(0) - 1)
-    def _():
-        out[...] = project(sums, weight)
-
-
-def early_kernel(info, x0, x1, x2, x3, depth, point, branch, pooling, channel0, channel1, channel2,
-                 sums, pool, plain, shifted, raw, spread, taps):
-    accumulate(sums, pyramid_tile(info, (x0, x1, x2, x3), depth, point, branch, plain, shifted,
-                                  raw, spread, taps))
-    term = pool_term([channel0[...], channel1[...], channel2[...], channel_sum(plain)], pooling)
-
-    @pl.when(pl.program_id(0) == 0)
-    def _():
-        pool[...] = term
-
-    @pl.when(pl.program_id(0) > 0)
-    def _():
-        pool[...] += term
-
-
-def last_kernel(info, x0, x1, x2, x3, depth, point, branch, weight, pooling, channel0, channel1,
-                channel2, sums, pool, pre0, pre1, pre2, refine_depth, refine_point, out, plain,
-                shifted, raw, spread, taps, context, rows):
-    parts = pyramid_tile(info, (x0, x1, x2, x3), depth, point, branch, plain, shifted, raw, spread,
-                         taps)
-    parts = [sums[index] + parts[index] for index in range(4)]
-    term = pool_term([channel0[...], channel1[...], channel2[...], channel_sum(plain)], pooling)
-    vector = jnp.maximum(pool[...] + term, 0.0).astype(BF16)
-    bias = jnp.dot(vector, weight[4 * HALF:5 * HALF, :], preferred_element_type=F32)[0:1, :]
+def context_of(sums, weight, bias):
+    return jnp.maximum(project(sums, weight) + bias[...], 0.0).astype(BF16)
+
+
+def place(context, info, index, value):
+    first = CLASS_ROWS * jnp.bitwise_xor(info[1], ORDER[index])
+    value = value.astype(F32).reshape(BANDS, CLASS_ROWS, COLS, HALF)
+    for band in range(BANDS):
+        for row in range(CLASS_ROWS):
+            context[RATE * band + first + row + 1] = value[band, row]
+
+
+def refine(info, context, rows, refine_depth, refine_point, out, first, count):
+    start = CLASS_ROWS * jnp.bitwise_xor(info[1], ORDER[3]) + first + ROWS
+    column = lax.broadcasted_iota(jnp.int32, (COLS, HALF), 0)
+    wide = refine_depth[...].astype(F32)
     context[0] = jnp.zeros((COLS, HALF), F32)
     context[ROWS + 1] = jnp.zeros((COLS, HALF), F32)
-    pres = (pre0[...], pre1[...], pre2[...], project(parts, weight))
-    for index, pre in enumerate(pres):
-        first = CLASS_ROWS * jnp.bitwise_xor(info[1], ORDER[index])
-        value = jnp.maximum(pre + bias, 0.0).astype(BF16).astype(F32)
-        value = value.reshape(BANDS, CLASS_ROWS, COLS, HALF)
-        for band in range(BANDS):
-            for row in range(CLASS_ROWS):
-                context[RATE * band + first + row + 1] = value[band, row]
-    column = lax.broadcasted_iota(jnp.int32, (COLS, HALF), 0)
-    wide = refine_depth[...].astype(F32)
-
-    def step(row, carry):
+
+    def place_of(index):
+        return (start + RATE * (index // count) + index % count) % ROWS
+
+    def step(index, carry):
+        row = place_of(index)
         lines = [context[row + up] for up in range(3)]
         sides = []
         for side in range(3):
@@ -176,12 +138,60 @@
         left = jnp.where(column == 0, 0.0, pltpu.roll(sides[0], 1, 0))
         right = jnp.where(column == COLS - 1, 0.0, pltpu.roll(sides[2], COLS - 1, 0))
         total = jnp.maximum(sides[1] + left + right, 0.0).astype(BF16)
-        rows[pl.ds(pl.multiple_of(row * COLS, COLS), COLS), :] = total
+        rows[pl.ds(pl.multiple_of(index * COLS, COLS), COLS), :] = total
         return carry
 
-    lax.fori_loop(0, ROWS, step, 0, unroll=4)
+    lax.fori_loop(0, BANDS * count, step, 0, unroll=4)
     product = jnp.dot(rows[...], refine_point[...], preferred_element_type=F32)
-    out[...] = jnp.maximum(product, 0.0).astype(BF16)
+    product = jnp.maximum(product, 0.0).astype(BF16)
+    for index in range(BANDS * count):
+        place = pl.multiple_of(place_of(index) * COLS, COLS)
+        out[pl.ds(place, COLS), :] = product[index * COLS:(index + 1) * COLS, :]
+
+
+def class_kernel(info, x0, x1, x2, x3, depth, point, branch, weight, bias, out, plain, shifted,
+                 raw, spread, taps, sums):
+    accumulate(sums, pyramid_tile(info, (x0, x1, x2, x3), depth, point, branch, plain, shifted,
+                                  raw, spread, taps))
+
+    @pl.when(pl.program_id(0) == pl.num_programs(0) - 1)
+    def _():
+        out[...] = context_of(sums, weight, bias)
+
+
+def third_kernel(info, x0, x1, x2, x3, depth, point, branch, weight, bias, context0, context1,
+                 refine_depth, refine_point, out, ready, plain, shifted, raw, spread, taps, sums,
+                 context, rows):
+    accumulate(sums, pyramid_tile(info, (x0, x1, x2, x3), depth, point, branch, plain, shifted,
+                                  raw, spread, taps))
+
+    @pl.when(pl.program_id(0) == pl.num_programs(0) - 1)
+    def _():
+        value = context_of(sums, weight, bias)
+        out[...] = value
+        place(context, info, 0, context0[...])
+        place(context, info, 1, context1[...])
+        place(context, info, 2, value)
+        refine(info, context, rows, refine_depth, refine_point, ready, CLASS_ROWS + 1, READY)
+
+
+def early_kernel(info, x0, x1, x2, x3, depth, point, branch, sums, plain, shifted, raw, spread,
+                 taps):
+    accumulate(sums, pyramid_tile(info, (x0, x1, x2, x3), depth, point, branch, plain, shifted,
+                                  raw, spread, taps))
+
+
+def last_kernel(info, x0, x1, x2, x3, depth, point, branch, weight, bias, sums, context1, context2,
+                refine_depth, refine_point, ready, out, plain, shifted, raw, spread, taps, context,
+                rows):
+    parts = pyramid_tile(info, (x0, x1, x2, x3), depth, point, branch, plain, shifted, raw, spread,
+                         taps)
+    parts = [sums[index] + parts[index] for index in range(4)]
+    place(context, info, 1, context1[...])
+    place(context, info, 2, context2[...])
+    place(context, info, 3, context_of(parts, weight, bias))
+    out[...] = ready[...]
+    refine(info, context, rows, refine_depth, refine_point, out, -1, RATE - READY)
 
 
 def whole(shape):
@@ -201,12 +211,6 @@
     return specs
 
 
-def channel_specs(start):
-    offset = start // TILE
-    specs = [pl.BlockSpec((TILE, HALF), lambda i, info: (offset + i, 0))]
-    return specs + [pl.BlockSpec((8, TILE), lambda i, info: (0, offset + i)) for _ in range(3)]
-
-
 def pyramid_scratch():
     return [
         pltpu.VMEM((BANDS, CLASS_ROWS, COLS, TILE), F32),
@@ -222,73 +226,33 @@
 )
 
 
-def class_call(info, blocks, depth, point, branch, weight):
-    channels = depth.shape[2]
+SUMS = (4, BANDS * BLOCK, HALF)
+CONTEXT = (BANDS * BLOCK, HALF)
+IMAGE = (ROWS * COLS, HALF)
+
+
+def context_scratch(count):
+    return [
+        pltpu.VMEM((ROWS + 2, COLS, HALF), F32),
+        pltpu.VMEM((BANDS * count * COLS, HALF), BF16),
+    ]
+
+
+def call(kernel, name, info, blocks, weights, start, channels, extra, outs, scratch):
+    specs = pyramid_specs(blocks, start, channels) + [whole(item.shape) for item in extra]
     return pl.pallas_call(
-        class_kernel,
+        kernel,
         grid_spec=pltpu.PrefetchScalarGridSpec(
             num_scalar_prefetch=1,
             grid=(channels // TILE,),
-            in_specs=pyramid_specs(blocks, 0, channels) + [whole((5 * HALF, HALF))],
-            out_specs=[
-                whole((BANDS * BLOCK, HALF)),
-                pl.BlockSpec((8, TILE), lambda i, info: (0, i)),
-            ],
-            scratch_shapes=pyramid_scratch() + [pltpu.VMEM((4, BANDS * BLOCK, HALF), F32)],
+            in_specs=specs,
+            out_specs=[whole(item.shape) for item in outs],
+            scratch_shapes=pyramid_scratch() + scratch,
         ),
-        out_shape=[
-            jax.ShapeDtypeStruct((BANDS * BLOCK, HALF), F32),
-            jax.ShapeDtypeStruct((8, channels), F32),
-        ],
+        out_shape=outs,
         compiler_params=PARAMS,
-        name="pyramid_class",
-    )(info, *blocks, depth, point, branch, weight)
-
-
-def early_call(info, blocks, depth, point, branch, pooling, channel):
-    channels = depth.shape[2] - LATE
-    return pl.pallas_call(
-        early_kernel,
-        grid_spec=pltpu.PrefetchScalarGridSpec(
-            num_scalar_prefetch=1,
-            grid=(channels // TILE,),
-            in_specs=pyramid_specs(blocks, 0, channels) + channel_specs(0),
-            out_specs=[whole((4, BANDS * BLOCK, HALF)), whole((16, HALF))],
-            scratch_shapes=pyramid_scratch(),
-        ),
-        out_shape=[
-            jax.ShapeDtypeStruct((4, BANDS * BLOCK, HALF), F32),
-            jax.ShapeDtypeStruct((16, HALF), F32),
-        ],
-        compiler_params=PARAMS,
-        name="pyramid_early",
-    )(info, *blocks, depth, point, branch, pooling, *channel)
-
-
-def last_call(info, blocks, depth, point, branch, weight, pooling, channel, sums, pool, pres,
-              refine_depth, refine_point):
-    start = depth.shape[2] - LATE
-    specs = pyramid_specs(blocks, start, LATE) + [whole((5 * HALF, HALF))] + channel_specs(start)
-    specs += [whole((4, BANDS * BLOCK, HALF)), whole((16, HALF))]
-    specs += [whole((BANDS * BLOCK, HALF)) for _ in range(3)]
-    specs += [whole((9, HALF)), whole((HALF, HALF))]
-    return pl.pallas_call(
-        last_kernel,
-        grid_spec=pltpu.PrefetchScalarGridSpec(
-            num_scalar_prefetch=1,
-            grid=(1,),
-            in_specs=specs,
-            out_specs=whole((ROWS * COLS, HALF)),
-            scratch_shapes=pyramid_scratch() + [
-                pltpu.VMEM((ROWS + 2, COLS, HALF), F32),
-                pltpu.VMEM((ROWS * COLS, HALF), BF16),
-            ],
-        ),
-        out_shape=jax.ShapeDtypeStruct((ROWS * COLS, HALF), BF16),
-        compiler_params=PARAMS,
-        name="pyramid_last",
-    )(info, *blocks, depth, point, branch, weight, pooling, *channel, sums, pool, *pres,
-      refine_depth, refine_point)
+        name=name,
+    )(info, *blocks, *weights, *extra)
 
 
 class Sender:
@@ -335,6 +299,17 @@
             row = jnp.bitwise_xor(self.me % self.sub, piece) * block
             joined = lax.dynamic_update_slice(joined, got[piece].reshape(block, size), (row, 0))
         return joined
+
+
+def pool_bias(features, after, pooling_weight, project_weight):
+    features, _ = lax.optimization_barrier((features, after))
+    cells = features.shape[1] * lax.axis_size("space")
+    total = jnp.sum(features.astype(F32), axis=1)
+    total = lax.psum_scatter(total, "space", scatter_dimension=0, tiled=True)
+    pooled = (total / cells).astype(BF16)
+    vector = jnp.dot(pooled, pooling_weight, preferred_element_type=F32)
+    vector = jnp.maximum(vector, 0.0).astype(BF16)
+    return jnp.dot(vector, project_weight[4 * HALF:], preferred_element_type=F32)
 
 
 def body(
@@ -367,7 +342,12 @@
         send.cut(origin, hop, ORDER[3], early, LATE)
     for hop in NEAR:
         send.cut(origin, hop, ORDER[3], 0, channels)
-    shared = (depth_weights, point_weights, branch_weight)
+    bias = pool_bias(features, send.values[(2 * CLASSES + ORDER[1]) * send.sub, 0], pooling_weight, project_weight)
+    weights = (depth_weights, point_weights, branch_weight)
+    joined = project_weight[:4 * HALF]
+    sums = pltpu.VMEM(SUMS, F32)
+    context = jax.ShapeDtypeStruct(CONTEXT, BF16)
+    image = jax.ShapeDtypeStruct(IMAGE, BF16)
     done = []
     for index in range(3):
         after = [done[index - 2]] if index >= 2 else []
@@ -375,9 +355,14 @@
         for hop in FAR + NEAR:
             blocks[hop] = send.send(hop, ORDER[index], 0, after if hop == FAR[0] else [])
         blocks = [blocks[hop] for hop in range(BANDS)]
-        done.append(class_call(info, blocks, *shared, project_weight))
-    pres = [item[0] for item in done]
-    channel = [item[1] for item in done]
+        if index < 2:
+            done += call(class_kernel, "pyramid_class", info, blocks, weights, 0, channels,
+                         (joined, bias), [context], [sums])
+        else:
+            extra = (joined, bias, done[0], done[1], refine_depth, refine_point)
+            value, ready = call(third_kernel, "pyramid_third", info, blocks, weights, 0, channels,
+                                extra, [context, image], [sums] + context_scratch(READY))
+            done.append(value)
     blocks = {}
     for hop in FAR + NEAR:
         blocks[hop] = send.send(hop, ORDER[3], 0, [done[1]] if hop == FAR[0] else [])
@@ -386,11 +371,11 @@
         late[hop] = send.send(hop, ORDER[3], early, [done[2]] if hop == FAR[1] else [])
     blocks = [blocks[hop] for hop in range(BANDS)]
     late = [late[hop] for hop in range(BANDS)]
-    sums, pool = early_call(info, blocks, *shared, pooling_weight, channel)
-    refined = last_call(
-        info, late, *shared, project_weight, pooling_weight, channel, sums, pool, pres,
-        refine_depth, refine_point
-    )
+    partial, = call(early_kernel, "pyramid_early", info, blocks, weights, 0, early, (),
+                    [jax.ShapeDtypeStruct(SUMS, F32)], [])
+    extra = (joined, bias, partial, done[1], done[2], refine_depth, refine_point, ready)
+    refined, = call(last_kernel, "pyramid_last", info, late, weights, early, LATE, extra, [image],
+                    context_scratch(RATE - READY))
     return lax.all_to_all(refined.reshape(parts, block, HALF), "space", 0, 0, tiled=True)
 
 

time: 266 us -> 354 us (1.33)
  waiting for transfers between devices: 44 us -> 189 us
  starting transfers between devices: 118 us -> 45.2 us
  between operations: 0.14 us -> 13.5 us
    unnamed x0 -> x2, waiting for transfers between devices: none -> 127 us
    ppermute x17, starting transfers between devices: 118 us -> 45.2 us  [send(): lax.ppermute(value, 'space', [(i, i ^ distance) for i in range(self.parts)])]
    ppermute x17, waiting for transfers between devices: 44 us -> 62.1 us  [send(): lax.ppermute(value, 'space', [(i, i ^ distance) for i in range(self.parts)])]
  transfers between devices with their start and end apart: 17 -> 18, of which waited for: 5 -> 8; matrix products, arithmetic and copies ran while one was open for 3% -> 4% of each run, Pallas kernels for 15% -> 12%
where the time goes in v5:
time: 354 us
  waiting for transfers between devices  189 us (53%)
  Pallas kernels  49.4 us (14%)
  starting transfers between devices  45.2 us (13%)
  blocking collectives  34.9 us (10%)
  local copies, waits for them, and re-layouts  16.3 us (5%)
  between operations  13.5 us (4%)
    unnamed x2, waiting for transfers between devices  127 us
    ppermute x17, waiting for transfers between devices, send(): lax.ppermute(value, 'space', [(i, i ^ distance) for i in range(self.parts)])  62.1 us
    pallas_call x5, Pallas kernels, call(): pl.pallas_call(kernel, grid_spec=pltpu.PrefetchScalarGridSpec(num_scalar_...  49.4 us
    ppermute x17, starting transfers between devices, send(): lax.ppermute(value, 'space', [(i, i ^ distance) for i in range(self.parts)])  45.2 us
    all_to_all x1, blocking collectives, body(): lax.all_to_all(refined.reshape(parts, block, HALF), 'space', 0, 0, tiled=...  34.9 us
  transfers between devices with their start and end apart: 18, of which 8 were waited for; matrix products, arithmetic and copies ran while one was open for 4% of the time, Pallas kernels for 12%

profile of v5, /device:TPU:0, one launch (start us, length us, event | category | flops | bytes accessed | tf_op | source)
XLA Modules:
  0.0 353.5 jit_solution(12831751220408686690)
XLA Ops:
  6.5 2.8 constant_dynamic-slice_fusion.14
  9.3 4.0 %collective-permute-start.8 = (bf16[1,144,2048]{2,1,0:T(8,128)(2,1)}, bf16[1,144,2048]{2,1,0:T(8,128)(2,1)}, u32[]{:S(2)}, u32[]{:S(2)}) collective-permute-start(bf16[1,144,2048]{2,1,0:T(8,128)(2,1)} %get-tuple-element.52), channel_id=1, source_target_pairs={{0,8},{1,9},{2,10},{3,11},{4,12},{5,13},{6,14},{7,15},{8,0},{9,1},... | collective-permute-start | bytes 1769480 | tf_op jit(solution)/shard_map/ppermute | solution.py:288
  13.4 6.0 %dynamic-slice_bitcast_fusion = (bf16[144,2048]{1,0:T(8,128)(2,1)S(1)}, bf16[1,144,2048]{2,1,0:T(8,128)(2,1)}, bf16[1,144,2048]{2,1,0:T(8,128)(2,1)}, bf16[1,144...) fusion(bf16[16,144,2048]{2,1,0:T(8,128)(2,1)} %param.8, ...), kind=kLoop, calls=%fused_computation.1 | loop fusion | bytes 12976172 | tf_op jit(solution)/shard_map/reshape | solution.py:296
  21.1 2.8 convert_reduce_fusion
  25.5 2.8 collective-permute-start.5
  30.8 126.5 %all-reduce.3.cloned.1.call-done = f32[16,2048]{1,0:T(8,128)} async-done(((f32[16,2048]{1,0:T(8,128)}), f32[16,2048]{1,0:T(8,128)}) %all-reduce.3.cloned.1.call-update) | async-done | bytes 131088
  165.5 10.0 %pyramid_class.3.context0 = bf16[576,256]{1,0:T(8,128)(2,1)S(1)} custom-call(s32[2]{0:T(128)S(1)} %pad_add_fusion.info, bf16[144,2048]{1,0:T(8,128)(2,1)S(1)} %get-tuple-element.37.x0, bf16[144,2048]{1,0:T(8,128)(2,1)} %bitcast.14.x1, bf16[144,2048]{1,0:T(8,128)(2,1)} %bitcast.15.x2, bf16[144,2048]{1,0:T(8,128)(2,1)} %bitcast.16.x3, ...), custom_call_target="tpu_custom_call" | custom-call | tf_op jit(solution)/shard_map/pyramid_class/pallas_call | solution.py:243
  175.5 2.6 collective-permute-start.14
  178.1 2.9 collective-permute-done.10
  181.0 2.9 collective-permute-start.6
  186.8 8.6 %collective-permute-done.9 = bf16[1,144,2048]{2,1,0:T(8,128)(2,1)} collective-permute-done((bf16[1,144,2048]{2,1,0:T(8,128)(2,1)}, bf16[1,144,2048]{2,1,0:T(8,128)(2,1)}, u32[]{:S(2)}, u32[]{:S(2)}) %collective-permute-start.9) | collective-permute-done | bytes 589856 | tf_op jit(solution)/shard_map/ppermute | solution.py:288
  195.4 3.8 %collective-permute-start.4 = (bf16[1,144,2048]{2,1,0:T(8,128)(2,1)}, bf16[1,144,2048]{2,1,0:T(8,128)(2,1)S(1)}, u32[]{:S(2)}, u32[]{:S(2)}) collective-permute-start(bf16[1,144,2048]{2,1,0:T(8,128)(2,1)} %get-tuple-element.23), channel_id=1, source_target_pairs={{0,6},{1,7},{2,4},{3,5},{4,2},{5,3},{6,0},{7,1},{8,14},{9,15},{10,... | collective-permute-start | bytes 1769480 | tf_op jit(solution)/shard_map/ppermute | solution.py:288
  199.3 9.8 %pyramid_class.2.context1 = bf16[576,256]{1,0:T(8,128)(2,1)S(1)} custom-call(s32[2]{0:T(128)S(1)} %pad_add_fusion.info, bf16[144,2048]{1,0:T(8,128)(2,1)S(1)} %bitcast.32, bf16[144,2048]{1,0:T(8,128)(2,1)} %bitcast.6.x1, bf16[144,2048]{1,0:T(8,128)(2,1)} %bitcast.7.x2, bf16[144,2048]{1,0:T(8,128)(2,1)} %bitcast.8.x3, bf16[3,9,2048]{2,1,0:T(8,128)(2,1)S(1)} %copy.14.depth, ...), custom_call_target="tpu_custom_call" | custom-call | tf_op jit(solution)/shard_map/pyramid_class/pallas_call | solution.py:243
  209.1 5.6 %collective-permute-done.1 = bf16[1,144,2048]{2,1,0:T(8,128)(2,1)} collective-permute-done((bf16[1,144,2048]{2,1,0:T(8,128)(2,1)}, bf16[1,144,2048]{2,1,0:T(8,128)(2,1)}, u32[]{:S(2)}, u32[]{:S(2)}) %collective-permute-start.1) | collective-permute-done | bytes 589856 | tf_op jit(solution)/shard_map/ppermute | solution.py:288
  215.0 25.0 %collective-permute-done.14 = bf16[1,144,2048]{2,1,0:T(8,128)(2,1)} collective-permute-done((bf16[1,144,2048]{2,1,0:T(8,128)(2,1)}, bf16[1,144,2048]{2,1,0:T(8,128)(2,1)}, u32[]{:S(2)}, u32[]{:S(2)}) %collective-permute-start.14) | collective-permute-done | bytes 589856 | tf_op jit(solution)/shard_map/ppermute | solution.py:288
  242.9 7.3 %collective-permute-done.12 = bf16[1,144,2048]{2,1,0:T(8,128)(2,1)S(1)} collective-permute-done((bf16[1,144,2048]{2,1,0:T(8,128)(2,1)}, bf16[1,144,2048]{2,1,0:T(8,128)(2,1)S(1)}, u32[]{:S(2)}, u32[]{:S(2)}) %collective-permute-start.12) | collective-permute-done | bytes 589856 | tf_op jit(solution)/shard_map/ppermute | solution.py:288
  250.2 15.3 %collective-permute-start.7 = (bf16[1,144,512]{2,1,0:T(8,128)(2,1)S(1)}, bf16[1,144,512]{2,1,0:T(8,128)(2,1)S(1)}, u32[]{:S(2)}, u32[]{:S(2)}) collective-permute-start(bf16[1,144,512]{2,1,0:T(8,128)(2,1)S(1)} %get-tuple-element.25), channel_id=1, source_target_pairs={{0,10},{1,11},{2,8},{3,9},{4,14},{5,15},{6,12},{7,13},{8,2},{9,3},... | collective-permute-start | bytes 442376 | tf_op jit(solution)/shard_map/ppermute | solution.py:288
  265.5 12.9 %pyramid_third.1 = (bf16[576,256]{1,0:T(8,128)(2,1)S(1)}, bf16[2304,256]{1,0:T(8,128)(2,1)}) custom-call(s32[2]{0:T(128)S(1)} %pad_add_fusion.info, bf16[144,2048]{1,0:T(8,128)(2,1)} %bitcast.40, bf16[144,2048]{1,0:T(8,128)(2,1)} %bitcast.12.x1, bf16[144,2048]{1,0:T(8,128)(2,1)} %bitcast.17.x2, bf16[144,2048]{1,0:T(8,128)(2,1)} %bitcast.18.x3, ...), custom_call_target="tpu_custom_call" | custom-call | tf_op jit(solution)/shard_map/pyramid_third/pallas_call | solution.py:243
  278.4 9.4 %collective-permute-done.11 = bf16[1,144,1536]{2,1,0:T(8,128)(2,1)S(1)} collective-permute-done((bf16[1,144,1536]{2,1,0:T(8,128)(2,1)S(1)}, bf16[1,144,1536]{2,1,0:T(8,128)(2,1)S(1)}, u32[]{:S(2)}, u32[]{:S(2)}) %collective-permute-start.11) | collective-permute-done | bytes 442400 | tf_op jit(solution)/shard_map/ppermute | solution.py:288
  287.8 2.3 collective-permute-start.15
  290.9 8.8 %pyramid_early.1.sums = f32[4,576,256]{2,1,0:T(8,128)} custom-call(s32[2]{0:T(128)S(1)} %pad_add_fusion.info, bf16[144,2048]{1,0:T(8,128)(2,1)S(1)} %bitcast.30, bf16[144,2048]{1,0:T(8,128)(2,1)} %bitcast.38, bf16[144,1536]{1,0:T(8,128)(2,1)S(1)} %bitcast.33, bf16[144,1536]{1,0:T(8,128)(2,1)S(1)} %bitcast.34, bf16[3,9,2048]{2,1,0:T(8,128)(2,1)S(1)} %copy.14.depth, ...), custom_call_target="tpu_custom_call" | custom-call | tf_op jit(solution)/shard_map/pyramid_early/pallas_call | solution.py:243
  299.7 3.3 collective-permute-done.7
  302.9 7.9 %pyramid_last.1 = bf16[2304,256]{1,0:T(8,128)(2,1)} custom-call(s32[2]{0:T(128)S(1)} %pad_add_fusion.info, bf16[144,2048]{1,0:T(8,128)(2,1)} %bitcast.31, bf16[144,2048]{1,0:T(8,128)(2,1)} %bitcast.39, bf16[144,512]{1,0:T(8,128)(2,1)S(1)} %bitcast.35, bf16[144,512]{1,0:T(8,128)(2,1)S(1)} %bitcast.36, bf16[3,9,2048]{2,1,0:T(8,128)(2,1)S(1)} %copy.14.depth, ...), custom_call_target="tpu_custom_call" | custom-call | tf_op jit(solution)/shard_map/pyramid_last/pallas_call | solution.py:243
  310.8 34.9 %all_to_all.5 = bf16[16,144,256]{2,1,0:T(8,128)(2,1)S(1)} all-to-all(bf16[16,144,256]{2,1,0:T(8,128)(2,1)} %bitcast.37), channel_id=1, replica_groups=mesh['dp'=2,'space'=16] {'space'}, dimensions={0} | all-to-all | bytes 2359296 | tf_op jit(solution)/shard_map/all_to_all | solution.py:379
  (51 shorter events, 21.8 us)
Async XLA Ops:
  6.5 150.8 %copy-start = (bf16[2048,256]{1,0:T(8,128)(2,1)S(1)}, bf16[2048,256]{1,0:T(8,128)(2,1)}, u32[]{:S(2)}) copy-start(bf16[2048,256]{1,0:T(8,128)(2,1)} %param.12) | copy-start | bytes 3145732
  6.5 150.8 %all-reduce.3.cloned.1.call-start = ((), (), s32[]{:S(2)}) async-start(), calls=%async_computation.1 | async-start | bytes 262144
  9.3 149.8 %collective-permute-start.8 = (bf16[1,144,2048]{2,1,0:T(8,128)(2,1)}, bf16[1,144,2048]{2,1,0:T(8,128)(2,1)}, u32[]{:S(2)}, u32[]{:S(2)}) collective-permute-start(bf16[1,144,2048]{2,1,0:T(8,128)(2,1)} %get-tuple-element.52), channel_id=1, source_target_pairs={{0,8},{1,9},{2,10},{3,11},{4,12},{5,13},{6,14},{7,15},{8,0},{9,1},... | collective-permute-start | bytes 1769480 | tf_op jit(solution)/shard_map/ppermute | solution.py:288
  13.3 15.5 %copy-start.7 = (bf16[3,9,2048]{2,0,1:T(4,128)(2,1)S(1)}, bf16[3,9,2048]{2,0,1:T(4,128)(2,1)}, u32[]{:S(2)}) copy-start(bf16[3,9,2048]{2,0,1:T(4,128)(2,1)} %param.9) | copy-start | bytes 331780
  13.4 16.7 %copy-start.8 = (u32[32]{0:T(128)S(1)}, u32[32]{0:T(128)}, u32[]{:S(2)}) copy-start(u32[32]{0:T(128)} %constant.76) | copy-start | bytes 388
  23.9 137.9 %collective-permute-start = (bf16[1,144,2048]{2,1,0:T(8,128)(2,1)}, bf16[1,144,2048]{2,1,0:T(8,128)(2,1)}, u32[]{:S(2)}, u32[]{:S(2)}) collective-permute-start(bf16[1,144,2048]{2,1,0:T(8,128)(2,1)} %get-tuple-element.50), channel_id=1, source_target_pairs={{0,4},{1,5},{2,6},{3,7},{4,0},{5,1},{6,2},{7,3},{8,12},{9,13},{10,... | collective-permute-start | bytes 1769480 | tf_op jit(solution)/shard_map/ppermute | solution.py:288
  25.5 138.4 %collective-permute-start.13 = (bf16[1,144,2048]{2,1,0:T(8,128)(2,1)}, bf16[1,144,2048]{2,1,0:T(8,128)(2,1)}, u32[]{:S(2)}, u32[]{:S(2)}) collective-permute-start(bf16[1,144,2048]{2,1,0:T(8,128)(2,1)} %get-tuple-element.51), channel_id=1, source_target_pairs={{0,12},{1,13},{2,14},{3,15},{4,8},{5,9},{6,10},{7,11},{8,4},{9,5},... | collective-permute-start | bytes 1769480 | tf_op jit(solution)/shard_map/ppermute | solution.py:288
  25.5 150.0 %collective-permute-start.5 = (bf16[1,144,2048]{2,1,0:T(8,128)(2,1)}, bf16[1,144,2048]{2,1,0:T(8,128)(2,1)}, u32[]{:S(2)}, u32[]{:S(2)}) collective-permute-start(bf16[1,144,2048]{2,1,0:T(8,128)(2,1)} %get-tuple-element.42), channel_id=1, source_target_pairs={{0,9},{1,8},{2,11},{3,10},{4,13},{5,12},{6,15},{7,14},{8,1},{9,0},... | collective-permute-start | bytes 1769480 | tf_op jit(solution)/shard_map/ppermute | solution.py:288
  28.3 155.6 %collective-permute-start.3 = (bf16[1,144,2048]{2,1,0:T(8,128)(2,1)}, bf16[1,144,2048]{2,1,0:T(8,128)(2,1)S(1)}, u32[]{:S(2)}, u32[]{:S(2)}) collective-permute-start(bf16[1,144,2048]{2,1,0:T(8,128)(2,1)} %get-tuple-element.44), channel_id=1, source_target_pairs={{0,1},{1,0},{2,3},{3,2},{4,5},{5,4},{6,7},{7,6},{8,9},{9,8},{10,11... | collective-permute-start | bytes 1769480 | tf_op jit(solution)/shard_map/ppermute | solution.py:288
  30.1 235.5 %copy-start.2 = (bf16[256,256]{1,0:T(8,128)(2,1)S(1)}, bf16[256,256]{1,0:T(8,128)(2,1)}, u32[]{:S(2)}) copy-start(bf16[256,256]{1,0:T(8,128)(2,1)} %refine_point.3) | copy-start | bytes 393220
  30.1 235.5 %copy-start.3 = (bf16[9,256]{1,0:T(8,128)(2,1)S(1)}, bf16[9,256]{1,0:T(8,128)(2,1)}, u32[]{:S(2)}) copy-start(bf16[9,256]{1,0:T(8,128)(2,1)} %refine_depth.3) | copy-start | bytes 13828
  159.1 22.0 %collective-permute-start.10 = (bf16[1,144,2048]{2,1,0:T(8,128)(2,1)}, bf16[1,144,2048]{2,1,0:T(8,128)(2,1)}, u32[]{:S(2)}, u32[]{:S(2)}) collective-permute-start(bf16[1,144,2048]{2,1,0:T(8,128)(2,1)} %get-tuple-element.40), channel_id=1, source_target_pairs={{0,5},{1,4},{2,7},{3,6},{4,1},{5,0},{6,3},{7,2},{8,13},{9,12},{10,... | collective-permute-start | bytes 1769480 | tf_op jit(solution)/shard_map/ppermute | solution.py:288
  161.8 33.6 %collective-permute-start.9 = (bf16[1,144,2048]{2,1,0:T(8,128)(2,1)}, bf16[1,144,2048]{2,1,0:T(8,128)(2,1)}, u32[]{:S(2)}, u32[]{:S(2)}) collective-permute-start(bf16[1,144,2048]{2,1,0:T(8,128)(2,1)} %get-tuple-element.26), channel_id=1, source_target_pairs={{0,13},{1,12},{2,15},{3,14},{4,9},{5,8},{6,11},{7,10},{8,5},{9,4},... | collective-permute-start | bytes 1769480 | tf_op jit(solution)/shard_map/ppermute | solution.py:288
  163.9 50.8 %collective-permute-start.1 = (bf16[1,144,2048]{2,1,0:T(8,128)(2,1)}, bf16[1,144,2048]{2,1,0:T(8,128)(2,1)}, u32[]{:S(2)}, u32[]{:S(2)}) collective-permute-start(bf16[1,144,2048]{2,1,0:T(8,128)(2,1)} %get-tuple-element.21), channel_id=1, source_target_pairs={{0,7},{1,6},{2,5},{3,4},{4,3},{5,2},{6,1},{7,0},{8,15},{9,14},{10,... | collective-permute-start | bytes 1769480 | tf_op jit(solution)/shard_map/ppermute | solution.py:288
  175.5 64.5 %collective-permute-start.14 = (bf16[1,144,2048]{2,1,0:T(8,128)(2,1)}, bf16[1,144,2048]{2,1,0:T(8,128)(2,1)}, u32[]{:S(2)}, u32[]{:S(2)}) collective-permute-start(bf16[1,144,2048]{2,1,0:T(8,128)(2,1)} %get-tuple-element.30), channel_id=1, source_target_pairs={{0,11},{1,10},{2,9},{3,8},{4,15},{5,14},{6,13},{7,12},{8,3},{9,2},... | collective-permute-start | bytes 1769480 | tf_op jit(solution)/shard_map/ppermute | solution.py:288
  181.0 59.0 %collective-permute-start.6 = (bf16[1,144,2048]{2,1,0:T(8,128)(2,1)}, bf16[1,144,2048]{2,1,0:T(8,128)(2,1)}, u32[]{:S(2)}, u32[]{:S(2)}) collective-permute-start(bf16[1,144,2048]{2,1,0:T(8,128)(2,1)} %get-tuple-element.24), channel_id=1, source_target_pairs={{0,15},{1,14},{2,13},{3,12},{4,11},{5,10},{6,9},{7,8},{8,7},{9,6},... | collective-permute-start | bytes 1769480 | tf_op jit(solution)/shard_map/ppermute | solution.py:288
  183.9 66.2 %collective-permute-start.12 = (bf16[1,144,2048]{2,1,0:T(8,128)(2,1)}, bf16[1,144,2048]{2,1,0:T(8,128)(2,1)S(1)}, u32[]{:S(2)}, u32[]{:S(2)}) collective-permute-start(bf16[1,144,2048]{2,1,0:T(8,128)(2,1)} %get-tuple-element.29), channel_id=1, source_target_pairs={{0,3},{1,2},{2,1},{3,0},{4,7},{5,6},{6,5},{7,4},{8,11},{9,10},{10,... | collective-permute-start | bytes 1769480 | tf_op jit(solution)/shard_map/ppermute | solution.py:288
  195.4 94.6 %collective-permute-start.4 = (bf16[1,144,2048]{2,1,0:T(8,128)(2,1)}, bf16[1,144,2048]{2,1,0:T(8,128)(2,1)S(1)}, u32[]{:S(2)}, u32[]{:S(2)}) collective-permute-start(bf16[1,144,2048]{2,1,0:T(8,128)(2,1)} %get-tuple-element.23), channel_id=1, source_target_pairs={{0,6},{1,7},{2,4},{3,5},{4,2},{5,3},{6,0},{7,1},{8,14},{9,15},{10,... | collective-permute-start | bytes 1769480 | tf_op jit(solution)/shard_map/ppermute | solution.py:288
  214.7 75.4 %collective-permute-start.2 = (bf16[1,144,2048]{2,1,0:T(8,128)(2,1)}, bf16[1,144,2048]{2,1,0:T(8,128)(2,1)S(1)}, u32[]{:S(2)}, u32[]{:S(2)}) collective-permute-start(bf16[1,144,2048]{2,1,0:T(8,128)(2,1)} %get-tuple-element.22), channel_id=1, source_target_pairs={{0,2},{1,3},{2,0},{3,1},{4,6},{5,7},{6,4},{7,5},{8,10},{9,11},{10,... | collective-permute-start | bytes 1769480 | tf_op jit(solution)/shard_map/ppermute | solution.py:288
  240.0 47.8 %collective-permute-start.11 = (bf16[1,144,1536]{2,1,0:T(8,128)(2,1)S(1)}, bf16[1,144,1536]{2,1,0:T(8,128)(2,1)S(1)}, u32[]{:S(2)}, u32[]{:S(2)}) collective-permute-start(bf16[1,144,1536]{2,1,0:T(8,128)(2,1)S(1)} %get-tuple-element.28), channel_id=1, source_target_pairs={{0,10},{1,11},{2,8},{3,9},{4,14},{5,15},{6,12},{7,13},{8,2},{9,3},... | collective-permute-start | bytes 1327112 | tf_op jit(solution)/shard_map/ppermute | solution.py:288
  240.0 50.0 %collective-permute-start.16 = (bf16[1,144,1536]{2,1,0:T(8,128)(2,1)S(1)}, bf16[1,144,1536]{2,1,0:T(8,128)(2,1)S(1)}, u32[]{:S(2)}, u32[]{:S(2)}) collective-permute-start(bf16[1,144,1536]{2,1,0:T(8,128)(2,1)S(1)} %get-tuple-element.33), channel_id=1, source_target_pairs={{0,14},{1,15},{2,12},{3,13},{4,10},{5,11},{6,8},{7,9},{8,6},{9,7},... | collective-permute-start | bytes 1327112 | tf_op jit(solution)/shard_map/ppermute | solution.py:288
  250.2 15.3 %copy-start.6 = (bf16[1,144,2048]{2,1,0:T(8,128)(2,1)}, bf16[1,144,2048]{2,1,0:T(8,128)(2,1)S(1)}, u32[]{:S(2)}) copy-start(bf16[1,144,2048]{2,1,0:T(8,128)(2,1)S(1)} %collective-permute-done.12) | copy-start | bytes 1769476
  250.2 52.7 %collective-permute-start.7 = (bf16[1,144,512]{2,1,0:T(8,128)(2,1)S(1)}, bf16[1,144,512]{2,1,0:T(8,128)(2,1)S(1)}, u32[]{:S(2)}, u32[]{:S(2)}) collective-permute-start(bf16[1,144,512]{2,1,0:T(8,128)(2,1)S(1)} %get-tuple-element.25), channel_id=1, source_target_pairs={{0,10},{1,11},{2,8},{3,9},{4,14},{5,15},{6,12},{7,13},{8,2},{9,3},... | collective-permute-start | bytes 442376 | tf_op jit(solution)/shard_map/ppermute | solution.py:288
  287.8 15.2 %collective-permute-start.15 = (bf16[1,144,512]{2,1,0:T(8,128)(2,1)S(1)}, bf16[1,144,512]{2,1,0:T(8,128)(2,1)S(1)}, u32[]{:S(2)}, u32[]{:S(2)}) collective-permute-start(bf16[1,144,512]{2,1,0:T(8,128)(2,1)S(1)} %get-tuple-element.32), channel_id=1, source_target_pairs={{0,14},{1,15},{2,12},{3,13},{4,10},{5,11},{6,8},{7,9},{8,6},{9,7},... | collective-permute-start | bytes 442376 | tf_op jit(solution)/shard_map/ppermute | solution.py:288
  (3 other events, 21.4 us)
Sparse Core Ops, SparseCore 0:
  24.0 133.2 all-reduce.2

commit v6 on v4

--- a/solution.py
+++ b/solution.py
@@ -19,7 +19,7 @@
 NEAR = (1, 0)
 FAR = (2, 3)
 FAR_LAG = 3
-NEAR_LAG = 3
+NEAR_LAG = 2
 F32 = jnp.float32
 BF16 = jnp.bfloat16
 
@@ -380,7 +380,7 @@
     channel = [item[1] for item in done]
     blocks = {}
     for hop in FAR + NEAR:
-        blocks[hop] = send.send(hop, ORDER[3], 0, [done[1]] if hop == FAR[0] else [])
+        blocks[hop] = send.send(hop, ORDER[3], 0, [done[1]] if hop == FAR[1] else [])
     late = dict(blocks)
     for hop in FAR:
         late[hop] = send.send(hop, ORDER[3], early, [done[2]] if hop == FAR[1] else [])

time: 266 us -> 259 us (0.974)
  starting transfers between devices: 118 us -> 95.7 us
  waiting for transfers between devices: 44 us -> 64 us
  blocking collectives: 37.5 us -> 33 us
    ppermute x17, starting transfers between devices: 118 us -> 95.7 us  [send(): lax.ppermute(value, 'space', [(i, i ^ distance) for i in range(self.parts)])]
    ppermute x17, waiting for transfers between devices: 44 us -> 64 us  [send(): lax.ppermute(value, 'space', [(i, i ^ distance) for i in range(self.parts)])]
    all_to_all x1, blocking collectives: 37.5 us -> 33 us  [body(): lax.all_to_all(refined.reshape(parts, block, HALF), 'space', 0, 0, tiled=...]
    unnamed x22 -> x26, local copies, waits for them, and re-layouts: 6.26 us -> 6.24 us
where the time goes in v6:
time: 259 us; the launch traced here: 258 us
  starting transfers between devices  95.7 us (37%)
  waiting for transfers between devices  64 us (25%)
  Pallas kernels  49.3 us (19%)
  blocking collectives  33 us (13%)
  local copies, waits for them, and re-layouts  16.1 us (6%)
    ppermute x17, starting transfers between devices, send(): lax.ppermute(value, 'space', [(i, i ^ distance) for i in range(self.parts)])  95.7 us
    ppermute x17, waiting for transfers between devices, send(): lax.ppermute(value, 'space', [(i, i ^ distance) for i in range(self.parts)])  64 us
    all_to_all x1, blocking collectives, body(): lax.all_to_all(refined.reshape(parts, block, HALF), 'space', 0, 0, tiled=...  33 us
    pallas_call x3, Pallas kernels, class_call(): pl.pallas_call(class_kernel, grid_spec=pltpu.PrefetchScalarGridSpec(num_s...  30.3 us
    pallas_call x1, Pallas kernels, last_call(): pl.pallas_call(last_kernel, grid_spec=pltpu.PrefetchScalarGridSpec(num_sc...  9.91 us
    pallas_call x1, Pallas kernels, early_call(): pl.pallas_call(early_kernel, grid_spec=pltpu.PrefetchScalarGridSpec(num_s...  9.06 us
    unnamed x26, local copies, waits for them, and re-layouts  6.24 us
  transfers between devices with their start and end apart: 17, of which 5 were waited for; matrix products, arithmetic and copies ran while one was open for 3% of the time, Pallas kernels for 15%

profile of v6, /device:TPU:0, one launch (start us, length us, event | category | flops | bytes accessed | tf_op | source)
XLA Modules:
  0.0 258.4 jit_solution(6081663438849226885)
XLA Ops:
  0.0 2.7 %constant_dynamic-slice_fusion.14 = (bf16[1,144,2048]{2,1,0:T(8,128)(2,1)}, bf16[1,144,2048]{2,1,0:T(8,128)(2,1)}, bf16[1,144,2048]{2,1,0:T(8,128)(2,1)}) fusion(bf16[16,144,2048]{2,1,0:T(8,128)(2,1)} %param.8, s32[]{:T(128)S(6)} %select_n.66, s32[]{:T(128)S(6)} %select_n.65, s32[]{:T(128)S(6)} %select_n.64), kind=kLoop, calls=%fused_computation.15 | loop fusion | bytes 3538956 | tf_op jit(solution)/shard_map/dynamic_slice | solution.py:308
  2.7 3.0 %collective-permute-start = (bf16[1,144,2048]{2,1,0:T(8,128)(2,1)}, bf16[1,144,2048]{2,1,0:T(8,128)(2,1)S(1)}, u32[]{:S(2)}, u32[]{:S(2)}) collective-permute-start(bf16[1,144,2048]{2,1,0:T(8,128)(2,1)} %get-tuple-element.62), channel_id=1, source_target_pairs={{0,4},{1,5},{2,6},{3,7},{4,0},{5,1},{6,2},{7,3},{8,12},{9,13},{10,... | collective-permute-start | bytes 1769480 | tf_op jit(solution)/shard_map/ppermute | solution.py:324
  5.7 2.6 %collective-permute-start.10 = (bf16[1,144,2048]{2,1,0:T(8,128)(2,1)}, bf16[1,144,2048]{2,1,0:T(8,128)(2,1)}, u32[]{:S(2)}, u32[]{:S(2)}) collective-permute-start(bf16[1,144,2048]{2,1,0:T(8,128)(2,1)} %get-tuple-element.64), channel_id=1, source_target_pairs={{0,8},{1,9},{2,10},{3,11},{4,12},{5,13},{6,14},{7,15},{8,0},{9,1},... | collective-permute-start | bytes 1769480 | tf_op jit(solution)/shard_map/ppermute | solution.py:324
  8.3 5.0 %dynamic-slice_bitcast_fusion = (bf16[144,2048]{1,0:T(8,128)(2,1)S(1)}, bf16[1,144,2048]{2,1,0:T(8,128)(2,1)}, bf16[1,144,2048]{2,1,0:T(8,128)(2,1)}, bf16[1,144...) fusion(bf16[16,144,2048]{2,1,0:T(8,128)(2,1)} %param.8, ...), kind=kLoop, calls=%fused_computation | loop fusion | bytes 12976172 | tf_op jit(solution)/shard_map/reshape | solution.py:332
  14.7 17.9 %collective-permute-done = bf16[1,144,2048]{2,1,0:T(8,128)(2,1)S(1)} collective-permute-done((bf16[1,144,2048]{2,1,0:T(8,128)(2,1)}, bf16[1,144,2048]{2,1,0:T(8,128)(2,1)S(1)}, u32[]{:S(2)}, u32[]{:S(2)}) %collective-permute-start) | collective-permute-done | bytes 589856 | tf_op jit(solution)/shard_map/ppermute | solution.py:324
  35.4 3.5 %collective-permute-start.13 = (bf16[1,144,2048]{2,1,0:T(8,128)(2,1)}, bf16[1,144,2048]{2,1,0:T(8,128)(2,1)}, u32[]{:S(2)}, u32[]{:S(2)}) collective-permute-start(bf16[1,144,2048]{2,1,0:T(8,128)(2,1)} %get-tuple-element.63), channel_id=1, source_target_pairs={{0,12},{1,13},{2,14},{3,15},{4,8},{5,9},{6,10},{7,11},{8,4},{9,5},... | collective-permute-start | bytes 1769480 | tf_op jit(solution)/shard_map/ppermute | solution.py:324
  40.5 5.5 %collective-permute-done.4 = bf16[1,144,2048]{2,1,0:T(8,128)(2,1)S(1)} collective-permute-done((bf16[1,144,2048]{2,1,0:T(8,128)(2,1)S(1)}, bf16[1,144,2048]{2,1,0:T(8,128)(2,1)S(1)}, u32[]{:S(2)}, u32[]{:S(2)}) %collective-permute-start.4) | collective-permute-done | bytes 589856 | tf_op jit(solution)/shard_map/ppermute | solution.py:324
  46.1 3.3 %collective-permute-start.5 = (bf16[1,144,2048]{2,1,0:T(8,128)(2,1)}, bf16[1,144,2048]{2,1,0:T(8,128)(2,1)}, u32[]{:S(2)}, u32[]{:S(2)}) collective-permute-start(bf16[1,144,2048]{2,1,0:T(8,128)(2,1)} %get-tuple-element.30), channel_id=1, source_target_pairs={{0,7},{1,6},{2,5},{3,4},{4,3},{5,2},{6,1},{7,0},{8,15},{9,14},{10,... | collective-permute-start | bytes 1769480 | tf_op jit(solution)/shard_map/ppermute | solution.py:324
  49.4 10.4 %collective-permute-done.1 = bf16[1,144,2048]{2,1,0:T(8,128)(2,1)S(1)} collective-permute-done((bf16[1,144,2048]{2,1,0:T(8,128)(2,1)S(1)}, bf16[1,144,2048]{2,1,0:T(8,128)(2,1)S(1)}, u32[]{:S(2)}, u32[]{:S(2)}) %collective-permute-start.1) | collective-permute-done | bytes 589856 | tf_op jit(solution)/shard_map/ppermute | solution.py:324
  61.9 10.1 %pyramid_class.3 = (f32[576,256]{1,0:T(8,128)S(1)}, f32[8,2048]{1,0:T(8,128)S(1)}) custom-call(s32[2]{0:T(128)S(1)} %pad_add_fusion.info, bf16[144,2048]{1,0:T(8,128)(2,1)S(1)} %get-tuple-element.49.x0, bf16[144,2048]{1,0:T(8,128)(2,1)} %bitcast.33, bf16[144,2048]{1,0:T(8,128)(2,1)} %bitcast.9.x2, bf16[144,2048]{1,0:T(8,128)(2,1)} %bitcast.10.x3, ...), custom_call_target="tpu_custom_call" | custom-call | tf_op jit(solution)/shard_map/pyramid_class/pallas_call | solution.py:227
  72.8 30.3 %collective-permute-start.14 = (bf16[1,144,2048]{2,1,0:T(8,128)(2,1)}, bf16[1,144,2048]{2,1,0:T(8,128)(2,1)S(1)}, u32[]{:S(2)}, u32[]{:S(2)}) collective-permute-start(bf16[1,144,2048]{2,1,0:T(8,128)(2,1)} %get-tuple-element.38), channel_id=1, source_target_pairs={{0,11},{1,10},{2,9},{3,8},{4,15},{5,14},{6,13},{7,12},{8,3},{9,2},... | collective-permute-start | bytes 1769480 | tf_op jit(solution)/shard_map/ppermute | solution.py:324
  103.1 17.9 %collective-permute-done.7 = bf16[1,144,2048]{2,1,0:T(8,128)(2,1)} collective-permute-done((bf16[1,144,2048]{2,1,0:T(8,128)(2,1)}, bf16[1,144,2048]{2,1,0:T(8,128)(2,1)}, u32[]{:S(2)}, u32[]{:S(2)}) %collective-permute-start.7) | collective-permute-done | bytes 589856 | tf_op jit(solution)/shard_map/ppermute | solution.py:324
  121.0 6.0 %collective-permute-start.8 = (bf16[1,144,2048]{2,1,0:T(8,128)(2,1)}, bf16[1,144,2048]{2,1,0:T(8,128)(2,1)S(1)}, u32[]{:S(2)}, u32[]{:S(2)}) collective-permute-start(bf16[1,144,2048]{2,1,0:T(8,128)(2,1)} %get-tuple-element.32), channel_id=1, source_target_pairs={{0,15},{1,14},{2,13},{3,12},{4,11},{5,10},{6,9},{7,8},{8,7},{9,6},... | collective-permute-start | bytes 1769480 | tf_op jit(solution)/shard_map/ppermute | solution.py:324
  128.3 14.0 %collective-permute-start.6 = (bf16[1,144,2048]{2,1,0:T(8,128)(2,1)S(1)}, bf16[1,144,2048]{2,1,0:T(8,128)(2,1)S(1)}, u32[]{:S(2)}, u32[]{:S(2)}) collective-permute-start(bf16[1,144,2048]{2,1,0:T(8,128)(2,1)S(1)} %get-tuple-element.31), channel_id=1, source_target_pairs={{0,6},{1,7},{2,4},{3,5},{4,2},{5,3},{6,0},{7,1},{8,14},{9,15},{10,... | collective-permute-start | bytes 1769480 | tf_op jit(solution)/shard_map/ppermute | solution.py:324
  142.4 2.5 collective-permute-start.12
  144.9 10.1 %pyramid_class.5 = (f32[576,256]{1,0:T(8,128)S(1)}, f32[8,2048]{1,0:T(8,128)S(1)}) custom-call(s32[2]{0:T(128)S(1)} %pad_add_fusion.info, bf16[144,2048]{1,0:T(8,128)(2,1)S(1)} %bitcast.26, bf16[144,2048]{1,0:T(8,128)(2,1)} %bitcast.34, bf16[144,2048]{1,0:T(8,128)(2,1)} %bitcast.16.x2, bf16[144,2048]{1,0:T(8,128)(2,1)} %bitcast.17.x3, ...), custom_call_target="tpu_custom_call" | custom-call | tf_op jit(solution)/shard_map/pyramid_class/pallas_call | solution.py:227
  155.8 12.1 %collective-permute-done.14 = bf16[1,144,2048]{2,1,0:T(8,128)(2,1)S(1)} collective-permute-done((bf16[1,144,2048]{2,1,0:T(8,128)(2,1)}, bf16[1,144,2048]{2,1,0:T(8,128)(2,1)S(1)}, u32[]{:S(2)}, u32[]{:S(2)}) %collective-permute-start.14) | collective-permute-done | bytes 589856 | tf_op jit(solution)/shard_map/ppermute | solution.py:324
  168.0 4.0 %collective-permute-start.16 = (bf16[1,144,1536]{2,1,0:T(8,128)(2,1)S(1)}, bf16[1,144,1536]{2,1,0:T(8,128)(2,1)S(1)}, u32[]{:S(2)}, u32[]{:S(2)}) collective-permute-start(bf16[1,144,1536]{2,1,0:T(8,128)(2,1)S(1)} %get-tuple-element.44), channel_id=1, source_target_pairs={{0,14},{1,15},{2,12},{3,13},{4,10},{5,11},{6,8},{7,9},{8,6},{9,7},... | collective-permute-start | bytes 1327112 | tf_op jit(solution)/shard_map/ppermute | solution.py:324
  173.0 17.0 %collective-permute-start.9 = (bf16[1,144,512]{2,1,0:T(8,128)(2,1)S(1)}, bf16[1,144,512]{2,1,0:T(8,128)(2,1)S(1)}, u32[]{:S(2)}, u32[]{:S(2)}) collective-permute-start(bf16[1,144,512]{2,1,0:T(8,128)(2,1)S(1)} %get-tuple-element.33), channel_id=1, source_target_pairs={{0,10},{1,11},{2,8},{3,9},{4,14},{5,15},{6,12},{7,13},{8,2},{9,3},... | collective-permute-start | bytes 442376 | tf_op jit(solution)/shard_map/ppermute | solution.py:324
  190.0 10.1 %pyramid_class.4 = (f32[576,256]{1,0:T(8,128)S(1)}, f32[8,2048]{1,0:T(8,128)S(1)}) custom-call(s32[2]{0:T(128)S(1)} %pad_add_fusion.info, bf16[144,2048]{1,0:T(8,128)(2,1)S(1)} %bitcast.27, bf16[144,2048]{1,0:T(8,128)(2,1)} %bitcast.6.x1, bf16[144,2048]{1,0:T(8,128)(2,1)} %bitcast.35, bf16[144,2048]{1,0:T(8,128)(2,1)} %bitcast.36, ...), custom_call_target="tpu_custom_call" | custom-call | tf_op jit(solution)/shard_map/pyramid_class/pallas_call | solution.py:227
  201.0 2.5 collective-permute-start.15
  204.3 9.1 %pyramid_early.1 = (f32[4,576,256]{2,1,0:T(8,128)}, f32[16,256]{1,0:T(8,128)S(1)}) custom-call(s32[2]{0:T(128)S(1)} %pad_add_fusion.info, bf16[144,2048]{1,0:T(8,128)(2,1)S(1)} %bitcast.24, bf16[144,2048]{1,0:T(8,128)(2,1)} %bitcast.22, bf16[144,1536]{1,0:T(8,128)(2,1)S(1)} %bitcast.28, bf16[144,1536]{1,0:T(8,128)(2,1)S(1)} %bitcast.29, ...), custom_call_target="tpu_custom_call" | custom-call | tf_op jit(solution)/shard_map/pyramid_early/pallas_call | solution.py:250
  214.4 9.9 %pyramid_last.1 = bf16[2304,256]{1,0:T(8,128)(2,1)} custom-call(s32[2]{0:T(128)S(1)} %pad_add_fusion.info, bf16[144,2048]{1,0:T(8,128)(2,1)S(1)} %bitcast.25, bf16[144,2048]{1,0:T(8,128)(2,1)S(1)} %bitcast.23, bf16[144,512]{1,0:T(8,128)(2,1)S(1)} %bitcast.30, bf16[144,512]{1,0:T(8,128)(2,1)S(1)} %bitcast.31, bf16[3,9,2048]{2,1,0:T(8,128)(2,1)S(1)} %copy.9.depth, ...), custom_call_target="tpu_custom_call" | custom-call | tf_op jit(solution)/shard_map/pyramid_last/pallas_call | solution.py:275
  224.3 33.0 %all_to_all.5 = bf16[16,144,256]{2,1,0:T(8,128)(2,1)S(1)} all-to-all(bf16[16,144,256]{2,1,0:T(8,128)(2,1)} %bitcast.32), channel_id=1, replica_groups=mesh['dp'=2,'space'=16] {'space'}, dimensions={0} | all-to-all | bytes 2359296 | tf_op jit(solution)/shard_map/all_to_all | solution.py:394
  (47 shorter events, 15.6 us)
Async XLA Ops:
  0.0 61.7 %copy-start.11 = (bf16[3,9,2048]{2,0,1:T(4,128)(2,1)S(1)}, bf16[3,9,2048]{2,0,1:T(4,128)(2,1)}, u32[]{:S(2)}) copy-start(bf16[3,9,2048]{2,0,1:T(4,128)(2,1)} %param.9) | copy-start | bytes 331780
  2.7 29.9 %collective-permute-start = (bf16[1,144,2048]{2,1,0:T(8,128)(2,1)}, bf16[1,144,2048]{2,1,0:T(8,128)(2,1)S(1)}, u32[]{:S(2)}, u32[]{:S(2)}) collective-permute-start(bf16[1,144,2048]{2,1,0:T(8,128)(2,1)} %get-tuple-element.62), channel_id=1, source_target_pairs={{0,4},{1,5},{2,6},{3,7},{4,0},{5,1},{6,2},{7,3},{8,12},{9,13},{10,... | collective-permute-start | bytes 1769480 | tf_op jit(solution)/shard_map/ppermute | solution.py:324
  5.7 33.2 %collective-permute-start.10 = (bf16[1,144,2048]{2,1,0:T(8,128)(2,1)}, bf16[1,144,2048]{2,1,0:T(8,128)(2,1)}, u32[]{:S(2)}, u32[]{:S(2)}) collective-permute-start(bf16[1,144,2048]{2,1,0:T(8,128)(2,1)} %get-tuple-element.64), channel_id=1, source_target_pairs={{0,8},{1,9},{2,10},{3,11},{4,12},{5,13},{6,14},{7,15},{8,0},{9,1},... | collective-permute-start | bytes 1769480 | tf_op jit(solution)/shard_map/ppermute | solution.py:324
  13.3 32.8 %collective-permute-start.4 = (bf16[1,144,2048]{2,1,0:T(8,128)(2,1)S(1)}, bf16[1,144,2048]{2,1,0:T(8,128)(2,1)S(1)}, u32[]{:S(2)}, u32[]{:S(2)}) collective-permute-start(bf16[1,144,2048]{2,1,0:T(8,128)(2,1)S(1)} %get-tuple-element.54), channel_id=1, source_target_pairs={{0,5},{1,4},{2,7},{3,6},{4,1},{5,0},{6,3},{7,2},{8,13},{9,12},{10,... | collective-permute-start | bytes 1769480 | tf_op jit(solution)/shard_map/ppermute | solution.py:324
  33.5 26.3 %collective-permute-start.1 = (bf16[1,144,2048]{2,1,0:T(8,128)(2,1)S(1)}, bf16[1,144,2048]{2,1,0:T(8,128)(2,1)S(1)}, u32[]{:S(2)}, u32[]{:S(2)}) collective-permute-start(bf16[1,144,2048]{2,1,0:T(8,128)(2,1)S(1)} %get-tuple-element.27), channel_id=1, source_target_pairs={{0,1},{1,0},{2,3},{3,2},{4,5},{5,4},{6,7},{7,6},{8,9},{9,8},{10,11... | collective-permute-start | bytes 1769480 | tf_op jit(solution)/shard_map/ppermute | solution.py:324
  35.4 26.5 %collective-permute-start.13 = (bf16[1,144,2048]{2,1,0:T(8,128)(2,1)}, bf16[1,144,2048]{2,1,0:T(8,128)(2,1)}, u32[]{:S(2)}, u32[]{:S(2)}) collective-permute-start(bf16[1,144,2048]{2,1,0:T(8,128)(2,1)} %get-tuple-element.63), channel_id=1, source_target_pairs={{0,12},{1,13},{2,14},{3,15},{4,8},{5,9},{6,10},{7,11},{8,4},{9,5},... | collective-permute-start | bytes 1769480 | tf_op jit(solution)/shard_map/ppermute | solution.py:324
  39.0 82.1 %collective-permute-start.7 = (bf16[1,144,2048]{2,1,0:T(8,128)(2,1)}, bf16[1,144,2048]{2,1,0:T(8,128)(2,1)}, u32[]{:S(2)}, u32[]{:S(2)}) collective-permute-start(bf16[1,144,2048]{2,1,0:T(8,128)(2,1)} %get-tuple-element.52), channel_id=1, source_target_pairs={{0,9},{1,8},{2,11},{3,10},{4,13},{5,12},{6,15},{7,14},{8,1},{9,0},... | collective-permute-start | bytes 1769480 | tf_op jit(solution)/shard_map/ppermute | solution.py:324
  39.0 89.3 %collective-permute-start.11 = (bf16[1,144,2048]{2,1,0:T(8,128)(2,1)}, bf16[1,144,2048]{2,1,0:T(8,128)(2,1)}, u32[]{:S(2)}, u32[]{:S(2)}) collective-permute-start(bf16[1,144,2048]{2,1,0:T(8,128)(2,1)} %get-tuple-element.34), channel_id=1, source_target_pairs={{0,13},{1,12},{2,15},{3,14},{4,9},{5,8},{6,11},{7,10},{8,5},{9,4},... | collective-permute-start | bytes 1769480 | tf_op jit(solution)/shard_map/ppermute | solution.py:324
  46.1 13.7 %copy-start.8 = (bf16[1,144,2048]{2,1,0:T(8,128)(2,1)}, bf16[1,144,2048]{2,1,0:T(8,128)(2,1)S(1)}, u32[]{:S(2)}) copy-start(bf16[1,144,2048]{2,1,0:T(8,128)(2,1)S(1)} %collective-permute-done.4) | copy-start | bytes 1769476
  46.1 82.2 %collective-permute-start.5 = (bf16[1,144,2048]{2,1,0:T(8,128)(2,1)}, bf16[1,144,2048]{2,1,0:T(8,128)(2,1)}, u32[]{:S(2)}, u32[]{:S(2)}) collective-permute-start(bf16[1,144,2048]{2,1,0:T(8,128)(2,1)} %get-tuple-element.30), channel_id=1, source_target_pairs={{0,7},{1,6},{2,5},{3,4},{4,3},{5,2},{6,1},{7,0},{8,15},{9,14},{10,... | collective-permute-start | bytes 1769480 | tf_op jit(solution)/shard_map/ppermute | solution.py:324
  59.8 82.5 %collective-permute-start.2 = (bf16[1,144,2048]{2,1,0:T(8,128)(2,1)}, bf16[1,144,2048]{2,1,0:T(8,128)(2,1)S(1)}, u32[]{:S(2)}, u32[]{:S(2)}) collective-permute-start(bf16[1,144,2048]{2,1,0:T(8,128)(2,1)} %get-tuple-element.28), channel_id=1, source_target_pairs={{0,3},{1,2},{2,1},{3,0},{4,7},{5,6},{6,5},{7,4},{8,11},{9,10},{10,... | collective-permute-start | bytes 1769480 | tf_op jit(solution)/shard_map/ppermute | solution.py:324
  72.8 95.2 %collective-permute-start.14 = (bf16[1,144,2048]{2,1,0:T(8,128)(2,1)}, bf16[1,144,2048]{2,1,0:T(8,128)(2,1)S(1)}, u32[]{:S(2)}, u32[]{:S(2)}) collective-permute-start(bf16[1,144,2048]{2,1,0:T(8,128)(2,1)} %get-tuple-element.38), channel_id=1, source_target_pairs={{0,11},{1,10},{2,9},{3,8},{4,15},{5,14},{6,13},{7,12},{8,3},{9,2},... | collective-permute-start | bytes 1769480 | tf_op jit(solution)/shard_map/ppermute | solution.py:324
  121.0 51.9 %collective-permute-start.8 = (bf16[1,144,2048]{2,1,0:T(8,128)(2,1)}, bf16[1,144,2048]{2,1,0:T(8,128)(2,1)S(1)}, u32[]{:S(2)}, u32[]{:S(2)}) collective-permute-start(bf16[1,144,2048]{2,1,0:T(8,128)(2,1)} %get-tuple-element.32), channel_id=1, source_target_pairs={{0,15},{1,14},{2,13},{3,12},{4,11},{5,10},{6,9},{7,8},{8,7},{9,6},... | collective-permute-start | bytes 1769480 | tf_op jit(solution)/shard_map/ppermute | solution.py:324
  128.3 75.2 %collective-permute-start.6 = (bf16[1,144,2048]{2,1,0:T(8,128)(2,1)S(1)}, bf16[1,144,2048]{2,1,0:T(8,128)(2,1)S(1)}, u32[]{:S(2)}, u32[]{:S(2)}) collective-permute-start(bf16[1,144,2048]{2,1,0:T(8,128)(2,1)S(1)} %get-tuple-element.31), channel_id=1, source_target_pairs={{0,6},{1,7},{2,4},{3,5},{4,2},{5,3},{6,0},{7,1},{8,14},{9,15},{10,... | collective-permute-start | bytes 1769480 | tf_op jit(solution)/shard_map/ppermute | solution.py:324
  142.3 61.2 %collective-permute-start.3 = (bf16[1,144,2048]{2,1,0:T(8,128)(2,1)S(1)}, bf16[1,144,2048]{2,1,0:T(8,128)(2,1)S(1)}, u32[]{:S(2)}, u32[]{:S(2)}) collective-permute-start(bf16[1,144,2048]{2,1,0:T(8,128)(2,1)S(1)} %get-tuple-element.29), channel_id=1, source_target_pairs={{0,2},{1,3},{2,0},{3,1},{4,6},{5,7},{6,4},{7,5},{8,10},{9,11},{10,... | collective-permute-start | bytes 1769480 | tf_op jit(solution)/shard_map/ppermute | solution.py:324
  142.4 58.5 %collective-permute-start.12 = (bf16[1,144,1536]{2,1,0:T(8,128)(2,1)S(1)}, bf16[1,144,1536]{2,1,0:T(8,128)(2,1)S(1)}, u32[]{:S(2)}, u32[]{:S(2)}) collective-permute-start(bf16[1,144,1536]{2,1,0:T(8,128)(2,1)S(1)} %get-tuple-element.35), channel_id=1, source_target_pairs={{0,10},{1,11},{2,8},{3,9},{4,14},{5,15},{6,12},{7,13},{8,2},{9,3},... | collective-permute-start | bytes 1327112 | tf_op jit(solution)/shard_map/ppermute | solution.py:324
  155.8 57.5 %copy-start.5 = (bf16[256,256]{1,0:T(8,128)(2,1)S(1)}, bf16[256,256]{1,0:T(8,128)(2,1)}, u32[]{:S(2)}) copy-start(bf16[256,256]{1,0:T(8,128)(2,1)} %refine_point.1) | copy-start | bytes 393220
  155.8 57.5 %copy-start.6 = (bf16[9,256]{1,0:T(8,128)(2,1)S(1)}, bf16[9,256]{1,0:T(8,128)(2,1)}, u32[]{:S(2)}) copy-start(bf16[9,256]{1,0:T(8,128)(2,1)} %refine_depth.1) | copy-start | bytes 13828
  168.0 22.1 %copy-start.9 = (bf16[1,144,2048]{2,1,0:T(8,128)(2,1)}, bf16[1,144,2048]{2,1,0:T(8,128)(2,1)S(1)}, u32[]{:S(2)}) copy-start(bf16[1,144,2048]{2,1,0:T(8,128)(2,1)S(1)} %collective-permute-done.14) | copy-start | bytes 1769476
  168.0 35.5 %collective-permute-start.16 = (bf16[1,144,1536]{2,1,0:T(8,128)(2,1)S(1)}, bf16[1,144,1536]{2,1,0:T(8,128)(2,1)S(1)}, u32[]{:S(2)}, u32[]{:S(2)}) collective-permute-start(bf16[1,144,1536]{2,1,0:T(8,128)(2,1)S(1)} %get-tuple-element.44), channel_id=1, source_target_pairs={{0,14},{1,15},{2,12},{3,13},{4,10},{5,11},{6,8},{7,9},{8,6},{9,7},... | collective-permute-start | bytes 1327112 | tf_op jit(solution)/shard_map/ppermute | solution.py:324
  173.0 17.0 %copy-start.10 = (bf16[1,144,2048]{2,1,0:T(8,128)(2,1)}, bf16[1,144,2048]{2,1,0:T(8,128)(2,1)S(1)}, u32[]{:S(2)}) copy-start(bf16[1,144,2048]{2,1,0:T(8,128)(2,1)S(1)} %collective-permute-done.8) | copy-start | bytes 1769476
  173.0 40.3 %collective-permute-start.9 = (bf16[1,144,512]{2,1,0:T(8,128)(2,1)S(1)}, bf16[1,144,512]{2,1,0:T(8,128)(2,1)S(1)}, u32[]{:S(2)}, u32[]{:S(2)}) collective-permute-start(bf16[1,144,512]{2,1,0:T(8,128)(2,1)S(1)} %get-tuple-element.33), channel_id=1, source_target_pairs={{0,10},{1,11},{2,8},{3,9},{4,14},{5,15},{6,12},{7,13},{8,2},{9,3},... | collective-permute-start | bytes 442376 | tf_op jit(solution)/shard_map/ppermute | solution.py:324
  201.0 12.4 %collective-permute-start.15 = (bf16[1,144,512]{2,1,0:T(8,128)(2,1)S(1)}, bf16[1,144,512]{2,1,0:T(8,128)(2,1)S(1)}, u32[]{:S(2)}, u32[]{:S(2)}) collective-permute-start(bf16[1,144,512]{2,1,0:T(8,128)(2,1)S(1)} %get-tuple-element.41), channel_id=1, source_target_pairs={{0,14},{1,15},{2,12},{3,13},{4,10},{5,11},{6,8},{7,9},{8,6},{9,7},... | collective-permute-start | bytes 442376 | tf_op jit(solution)/shard_map/ppermute | solution.py:324
  213.4 1.1 copy-start.1
  (5 other events, 4.1 us)

commit v7 on v6

--- a/solution.py
+++ b/solution.py
@@ -143,24 +143,31 @@
 
 
 def last_kernel(info, x0, x1, x2, x3, depth, point, branch, weight, pooling, channel0, channel1,
-                channel2, sums, pool, pre0, pre1, pre2, refine_depth, refine_point, out, plain,
-                shifted, raw, spread, taps, context, rows):
+                channel2, sums_in, pool, pre0, pre1, pre2, refine_depth, refine_point, out, plain,
+                shifted, raw, spread, taps, context, rows, sums, pres, arrived):
+    copies = [pltpu.make_async_copy(sums_in, sums, arrived.at[3])]
+    for index, item in enumerate((pre0, pre1, pre2)):
+        copies.append(pltpu.make_async_copy(item, pres.at[index], arrived.at[index]))
+    for item in copies:
+        item.start()
     parts = pyramid_tile(info, (x0, x1, x2, x3), depth, point, branch, plain, shifted, raw, spread,
                          taps)
-    parts = [sums[index] + parts[index] for index in range(4)]
     term = pool_term([channel0[...], channel1[...], channel2[...], channel_sum(plain)], pooling)
     vector = jnp.maximum(pool[...] + term, 0.0).astype(BF16)
     bias = jnp.dot(vector, weight[4 * HALF:5 * HALF, :], preferred_element_type=F32)[0:1, :]
     context[0] = jnp.zeros((COLS, HALF), F32)
     context[ROWS + 1] = jnp.zeros((COLS, HALF), F32)
-    pres = (pre0[...], pre1[...], pre2[...], project(parts, weight))
-    for index, pre in enumerate(pres):
+    for item in copies:
+        item.wait()
+    last = project([sums[index] + parts[index] for index in range(4)], weight)
+    for index in range(4):
         first = CLASS_ROWS * jnp.bitwise_xor(info[1], ORDER[index])
-        value = jnp.maximum(pre + bias, 0.0).astype(BF16).astype(F32)
-        value = value.reshape(BANDS, CLASS_ROWS, COLS, HALF)
         for band in range(BANDS):
             for row in range(CLASS_ROWS):
-                context[RATE * band + first + row + 1] = value[band, row]
+                start = COLS * (CLASS_ROWS * band + row)
+                value = pres[index, start:start + COLS, :] if index < 3 else last[start:start + COLS, :]
+                value = jnp.maximum(value + bias, 0.0).astype(BF16).astype(F32)
+                context[RATE * band + first + row + 1] = value
     column = lax.broadcasted_iota(jnp.int32, (COLS, HALF), 0)
     wide = refine_depth[...].astype(F32)
 
@@ -218,7 +225,7 @@
 
 
 PARAMS = pltpu.CompilerParams(
-    dimension_semantics=("arbitrary",), vmem_limit_bytes=52 * 1024 * 1024
+    dimension_semantics=("arbitrary",), vmem_limit_bytes=32 * 1024 * 1024
 )
 
 
@@ -269,8 +276,8 @@
               refine_depth, refine_point):
     start = depth.shape[2] - LATE
     specs = pyramid_specs(blocks, start, LATE) + [whole((5 * HALF, HALF))] + channel_specs(start)
-    specs += [whole((4, BANDS * BLOCK, HALF)), whole((16, HALF))]
-    specs += [whole((BANDS * BLOCK, HALF)) for _ in range(3)]
+    specs += [pl.BlockSpec(memory_space=pl.ANY), whole((16, HALF))]
+    specs += [pl.BlockSpec(memory_space=pl.ANY) for _ in range(3)]
     specs += [whole((9, HALF)), whole((HALF, HALF))]
     return pl.pallas_call(
         last_kernel,
@@ -282,6 +289,9 @@
             scratch_shapes=pyramid_scratch() + [
                 pltpu.VMEM((ROWS + 2, COLS, HALF), F32),
                 pltpu.VMEM((ROWS * COLS, HALF), BF16),
+                pltpu.VMEM((4, BANDS * BLOCK, HALF), F32),
+                pltpu.VMEM((3, BANDS * BLOCK, HALF), F32),
+                pltpu.SemaphoreType.DMA((4,)),
             ],
         ),
         out_shape=jax.ShapeDtypeStruct((ROWS * COLS, HALF), BF16),

time: 259 us -> 254 us (0.981)
  Pallas kernels: 49.3 us -> 42.1 us
  local copies, waits for them, and re-layouts: 16.1 us -> 21.7 us
  waiting for transfers between devices: 64 us -> 60.8 us
    unnamed x26 -> x34, local copies, waits for them, and re-layouts: 6.24 us -> 11.4 us
    ppermute x17, waiting for transfers between devices: 64 us -> 60.8 us  [send(): lax.ppermute(value, 'space', [(i, i ^ distance) for i in range(self.parts)])]
    pallas_call x1, Pallas kernels: 9.91 us -> 7 us  [last_call(): pl.pallas_call(last_kernel, grid_spec=pltpu.PrefetchScalarGridSpec(num_sc...]
    pallas_call x1, Pallas kernels: 9.06 us -> 6.43 us  [early_call(): pl.pallas_call(early_kernel, grid_spec=pltpu.PrefetchScalarGridSpec(num_s...]
  transfers between devices with their start and end apart: 17 -> 17, of which waited for: 5 -> 7; matrix products, arithmetic and copies ran while one was open for 3% -> 3% of each run, Pallas kernels for 15% -> 14%
where the time goes in v7:
time: 254 us; the launch traced here: 253 us
  starting transfers between devices  94.6 us (37%)
  waiting for transfers between devices  60.8 us (24%)
  Pallas kernels  42.1 us (17%)
  blocking collectives  33.9 us (13%)
  local copies, waits for them, and re-layouts  21.7 us (9%)
    ppermute x17, starting transfers between devices, send(): lax.ppermute(value, 'space', [(i, i ^ distance) for i in range(self.parts)])  94.6 us
    ppermute x17, waiting for transfers between devices, send(): lax.ppermute(value, 'space', [(i, i ^ distance) for i in range(self.parts)])  60.8 us
    all_to_all x1, blocking collectives, body(): lax.all_to_all(refined.reshape(parts, block, HALF), 'space', 0, 0, tiled=...  33.9 us
    pallas_call x3, Pallas kernels, class_call(): pl.pallas_call(class_kernel, grid_spec=pltpu.PrefetchScalarGridSpec(num_s...  28.7 us
    unnamed x34, local copies, waits for them, and re-layouts  11.4 us
    pallas_call x1, Pallas kernels, last_call(): pl.pallas_call(last_kernel, grid_spec=pltpu.PrefetchScalarGridSpec(num_sc...  7 us
    pallas_call x1, Pallas kernels, early_call(): pl.pallas_call(early_kernel, grid_spec=pltpu.PrefetchScalarGridSpec(num_s...  6.43 us
    reshape x1, local copies, waits for them, and re-layouts, send(): return got[0].reshape(block, size)  5.29 us
  transfers between devices with their start and end apart: 17, of which 7 were waited for; matrix products, arithmetic and copies ran while one was open for 3% of the time, Pallas kernels for 14%

profile of v7, /device:TPU:0, one launch (start us, length us, event | category | flops | bytes accessed | tf_op | source)
XLA Modules:
  0.0 253.4 jit_solution(5993428688340581395)
XLA Ops:
  0.0 2.8 %constant_dynamic-slice_fusion.14 = (bf16[1,144,2048]{2,1,0:T(8,128)(2,1)}, bf16[1,144,2048]{2,1,0:T(8,128)(2,1)}, bf16[1,144,2048]{2,1,0:T(8,128)(2,1)}) fusion(bf16[16,144,2048]{2,1,0:T(8,128)(2,1)} %param.8, s32[]{:T(128)S(6)} %select_n.66, s32[]{:T(128)S(6)} %select_n.65, s32[]{:T(128)S(6)} %select_n.64), kind=kLoop, calls=%fused_computation.15 | loop fusion | bytes 3538956 | tf_op jit(solution)/shard_map/dynamic_slice | solution.py:318
  2.8 3.0 %collective-permute-start = (bf16[1,144,2048]{2,1,0:T(8,128)(2,1)}, bf16[1,144,2048]{2,1,0:T(8,128)(2,1)}, u32[]{:S(2)}, u32[]{:S(2)}) collective-permute-start(bf16[1,144,2048]{2,1,0:T(8,128)(2,1)} %get-tuple-element.62), channel_id=1, source_target_pairs={{0,4},{1,5},{2,6},{3,7},{4,0},{5,1},{6,2},{7,3},{8,12},{9,13},{10,... | collective-permute-start | bytes 1769480 | tf_op jit(solution)/shard_map/ppermute | solution.py:334
  5.9 2.6 %collective-permute-start.10 = (bf16[1,144,2048]{2,1,0:T(8,128)(2,1)}, bf16[1,144,2048]{2,1,0:T(8,128)(2,1)}, u32[]{:S(2)}, u32[]{:S(2)}) collective-permute-start(bf16[1,144,2048]{2,1,0:T(8,128)(2,1)} %get-tuple-element.64), channel_id=1, source_target_pairs={{0,8},{1,9},{2,10},{3,11},{4,12},{5,13},{6,14},{7,15},{8,0},{9,1},... | collective-permute-start | bytes 1769480 | tf_op jit(solution)/shard_map/ppermute | solution.py:334
  8.5 5.3 %dynamic-slice_bitcast_fusion = (bf16[144,2048]{1,0:T(8,128)(2,1)}, bf16[1,144,2048]{2,1,0:T(8,128)(2,1)}, bf16[1,144,2048]{2,1,0:T(8,128)(2,1)}, bf16[1,144,204...) fusion(bf16[16,144,2048]{2,1,0:T(8,128)(2,1)} %param.8, ...), kind=kLoop, calls=%fused_computation | loop fusion | bytes 12976172 | tf_op jit(solution)/shard_map/reshape | solution.py:342
  15.1 17.7 %collective-permute-done = bf16[1,144,2048]{2,1,0:T(8,128)(2,1)} collective-permute-done((bf16[1,144,2048]{2,1,0:T(8,128)(2,1)}, bf16[1,144,2048]{2,1,0:T(8,128)(2,1)}, u32[]{:S(2)}, u32[]{:S(2)}) %collective-permute-start) | collective-permute-done | bytes 589856 | tf_op jit(solution)/shard_map/ppermute | solution.py:334
  34.8 3.3 %collective-permute-start.13 = (bf16[1,144,2048]{2,1,0:T(8,128)(2,1)}, bf16[1,144,2048]{2,1,0:T(8,128)(2,1)}, u32[]{:S(2)}, u32[]{:S(2)}) collective-permute-start(bf16[1,144,2048]{2,1,0:T(8,128)(2,1)} %get-tuple-element.63), channel_id=1, source_target_pairs={{0,12},{1,13},{2,14},{3,15},{4,8},{5,9},{6,10},{7,11},{8,4},{9,5},... | collective-permute-start | bytes 1769480 | tf_op jit(solution)/shard_map/ppermute | solution.py:334
  39.7 6.4 %collective-permute-done.4 = bf16[1,144,2048]{2,1,0:T(8,128)(2,1)S(1)} collective-permute-done((bf16[1,144,2048]{2,1,0:T(8,128)(2,1)S(1)}, bf16[1,144,2048]{2,1,0:T(8,128)(2,1)S(1)}, u32[]{:S(2)}, u32[]{:S(2)}) %collective-permute-start.4) | collective-permute-done | bytes 589856 | tf_op jit(solution)/shard_map/ppermute | solution.py:334
  46.9 3.4 %collective-permute-start.5 = (bf16[1,144,2048]{2,1,0:T(8,128)(2,1)}, bf16[1,144,2048]{2,1,0:T(8,128)(2,1)}, u32[]{:S(2)}, u32[]{:S(2)}) collective-permute-start(bf16[1,144,2048]{2,1,0:T(8,128)(2,1)} %get-tuple-element.30), channel_id=1, source_target_pairs={{0,7},{1,6},{2,5},{3,4},{4,3},{5,2},{6,1},{7,0},{8,15},{9,14},{10,... | collective-permute-start | bytes 1769480 | tf_op jit(solution)/shard_map/ppermute | solution.py:334
  50.3 9.1 %collective-permute-done.1 = bf16[1,144,2048]{2,1,0:T(8,128)(2,1)S(1)} collective-permute-done((bf16[1,144,2048]{2,1,0:T(8,128)(2,1)S(1)}, bf16[1,144,2048]{2,1,0:T(8,128)(2,1)S(1)}, u32[]{:S(2)}, u32[]{:S(2)}) %collective-permute-start.1) | collective-permute-done | bytes 589856 | tf_op jit(solution)/shard_map/ppermute | solution.py:334
  65.8 9.6 %pyramid_class.3 = (f32[576,256]{1,0:T(8,128)S(1)}, f32[8,2048]{1,0:T(8,128)S(1)}) custom-call(s32[2]{0:T(128)S(1)} %pad_add_fusion.info, bf16[144,2048]{1,0:T(8,128)(2,1)S(1)} %copy-done.6, bf16[144,2048]{1,0:T(8,128)(2,1)} %bitcast.8.x1, bf16[144,2048]{1,0:T(8,128)(2,1)} %bitcast.9.x2, bf16[144,2048]{1,0:T(8,128)(2,1)} %bitcast.10.x3, ...), custom_call_target="tpu_custom_call" | custom-call | tf_op jit(solution)/shard_map/pyramid_class/pallas_call | solution.py:234
  76.2 29.0 %collective-permute-start.14 = (bf16[1,144,2048]{2,1,0:T(8,128)(2,1)}, bf16[1,144,2048]{2,1,0:T(8,128)(2,1)}, u32[]{:S(2)}, u32[]{:S(2)}) collective-permute-start(bf16[1,144,2048]{2,1,0:T(8,128)(2,1)} %get-tuple-element.38), channel_id=1, source_target_pairs={{0,11},{1,10},{2,9},{3,8},{4,15},{5,14},{6,13},{7,12},{8,3},{9,2},... | collective-permute-start | bytes 1769480 | tf_op jit(solution)/shard_map/ppermute | solution.py:334
  105.3 15.1 %collective-permute-done.7 = bf16[1,144,2048]{2,1,0:T(8,128)(2,1)} collective-permute-done((bf16[1,144,2048]{2,1,0:T(8,128)(2,1)}, bf16[1,144,2048]{2,1,0:T(8,128)(2,1)}, u32[]{:S(2)}, u32[]{:S(2)}) %collective-permute-start.7) | collective-permute-done | bytes 589856 | tf_op jit(solution)/shard_map/ppermute | solution.py:334
  120.3 6.1 %collective-permute-start.8 = (bf16[1,144,2048]{2,1,0:T(8,128)(2,1)}, bf16[1,144,2048]{2,1,0:T(8,128)(2,1)S(1)}, u32[]{:S(2)}, u32[]{:S(2)}) collective-permute-start(bf16[1,144,2048]{2,1,0:T(8,128)(2,1)} %get-tuple-element.32), channel_id=1, source_target_pairs={{0,15},{1,14},{2,13},{3,12},{4,11},{5,10},{6,9},{7,8},{8,7},{9,6},... | collective-permute-start | bytes 1769480 | tf_op jit(solution)/shard_map/ppermute | solution.py:334
  127.6 14.0 %collective-permute-start.6 = (bf16[1,144,2048]{2,1,0:T(8,128)(2,1)}, bf16[1,144,2048]{2,1,0:T(8,128)(2,1)S(1)}, u32[]{:S(2)}, u32[]{:S(2)}) collective-permute-start(bf16[1,144,2048]{2,1,0:T(8,128)(2,1)} %get-tuple-element.31), channel_id=1, source_target_pairs={{0,6},{1,7},{2,4},{3,5},{4,2},{5,3},{6,0},{7,1},{8,14},{9,15},{10,... | collective-permute-start | bytes 1769480 | tf_op jit(solution)/shard_map/ppermute | solution.py:334
  148.1 9.5 %pyramid_class.5 = (f32[576,256]{1,0:T(8,128)S(1)}, f32[8,2048]{1,0:T(8,128)S(1)}) custom-call(s32[2]{0:T(128)S(1)} %pad_add_fusion.info, bf16[144,2048]{1,0:T(8,128)(2,1)S(1)} %bitcast.28, bf16[144,2048]{1,0:T(8,128)(2,1)S(1)} %bitcast.27, bf16[144,2048]{1,0:T(8,128)(2,1)} %bitcast.16.x2, bf16[144,2048]{1,0:T(8,128)(2,1)} %bitcast.17.x3, ...), custom_call_target="tpu_custom_call" | custom-call | tf_op jit(solution)/shard_map/pyramid_class/pallas_call | solution.py:234
  157.7 10.1 %collective-permute-done.14 = bf16[1,144,2048]{2,1,0:T(8,128)(2,1)} collective-permute-done((bf16[1,144,2048]{2,1,0:T(8,128)(2,1)}, bf16[1,144,2048]{2,1,0:T(8,128)(2,1)}, u32[]{:S(2)}, u32[]{:S(2)}) %collective-permute-start.14) | collective-permute-done | bytes 589856 | tf_op jit(solution)/shard_map/ppermute | solution.py:334
  167.8 3.1 %collective-permute-start.16 = (bf16[1,144,1536]{2,1,0:T(8,128)(2,1)S(1)}, bf16[1,144,1536]{2,1,0:T(8,128)(2,1)S(1)}, u32[]{:S(2)}, u32[]{:S(2)}) collective-permute-start(bf16[1,144,1536]{2,1,0:T(8,128)(2,1)S(1)} %get-tuple-element.44), channel_id=1, source_target_pairs={{0,14},{1,15},{2,12},{3,13},{4,10},{5,11},{6,8},{7,9},{8,6},{9,7},... | collective-permute-start | bytes 1327112 | tf_op jit(solution)/shard_map/ppermute | solution.py:334
  171.9 16.9 %collective-permute-start.9 = (bf16[1,144,512]{2,1,0:T(8,128)(2,1)S(1)}, bf16[1,144,512]{2,1,0:T(8,128)(2,1)S(1)}, u32[]{:S(2)}, u32[]{:S(2)}) collective-permute-start(bf16[1,144,512]{2,1,0:T(8,128)(2,1)S(1)} %get-tuple-element.33), channel_id=1, source_target_pairs={{0,10},{1,11},{2,8},{3,9},{4,14},{5,15},{6,12},{7,13},{8,2},{9,3},... | collective-permute-start | bytes 442376 | tf_op jit(solution)/shard_map/ppermute | solution.py:334
  188.9 9.6 %pyramid_class.4 = (f32[576,256]{1,0:T(8,128)S(1)}, f32[8,2048]{1,0:T(8,128)S(1)}) custom-call(s32[2]{0:T(128)S(1)} %pad_add_fusion.info, bf16[144,2048]{1,0:T(8,128)(2,1)} %bitcast.5.x0, bf16[144,2048]{1,0:T(8,128)(2,1)} %bitcast.6.x1, bf16[144,2048]{1,0:T(8,128)(2,1)} %bitcast.11.x2, bf16[144,2048]{1,0:T(8,128)(2,1)S(1)} %bitcast.29, ...), custom_call_target="tpu_custom_call" | custom-call | tf_op jit(solution)/shard_map/pyramid_class/pallas_call | solution.py:234
  198.6 4.2 %collective-permute-start.15 = (bf16[1,144,512]{2,1,0:T(8,128)(2,1)S(1)}, bf16[1,144,512]{2,1,0:T(8,128)(2,1)S(1)}, u32[]{:S(2)}, u32[]{:S(2)}) collective-permute-start(bf16[1,144,512]{2,1,0:T(8,128)(2,1)S(1)} %get-tuple-element.41), channel_id=1, source_target_pairs={{0,14},{1,15},{2,12},{3,13},{4,10},{5,11},{6,8},{7,9},{8,6},{9,7},... | collective-permute-start | bytes 442376 | tf_op jit(solution)/shard_map/ppermute | solution.py:334
  202.8 6.4 %pyramid_early.1 = (f32[4,576,256]{2,1,0:T(8,128)S(1)}, f32[16,256]{1,0:T(8,128)S(1)}) custom-call(s32[2]{0:T(128)S(1)} %pad_add_fusion.info, bf16[144,2048]{1,0:T(8,128)(2,1)S(1)} %bitcast.25, bf16[144,2048]{1,0:T(8,128)(2,1)S(1)} %bitcast.23, bf16[144,1536]{1,0:T(8,128)(2,1)S(1)} %bitcast.30, bf16[144,1536]{1,0:T(8,128)(2,1)S(1)} %bitcast.31, ...), custom_call_target="tpu_custom_call" | custom-call | tf_op jit(solution)/shard_map/pyramid_early/pallas_call | solution.py:257
  209.2 2.2 collective-permute-done.9
  211.5 7.0 %pyramid_last.1 = bf16[2304,256]{1,0:T(8,128)(2,1)S(1)} custom-call(s32[2]{0:T(128)S(1)} %pad_add_fusion.info, bf16[144,2048]{1,0:T(8,128)(2,1)S(1)} %bitcast.26, bf16[144,2048]{1,0:T(8,128)(2,1)S(1)} %bitcast.24, bf16[144,512]{1,0:T(8,128)(2,1)S(1)} %bitcast.32, bf16[144,512]{1,0:T(8,128)(2,1)S(1)} %bitcast.33, bf16[3,9,2048]{2,1,0:T(8,128)(2,1)S(1)} %copy.9.depth, ...), custom_call_target="tpu_custom_call" | custom-call | tf_op jit(solution)/shard_map/pyramid_last/pallas_call | solution.py:282
  218.5 33.9 %all_to_all.5 = bf16[16,144,256]{2,1,0:T(8,128)(2,1)S(1)} all-to-all(bf16[16,144,256]{2,1,0:T(8,128)(2,1)S(1)} %bitcast.22), channel_id=1, replica_groups=mesh['dp'=2,'space'=16] {'space'}, dimensions={0} | all-to-all | bytes 2359296 | tf_op jit(solution)/shard_map/all_to_all | solution.py:404
  (55 shorter events, 22.9 us)
Async XLA Ops:
  0.0 62.3 %copy-start.15 = (bf16[3,9,2048]{2,0,1:T(4,128)(2,1)S(1)}, bf16[3,9,2048]{2,0,1:T(4,128)(2,1)}, u32[]{:S(2)}) copy-start(bf16[3,9,2048]{2,0,1:T(4,128)(2,1)} %param.9) | copy-start | bytes 331780
  0.0 62.5 %copy-start = (bf16[3,2048,256]{2,1,0:T(8,128)(2,1)S(1)}, bf16[3,2048,256]{2,1,0:T(8,128)(2,1)}, u32[]{:S(2)}) copy-start(bf16[3,2048,256]{2,1,0:T(8,128)(2,1)} %point.9) | copy-start | bytes 9437188
  2.8 30.0 %collective-permute-start = (bf16[1,144,2048]{2,1,0:T(8,128)(2,1)}, bf16[1,144,2048]{2,1,0:T(8,128)(2,1)}, u32[]{:S(2)}, u32[]{:S(2)}) collective-permute-start(bf16[1,144,2048]{2,1,0:T(8,128)(2,1)} %get-tuple-element.62), channel_id=1, source_target_pairs={{0,4},{1,5},{2,6},{3,7},{4,0},{5,1},{6,2},{7,3},{8,12},{9,13},{10,... | collective-permute-start | bytes 1769480 | tf_op jit(solution)/shard_map/ppermute | solution.py:334
  5.9 32.2 %collective-permute-start.10 = (bf16[1,144,2048]{2,1,0:T(8,128)(2,1)}, bf16[1,144,2048]{2,1,0:T(8,128)(2,1)}, u32[]{:S(2)}, u32[]{:S(2)}) collective-permute-start(bf16[1,144,2048]{2,1,0:T(8,128)(2,1)} %get-tuple-element.64), channel_id=1, source_target_pairs={{0,8},{1,9},{2,10},{3,11},{4,12},{5,13},{6,14},{7,15},{8,0},{9,1},... | collective-permute-start | bytes 1769480 | tf_op jit(solution)/shard_map/ppermute | solution.py:334
  13.7 32.3 %collective-permute-start.4 = (bf16[1,144,2048]{2,1,0:T(8,128)(2,1)S(1)}, bf16[1,144,2048]{2,1,0:T(8,128)(2,1)S(1)}, u32[]{:S(2)}, u32[]{:S(2)}) collective-permute-start(bf16[1,144,2048]{2,1,0:T(8,128)(2,1)S(1)} %get-tuple-element.54), channel_id=1, source_target_pairs={{0,5},{1,4},{2,7},{3,6},{4,1},{5,0},{6,3},{7,2},{8,13},{9,12},{10,... | collective-permute-start | bytes 1769480 | tf_op jit(solution)/shard_map/ppermute | solution.py:334
  32.9 26.6 %collective-permute-start.1 = (bf16[1,144,2048]{2,1,0:T(8,128)(2,1)S(1)}, bf16[1,144,2048]{2,1,0:T(8,128)(2,1)S(1)}, u32[]{:S(2)}, u32[]{:S(2)}) collective-permute-start(bf16[1,144,2048]{2,1,0:T(8,128)(2,1)S(1)} %get-tuple-element.27), channel_id=1, source_target_pairs={{0,1},{1,0},{2,3},{3,2},{4,5},{5,4},{6,7},{7,6},{8,9},{9,8},{10,11... | collective-permute-start | bytes 1769480 | tf_op jit(solution)/shard_map/ppermute | solution.py:334
  34.8 27.6 %collective-permute-start.13 = (bf16[1,144,2048]{2,1,0:T(8,128)(2,1)}, bf16[1,144,2048]{2,1,0:T(8,128)(2,1)}, u32[]{:S(2)}, u32[]{:S(2)}) collective-permute-start(bf16[1,144,2048]{2,1,0:T(8,128)(2,1)} %get-tuple-element.63), channel_id=1, source_target_pairs={{0,12},{1,13},{2,14},{3,15},{4,8},{5,9},{6,10},{7,11},{8,4},{9,5},... | collective-permute-start | bytes 1769480 | tf_op jit(solution)/shard_map/ppermute | solution.py:334
  38.1 82.2 %collective-permute-start.7 = (bf16[1,144,2048]{2,1,0:T(8,128)(2,1)}, bf16[1,144,2048]{2,1,0:T(8,128)(2,1)}, u32[]{:S(2)}, u32[]{:S(2)}) collective-permute-start(bf16[1,144,2048]{2,1,0:T(8,128)(2,1)} %get-tuple-element.52), channel_id=1, source_target_pairs={{0,9},{1,8},{2,11},{3,10},{4,13},{5,12},{6,15},{7,14},{8,1},{9,0},... | collective-permute-start | bytes 1769480 | tf_op jit(solution)/shard_map/ppermute | solution.py:334
  38.1 89.5 %collective-permute-start.11 = (bf16[1,144,2048]{2,1,0:T(8,128)(2,1)}, bf16[1,144,2048]{2,1,0:T(8,128)(2,1)}, u32[]{:S(2)}, u32[]{:S(2)}) collective-permute-start(bf16[1,144,2048]{2,1,0:T(8,128)(2,1)} %get-tuple-element.34), channel_id=1, source_target_pairs={{0,13},{1,12},{2,15},{3,14},{4,9},{5,8},{6,11},{7,10},{8,5},{9,4},... | collective-permute-start | bytes 1769480 | tf_op jit(solution)/shard_map/ppermute | solution.py:334
  46.9 80.7 %collective-permute-start.5 = (bf16[1,144,2048]{2,1,0:T(8,128)(2,1)}, bf16[1,144,2048]{2,1,0:T(8,128)(2,1)}, u32[]{:S(2)}, u32[]{:S(2)}) collective-permute-start(bf16[1,144,2048]{2,1,0:T(8,128)(2,1)} %get-tuple-element.30), channel_id=1, source_target_pairs={{0,7},{1,6},{2,5},{3,4},{4,3},{5,2},{6,1},{7,0},{8,15},{9,14},{10,... | collective-permute-start | bytes 1769480 | tf_op jit(solution)/shard_map/ppermute | solution.py:334
  60.3 81.3 %collective-permute-start.2 = (bf16[1,144,2048]{2,1,0:T(8,128)(2,1)}, bf16[1,144,2048]{2,1,0:T(8,128)(2,1)}, u32[]{:S(2)}, u32[]{:S(2)}) collective-permute-start(bf16[1,144,2048]{2,1,0:T(8,128)(2,1)} %get-tuple-element.28), channel_id=1, source_target_pairs={{0,3},{1,2},{2,1},{3,0},{4,7},{5,6},{6,5},{7,4},{8,11},{9,10},{10,... | collective-permute-start | bytes 1769480 | tf_op jit(solution)/shard_map/ppermute | solution.py:334
  62.5 1.2 copy-start.1
  76.2 91.6 %collective-permute-start.14 = (bf16[1,144,2048]{2,1,0:T(8,128)(2,1)}, bf16[1,144,2048]{2,1,0:T(8,128)(2,1)}, u32[]{:S(2)}, u32[]{:S(2)}) collective-permute-start(bf16[1,144,2048]{2,1,0:T(8,128)(2,1)} %get-tuple-element.38), channel_id=1, source_target_pairs={{0,11},{1,10},{2,9},{3,8},{4,15},{5,14},{6,13},{7,12},{8,3},{9,2},... | collective-permute-start | bytes 1769480 | tf_op jit(solution)/shard_map/ppermute | solution.py:334
  105.3 97.5 %copy-start.5 = (bf16[2048,256]{1,0:T(8,128)(2,1)S(1)}, bf16[2048,256]{1,0:T(8,128)(2,1)}, u32[]{:S(2)}) copy-start(bf16[2048,256]{1,0:T(8,128)(2,1)} %pooling.3) | copy-start | bytes 3145732
  120.3 51.6 %collective-permute-start.8 = (bf16[1,144,2048]{2,1,0:T(8,128)(2,1)}, bf16[1,144,2048]{2,1,0:T(8,128)(2,1)S(1)}, u32[]{:S(2)}, u32[]{:S(2)}) collective-permute-start(bf16[1,144,2048]{2,1,0:T(8,128)(2,1)} %get-tuple-element.32), channel_id=1, source_target_pairs={{0,15},{1,14},{2,13},{3,12},{4,11},{5,10},{6,9},{7,8},{8,7},{9,6},... | collective-permute-start | bytes 1769480 | tf_op jit(solution)/shard_map/ppermute | solution.py:334
  127.6 75.2 %collective-permute-start.6 = (bf16[1,144,2048]{2,1,0:T(8,128)(2,1)}, bf16[1,144,2048]{2,1,0:T(8,128)(2,1)S(1)}, u32[]{:S(2)}, u32[]{:S(2)}) collective-permute-start(bf16[1,144,2048]{2,1,0:T(8,128)(2,1)} %get-tuple-element.31), channel_id=1, source_target_pairs={{0,6},{1,7},{2,4},{3,5},{4,2},{5,3},{6,0},{7,1},{8,14},{9,15},{10,... | collective-permute-start | bytes 1769480 | tf_op jit(solution)/shard_map/ppermute | solution.py:334
  141.6 61.2 %collective-permute-start.3 = (bf16[1,144,2048]{2,1,0:T(8,128)(2,1)}, bf16[1,144,2048]{2,1,0:T(8,128)(2,1)S(1)}, u32[]{:S(2)}, u32[]{:S(2)}) collective-permute-start(bf16[1,144,2048]{2,1,0:T(8,128)(2,1)} %get-tuple-element.29), channel_id=1, source_target_pairs={{0,2},{1,3},{2,0},{3,1},{4,6},{5,7},{6,4},{7,5},{8,10},{9,11},{10,... | collective-permute-start | bytes 1769480 | tf_op jit(solution)/shard_map/ppermute | solution.py:334
  142.2 56.4 %collective-permute-start.12 = (bf16[1,144,1536]{2,1,0:T(8,128)(2,1)S(1)}, bf16[1,144,1536]{2,1,0:T(8,128)(2,1)S(1)}, u32[]{:S(2)}, u32[]{:S(2)}) collective-permute-start(bf16[1,144,1536]{2,1,0:T(8,128)(2,1)S(1)} %get-tuple-element.35), channel_id=1, source_target_pairs={{0,10},{1,11},{2,8},{3,9},{4,14},{5,15},{6,12},{7,13},{8,2},{9,3},... | collective-permute-start | bytes 1327112 | tf_op jit(solution)/shard_map/ppermute | solution.py:334
  157.7 53.8 %copy-start.8 = (f32[576,256]{1,0:T(8,128)S(1)}, f32[576,256]{1,0:T(8,128)}, u32[]{:S(2)}) copy-start(f32[576,256]{1,0:T(8,128)} %copy-done.7) | copy-start | bytes 1769476
  157.7 53.8 %copy-start.13 = (bf16[256,256]{1,0:T(8,128)(2,1)S(1)}, bf16[256,256]{1,0:T(8,128)(2,1)}, u32[]{:S(2)}) copy-start(bf16[256,256]{1,0:T(8,128)(2,1)} %refine_point.1) | copy-start | bytes 393220
  157.7 53.8 %copy-start.14 = (bf16[9,256]{1,0:T(8,128)(2,1)S(1)}, bf16[9,256]{1,0:T(8,128)(2,1)}, u32[]{:S(2)}) copy-start(bf16[9,256]{1,0:T(8,128)(2,1)} %refine_depth.1) | copy-start | bytes 13828
  167.8 34.9 %collective-permute-start.16 = (bf16[1,144,1536]{2,1,0:T(8,128)(2,1)S(1)}, bf16[1,144,1536]{2,1,0:T(8,128)(2,1)S(1)}, u32[]{:S(2)}, u32[]{:S(2)}) collective-permute-start(bf16[1,144,1536]{2,1,0:T(8,128)(2,1)S(1)} %get-tuple-element.44), channel_id=1, source_target_pairs={{0,14},{1,15},{2,12},{3,13},{4,10},{5,11},{6,8},{7,9},{8,6},{9,7},... | collective-permute-start | bytes 1327112 | tf_op jit(solution)/shard_map/ppermute | solution.py:334
  171.9 39.5 %collective-permute-start.9 = (bf16[1,144,512]{2,1,0:T(8,128)(2,1)S(1)}, bf16[1,144,512]{2,1,0:T(8,128)(2,1)S(1)}, u32[]{:S(2)}, u32[]{:S(2)}) collective-permute-start(bf16[1,144,512]{2,1,0:T(8,128)(2,1)S(1)} %get-tuple-element.33), channel_id=1, source_target_pairs={{0,10},{1,11},{2,8},{3,9},{4,14},{5,15},{6,12},{7,13},{8,2},{9,3},... | collective-permute-start | bytes 442376 | tf_op jit(solution)/shard_map/ppermute | solution.py:334
  198.6 12.9 %collective-permute-start.15 = (bf16[1,144,512]{2,1,0:T(8,128)(2,1)S(1)}, bf16[1,144,512]{2,1,0:T(8,128)(2,1)S(1)}, u32[]{:S(2)}, u32[]{:S(2)}) collective-permute-start(bf16[1,144,512]{2,1,0:T(8,128)(2,1)S(1)} %get-tuple-element.41), channel_id=1, source_target_pairs={{0,14},{1,15},{2,12},{3,13},{4,10},{5,11},{6,8},{7,9},{8,6},{9,7},... | collective-permute-start | bytes 442376 | tf_op jit(solution)/shard_map/ppermute | solution.py:334
  (9 other events, 9.1 us)
